TPU v7x, 256 devices: a whole 4x4x8 slice. The times are simulated.
256 devices in a mesh: region: 4 (over y), shard: 64 (over x, z, core).
Axes of the slice: x: 4, y: 4, z: 8, core: 2. Of those that a mesh axis runs over, the one named last changes fastest.
Arguments:
- features: bfloat16 [65536, 1024], P(('region', 'shard')), may hold values from -6 to 6
- proj_weight: bfloat16 [1024, 1024], replicated, may hold values from -0.1875 to 0.1875
- proj_bias: float32 [1024], replicated, may hold values from -3 to 3
- self_weight: bfloat16 [1024, 1024], replicated, may hold values from -0.1875 to 0.1875
- nbr_weight: bfloat16 [1024, 1024], replicated, may hold values from -0.1875 to 0.1875
- out_bias: float32 [1024], replicated, may hold values from -3 to 3
- nbr_ids: int32 [65536, 8], P(('region', 'shard')), may hold values from 0 to 16383, as said below
- nbr_counts: int32 [65536, 8], P(('region', 'shard')), may hold values from 1 to 32
- live_slots: int32 [512], P(('region', 'shard')), may hold values from 1 to 8
- query_ids: int32 [16384], P(('region', 'shard')), may hold values from 0 to 255
- positive_ids: int32 [16384], P(('region', 'shard')), may hold values from 0 to 255
- neg_blocks: int32 [256, 4], P(('region', 'shard')), may hold values from 0 to 7, as said below
Outputs:
- embedding: bfloat16 [65536, 1024], P(('region', 'shard'))
- hinge_terms: float32 [16384, 4], P(('region', 'shard'))
Inputs may be any that keep to these rules, and one draw needn't show every extreme that they name: `nbr_ids`: entries index items of the item's own region. Of the 2048 neighbour slots of one device, at most 64 name items held by any one device, and exactly 64 name the items of one device. `neg_blocks`: entry g names block g % 2 of the device at the same shard index in region g // 2; never a block of the device's own region.
All inputs are finite; a program needn't handle non-finite values.
Results may differ from a plain program's by a relative error of at most 0.0036.
Values may be sent and summed in bfloat16 or wider, within the bound.
A program may use at most 128 MiB of HBM per device.

v0:
```python
import jax
import jax.numpy as jnp
from jax import lax
from jax.sharding import PartitionSpec as P

score_scale = 32.0
margin_value = 1.0
norm_eps = 1e-06


def body(
    features,
    proj_weight,
    proj_bias,
    self_weight,
    nbr_weight,
    out_bias,
    nbr_ids,
    nbr_counts,
    live_slots,
    query_ids,
    positive_ids,
    neg_blocks,
):
    item_dev = features.shape[0]
    hidden = proj_weight.shape[1]
    fanout = nbr_ids.shape[1]
    block_rows = item_dev // live_slots.shape[0]
    shards = lax.axis_size("shard")
    live_item = jnp.repeat(live_slots, block_rows, total_repeat_length=item_dev)
    slot_weight = jnp.where(
        jnp.arange(fanout, dtype=jnp.int32)[None, :] < live_item[:, None], nbr_counts, 0
    )
    weight_sum = jnp.sum(slot_weight.astype(jnp.float32), axis=1, keepdims=True)
    flat_ids = nbr_ids.reshape(-1)
    owners = flat_ids // item_dev
    local_row = flat_ids % item_dev
    slots = flat_ids.shape[0]
    capacity = max(2, 2 * slots // shards)
    onehot = (owners[:, None] == jnp.arange(shards, dtype=jnp.int32)[None, :]).astype(jnp.int32)
    before = jnp.cumsum(onehot, axis=0) - onehot
    slot_rank = jnp.take_along_axis(before, owners[:, None], axis=1)[:, 0]
    requests = jnp.zeros((shards, capacity), jnp.int32).at[owners, slot_rank].set(local_row)
    wanted = lax.all_to_all(requests, "shard", split_axis=0, concat_axis=0, tiled=True)
    outgoing = jnp.take(features, wanted, axis=0)
    incoming = lax.all_to_all(outgoing, "shard", split_axis=0, concat_axis=0, tiled=True)
    gathered = incoming[owners, slot_rank]
    slot_proj = jnp.maximum(
        jnp.dot(gathered, proj_weight, preferred_element_type=jnp.float32) + proj_bias, 0.0
    ).astype(jnp.bfloat16)
    slot_proj = slot_proj.reshape(item_dev, fanout, hidden)
    summed = jnp.einsum(
        "ik,ikh->ih",
        slot_weight.astype(jnp.bfloat16),
        slot_proj,
        preferred_element_type=jnp.float32,
    )
    aggregate = (summed / weight_sum).astype(jnp.bfloat16)
    activation = (
        jnp.dot(features, self_weight, preferred_element_type=jnp.float32)
        + jnp.dot(aggregate, nbr_weight, preferred_element_type=jnp.float32)
        + out_bias
    )
    activation = jnp.maximum(activation, 0.0)
    embedding = (
        activation * lax.rsqrt(jnp.mean(activation * activation, axis=-1, keepdims=True) + norm_eps)
    ).astype(jnp.bfloat16)
    query_emb = jnp.take(embedding, query_ids, axis=0)
    positive_emb = jnp.take(embedding, positive_ids, axis=0)
    neg_lists = neg_blocks[0]
    positive_score = (
        score_scale
        / hidden
        * jnp.sum(query_emb.astype(jnp.float32) * positive_emb.astype(jnp.float32), axis=-1)
    )
    start_value = jnp.zeros((query_emb.shape[0], neg_lists.shape[0]), jnp.float32)
    scores = (
        score_scale
        / hidden
        * jnp.dot(
            query_emb,
            lax.all_gather(embedding, "region", axis=0, tiled=True).T,
            preferred_element_type=jnp.float32,
        )
    )
    hinge_all = jnp.maximum(scores - positive_score[:, None] + margin_value, 0.0)
    block_mean = jnp.mean(hinge_all.reshape(query_emb.shape[0], -1, block_rows), axis=-1)
    pool_ids = jnp.int32(0) // block_rows + jnp.arange(block_mean.shape[1], dtype=jnp.int32)
    picked = jnp.where(
        neg_lists[None, :, None] == pool_ids[None, None, :], block_mean[:, None, :], 0.0
    )
    hinge_terms = start_value + jnp.sum(picked, axis=-1)
    return (embedding, hinge_terms)


def solution(mesh):
    in_specs = (
        P(("region", "shard"), None),
        P(),
        P(),
        P(),
        P(),
        P(),
        P(("region", "shard"), None),
        P(("region", "shard"), None),
        P(("region", "shard")),
        P(("region", "shard")),
        P(("region", "shard")),
        P(("region", "shard"), None),
    )
    out_specs = (P(("region", "shard"), None), P(("region", "shard"), None))
    return jax.shard_map(body, mesh=mesh, in_specs=in_specs, out_specs=out_specs, check_vma=False)
```

profile of v0, /device:TPU:1, one launch (start us, length us, event | category | flops | bytes accessed | tf_op | source)
XLA Modules:
  0.0 386.8 jit_solution(6796952247601897155)
XLA Ops:
  7.2 0.0 copy-start
  7.2 1.0 copy.39
  8.2 0.1 reshape.447
  8.3 0.1 reshape.449
  8.4 0.1 reshape.450
  8.5 0.1 reshape.446
  8.7 18.1 %reduce-window.14 = s32[64,16,128]{2,1,0:T(8,128)S(1)} reduce-window(s32[64,16,128]{2,1,0:T(8,128)S(1)} %fusion.15, s32[]{:T(128)} %constant.161.clone.1), window={size=1x1x128 pad=0_0x0_0x127_0}, to_apply=%region_0.1 | reduce-window | flops 16646144 | bytes 1048580 | tf_op jit(solution)/shard_map/reduce-window.3
  26.8 0.2 slice.37
  27.0 0.4 copy.48
  27.5 0.2 reduce-window.15
  27.6 0.2 broadcast_add_fusion
  28.0 0.2 fusion.13
  28.2 0.0 copy-start.5
  28.2 0.0 copy-start.1
  28.2 16.8 %gather_fusion.2 = s32[2048]{0:T(1024)S(1)} fusion(s32[2048,64]{0,1:T(8,128)S(1)} %fusion.13, s32[2048]{0:T(1024)S(1)} %bitcast.55), kind=kCustom, calls=%fused_computation.4 | custom fusion | bytes 32768 | tf_op jit(solution)/shard_map/jit(take_along_axis)/gather | solution.py:42
  45.0 0.1 shift-left_or_fusion
  45.1 0.1 and_reduce_fusion
  45.2 0.1 multiply_reduce_fusion.2
  45.3 8.1 %scatter_custom_fusion = s32[4096]{0:T(1024)S(1)} fusion(s32[2048]{0:T(1024)S(1)} %broadcast_select_fusion.3, s32[2048]{0:T(1024)S(1)} %get-tuple-element.18, s32[]{:T(128)} %constant.161.clone.1), kind=kCustom, calls=%fused_computation.69 | custom fusion | bytes 16388
  53.4 0.1 all_to_all.13
  53.4 22.1 %all_to_all.20 = s32[64,1,64]{2,1,0:T(1,128)S(1)} all-to-all(s32[64,1,64]{2,1,0:T(1,128)S(1)} %all_to_all.13), channel_id=1, replica_groups=mesh['region'=4,'shard'=64] {'shard'}, dimensions={0} | all-to-all | bytes 32768 | tf_op jit(solution)/shard_map/all_to_all | solution.py:44
  75.5 0.1 reshape.485
  75.7 18.3 %gather_fusion = bf16[4096,1024]{1,0:T(8,128)(2,1)} fusion(bf16[256,1024]{1,0:T(8,128)(2,1)S(1)} %copy-done.1, s32[4096]{0:T(1024)S(1)} %broadcast_clamp_fusion), kind=kCustom, calls=%fused_computation.2 | custom fusion | bytes 16793600 | tf_op jit(solution)/shard_map/jit(_take)/gather | solution.py:45
  93.9 7.3 %broadcast_select_fusion = bf16[64,64,1024]{2,1,0:T(8,128)(2,1)} fusion(bf16[64,64,1024]{2,1,0:T(8,128)(2,1)} %bitcast.56, pred[64,64]{1,0:T(8,128)(4,1)S(1)} %compare_and_fusion), kind=kLoop, calls=%fused_computation.7 | loop fusion | flops 4194304 | bytes 16781312 | tf_op jit(solution)/shard_map/jit(_take)/select_n | solution.py:45
  101.2 5.9 %all-to-all-start.1 = ((bf16[64,64,1024]{2,1,0:T(8,128)(2,1)}), bf16[64,64,1024]{2,1,0:T(8,128)(2,1)}, u32[]{:S(2)}, u32[]{:S(2)}) async-start(bf16[64,64,1024]{2,1,0:T(8,128)(2,1)} %broadcast_select_fusion), calls=%async_computation.1 | async-start | bytes 16777216 | tf_op jit(solution)/shard_map/all_to_all | solution.py:46
  107.1 0.2 all-gather.2.cloned.1.call-start
  107.4 0.6 fusion.32
  108.0 1.3 compare_select_fusion.12
  109.3 0.2 copy.46
  109.5 3.3 fusion.33
  112.8 180.1 %all-to-all-done.1 = bf16[64,64,1024]{2,1,0:T(8,128)(2,1)} async-done(((bf16[64,64,1024]{2,1,0:T(8,128)(2,1)}), bf16[64,64,1024]{2,1,0:T(8,128)(2,1)}, u32[]{:S(2)}, u32[]{:S(2)}) %all-to-all-start.1) | async-done | bytes 8388640 | tf_op jit(solution)/shard_map/all_to_all | solution.py:46
  292.9 41.1 %gather_fusion.1 = bf16[2048,1024]{1,0:T(8,128)(2,1)} fusion(bf16[64,64,1024]{2,1,0:T(8,128)(2,1)} %all-to-all-done.1, s32[2048]{0:T(1024)S(1)} %bitcast.54), kind=kCustom, calls=%fused_computation.3 | custom fusion | bytes 8404992 | tf_op jit(solution)/shard_map/gather | solution.py:47
  334.0 9.6 %fusion.1 = f32[256,1,1024]{2,1,0:T(1,128)} fusion(bf16[256,8,1]{1,2,0:T(2,128)(2,1)S(1)} %copy.46, f32[1024]{0:T(1024)S(1)} %copy-done.6, bf16[2048,1024]{1,0:T(8,128)(2,1)} %gather_fusion.1, bf16[1024,1024]{1,0:T(8,128)(2,1)} %param.17), kind=kOutput, calls=%fused_computation.9 | convolution fusion | flops 4305453056 | bytes 7348224 | tf_op jit(solution)/shard_map/ik,ikh->ih/dot_general | solution.py:52
  343.7 0.0 copy-start.8
  343.7 0.0 copy-start.9
  343.7 0.0 copy-start.10
  343.7 2.1 multiply_reduce_fusion
  345.8 0.9 multiply_convert_fusion
  346.8 0.0 all-gather.2.cloned.1.call-update
  346.9 0.1 iota_compare_fusion.3
  347.0 1.9 gather_fusion.3
  348.9 1.9 gather_fusion.4
  350.8 0.2 multiply_reduce_fusion.1
  351.0 25.6 %all-gather.2.cloned.1.call-done = bf16[1024,1024]{1,0:T(8,128)(2,1)} async-done(((bf16[256,1024]{1,0:T(8,128)(2,1)}), bf16[1024,1024]{1,0:T(8,128)(2,1)}) %all-gather.2.cloned.1.call-update) | async-done | bytes 2097168 | tf_op jit(solution)/shard_map/all_gather | solution.py:82
  376.6 2.4 fusion.10
  379.0 0.1 reduce_sum.48
  379.2 0.1 copy.45
  379.2 0.7 select_reduce_fusion
  (42 shorter events, 0.4 us)
Async XLA Ops:
  7.2 336.5 %copy-start = (bf16[1024,1024]{1,0:T(8,128)(2,1)S(1)}, bf16[1024,1024]{1,0:T(8,128)(2,1)}, u32[]{:S(2)}) copy-start(bf16[1024,1024]{1,0:T(8,128)(2,1)} %param.20) | copy-start | bytes 6291460
  28.2 17.0 %copy-start.5 = (s32[2]{0:T(128)S(1)}, s32[2]{0:T(128)}, u32[]{:S(2)}) copy-start(s32[2]{0:T(128)} %constant.179) | copy-start | bytes 28
  28.2 47.4 %copy-start.1 = (bf16[256,1024]{1,0:T(8,128)(2,1)S(1)}, bf16[256,1024]{1,0:T(8,128)(2,1)}, u32[]{:S(2)}) copy-start(bf16[256,1024]{1,0:T(8,128)(2,1)} %param.16) | copy-start | bytes 1572868
  101.2 6.2 %copy-start.4 = (s32[2]{0:T(128)S(1)}, s32[2]{0:T(128)}, u32[]{:S(2)}) copy-start(s32[2]{0:T(128)} %param.24) | copy-start | bytes 28
  101.2 8.1 %copy-start.3 = (s32[256,8]{0,1:T(8,128)S(1)}, s32[256,8]{0,1:T(8,128)}, u32[]{:S(2)}) copy-start(s32[256,8]{0,1:T(8,128)} %param.23) | copy-start | bytes 24580
  101.2 191.7 %all-to-all-start.1 = ((bf16[64,64,1024]{2,1,0:T(8,128)(2,1)}), bf16[64,64,1024]{2,1,0:T(8,128)(2,1)}, u32[]{:S(2)}, u32[]{:S(2)}) async-start(bf16[64,64,1024]{2,1,0:T(8,128)(2,1)} %broadcast_select_fusion), calls=%async_computation.1 | async-start | bytes 16777216 | tf_op jit(solution)/shard_map/all_to_all | solution.py:46
  107.1 269.5 %all-gather.2.cloned.1.call-start = ((), (), s32[]{:S(2)}) async-start(), calls=%async_computation.2 | async-start | bytes 2621440 | tf_op jit(solution)/shard_map/all_gather | solution.py:82
  292.9 41.1 %copy-start.6 = (f32[1024]{0:T(1024)S(1)}, f32[1024]{0:T(1024)}, u32[]{:S(2)}) copy-start(f32[1024]{0:T(1024)} %param.18) | copy-start | bytes 12292
  334.0 9.6 %copy-start.2 = (f32[256,1024]{1,0:T(8,128)S(1)}, f32[256,1024]{1,0:T(8,128)}, u32[]{:S(2)}) copy-start(f32[256,1024]{1,0:T(8,128)} %fusion.33) | copy-start | bytes 3145732
  334.0 9.6 %copy-start.7 = (f32[1024]{0:T(1024)S(1)}, f32[1024]{0:T(1024)}, u32[]{:S(2)}) copy-start(f32[1024]{0:T(1024)} %param.21) | copy-start | bytes 12292
  343.7 3.1 copy-start.8
  343.7 3.2 copy-start.9
  343.7 3.2 copy-start.10
Sparse Core Ops, SparseCore 0:
  346.9 29.6 all-gather.1
where the time goes:
time: 388 us; the launch traced here: 387 us
  waiting for transfers between devices  206 us (53%)
  local copies, waits for them, and re-layouts  91.2 us (24%)
  other arithmetic  29.9 us (8%)
  blocking collectives  22.1 us (6%)
  matrix products  17.4 us (4%)
  between operations  14.4 us (4%)
  starting transfers between devices  6.13 us (2%)
    all_to_all x1, waiting for transfers between devices, body(): lax.all_to_all(outgoing, 'shard', split_axis=0, concat_axis=0, tiled=True)  180 us
    gather x1, local copies, waits for them, and re-layouts, body(): gathered = incoming[owners, slot_rank]  41.1 us
    all_gather x1, waiting for transfers between devices, body(): lax.all_gather(embedding, 'region', axis=0, tiled=True)  25.6 us
    all_to_all x1, blocking collectives, body(): lax.all_to_all(requests, 'shard', split_axis=0, concat_axis=0, tiled=True)  22.1 us
    another operation x3, other arithmetic  18.5 us
    gather x1, local copies, waits for them, and re-layouts, body(): outgoing = jnp.take(features, wanted, axis=0)  18.3 us
    gather x1, local copies, waits for them, and re-layouts, body(): slot_rank = jnp.take_along_axis(before, owners[:, None], axis=1)[:, 0]  16.8 us
    dot_general x1, matrix products, body(): jnp.einsum('ik,ikh->ih', slot_weight.astype(jnp.bfloat16), slot_proj, pre...  9.62 us
  transfers between devices with their start and end apart: 2, of which 2 were waited for; matrix products, arithmetic and copies ran while one was open for 2% of the time, Pallas kernels for 0%

commit v1 on v0

v1 whole, which is shorter than its diff:
```python
import jax
import jax.numpy as jnp
from jax import lax
from jax.sharding import PartitionSpec as P

score_scale = 32.0
margin_value = 1.0
norm_eps = 1e-06


def exclusive_counts(onehot, chunk):
    n, m = onehot.shape
    blocks = n // chunk
    oh = onehot.reshape(blocks, chunk, m)
    ii = lax.broadcasted_iota(jnp.int32, (chunk, chunk), 0)
    jj = lax.broadcasted_iota(jnp.int32, (chunk, chunk), 1)
    tri = (jj < ii).astype(jnp.bfloat16)
    within = jnp.einsum("ij,bjo->bio", tri, oh, preferred_element_type=jnp.float32)
    totals = jnp.sum(oh.astype(jnp.float32), axis=1)
    bi = lax.broadcasted_iota(jnp.int32, (blocks, blocks), 0)
    bj = lax.broadcasted_iota(jnp.int32, (blocks, blocks), 1)
    btri = (bj < bi).astype(jnp.float32)
    offsets = jnp.dot(btri, totals, precision=lax.Precision.HIGHEST)
    return (within + offsets[:, None, :]).reshape(n, m)


def body(
    features,
    proj_weight,
    proj_bias,
    self_weight,
    nbr_weight,
    out_bias,
    nbr_ids,
    nbr_counts,
    live_slots,
    query_ids,
    positive_ids,
    neg_blocks,
):
    item_dev = features.shape[0]
    hidden = proj_weight.shape[1]
    fanout = nbr_ids.shape[1]
    block_rows = item_dev // live_slots.shape[0]
    shards = lax.axis_size("shard")
    slots = item_dev * fanout
    capacity = max(2, 2 * slots // shards)

    projected = jnp.maximum(
        jnp.dot(features, proj_weight, preferred_element_type=jnp.float32) + proj_bias, 0.0
    ).astype(jnp.bfloat16)

    live_item = jnp.repeat(live_slots, block_rows, total_repeat_length=item_dev)
    slot_weight = jnp.where(
        jnp.arange(fanout, dtype=jnp.int32)[None, :] < live_item[:, None], nbr_counts, 0
    )
    weight_sum = jnp.sum(slot_weight.astype(jnp.float32), axis=1, keepdims=True)

    flat_ids = nbr_ids.reshape(-1)
    owners = flat_ids // item_dev
    local_row = flat_ids % item_dev
    owner_hot = owners[:, None] == jnp.arange(shards, dtype=jnp.int32)[None, :]
    counts = exclusive_counts(owner_hot.astype(jnp.bfloat16), 128)
    slot_rank = jnp.sum(jnp.where(owner_hot, counts, 0.0), axis=1).astype(jnp.int32)
    rank_hot = slot_rank[:, None] == jnp.arange(capacity, dtype=jnp.int32)[None, :]
    row_by_rank = jnp.where(rank_hot, local_row[:, None].astype(jnp.float32), 0.0)
    requests = jnp.dot(
        owner_hot.astype(jnp.bfloat16).T,
        row_by_rank.astype(jnp.bfloat16),
        preferred_element_type=jnp.float32,
    ).astype(jnp.int32)
    wanted = lax.all_to_all(requests, "shard", split_axis=0, concat_axis=0, tiled=True)
    pick = (
        wanted.reshape(-1)[:, None] == jnp.arange(item_dev, dtype=jnp.int32)[None, :]
    ).astype(jnp.bfloat16)
    outgoing = jnp.dot(pick, projected, preferred_element_type=jnp.float32).astype(jnp.bfloat16)
    outgoing = outgoing.reshape(shards, capacity, hidden)
    incoming = lax.all_to_all(outgoing, "shard", split_axis=0, concat_axis=0, tiled=True)

    column = (owners * capacity + slot_rank).reshape(item_dev, fanout)
    spread = jnp.where(
        column[:, :, None] == jnp.arange(shards * capacity, dtype=jnp.int32)[None, None, :],
        slot_weight[:, :, None].astype(jnp.float32),
        0.0,
    )
    mix = jnp.sum(spread, axis=1).astype(jnp.bfloat16)
    summed = jnp.dot(
        mix, incoming.reshape(shards * capacity, hidden), preferred_element_type=jnp.float32
    )
    aggregate = (summed / weight_sum).astype(jnp.bfloat16)
    activation = (
        jnp.dot(features, self_weight, preferred_element_type=jnp.float32)
        + jnp.dot(aggregate, nbr_weight, preferred_element_type=jnp.float32)
        + out_bias
    )
    activation = jnp.maximum(activation, 0.0)
    embedding = (
        activation * lax.rsqrt(jnp.mean(activation * activation, axis=-1, keepdims=True) + norm_eps)
    ).astype(jnp.bfloat16)

    items = jnp.arange(item_dev, dtype=jnp.int32)[None, :]
    query_pick = (query_ids[:, None] == items).astype(jnp.bfloat16)
    positive_pick = (positive_ids[:, None] == items).astype(jnp.bfloat16)
    query_emb = jnp.dot(query_pick, embedding, preferred_element_type=jnp.float32)
    positive_emb = jnp.dot(positive_pick, embedding, preferred_element_type=jnp.float32)
    positive_score = score_scale / hidden * jnp.sum(query_emb * positive_emb, axis=-1)
    neg_lists = neg_blocks[0]
    scores = (
        score_scale
        / hidden
        * jnp.dot(
            query_emb.astype(jnp.bfloat16),
            lax.all_gather(embedding, "region", axis=0, tiled=True).T,
            preferred_element_type=jnp.float32,
        )
    )
    hinge_all = jnp.maximum(scores - positive_score[:, None] + margin_value, 0.0)
    block_mean = jnp.mean(hinge_all.reshape(query_emb.shape[0], -1, block_rows), axis=-1)
    pool_ids = jnp.arange(block_mean.shape[1], dtype=jnp.int32)
    picked = jnp.where(
        neg_lists[None, :, None] == pool_ids[None, None, :], block_mean[:, None, :], 0.0
    )
    hinge_terms = jnp.sum(picked, axis=-1)
    return (embedding, hinge_terms)


def solution(mesh):
    in_specs = (
        P(("region", "shard"), None),
        P(),
        P(),
        P(),
        P(),
        P(),
        P(("region", "shard"), None),
        P(("region", "shard"), None),
        P(("region", "shard")),
        P(("region", "shard")),
        P(("region", "shard")),
        P(("region", "shard"), None),
    )
    out_specs = (P(("region", "shard"), None), P(("region", "shard"), None))
    return jax.shard_map(body, mesh=mesh, in_specs=in_specs, out_specs=out_specs, check_vma=False)
```

time: 388 us -> 283 us (0.73)
  local copies, waits for them, and re-layouts: 91.2 us -> 2.91 us
  waiting for transfers between devices: 206 us -> 190 us
  other arithmetic: 29.9 us -> 23.7 us
  matrix products: 17.4 us -> 23.4 us
    gather x5 -> x0, local copies, waits for them, and re-layouts: 80 us -> none  [the longest x1 41.1 us: body(): gathered = incoming[owners, slot_rank]]
    another operation x3 -> x0, other arithmetic: 18.5 us -> none
    reduce_sum x2 -> x3, other arithmetic: 0.9 us -> 19.2 us  [the longest x1 18.3 us: body(): mix = jnp.sum(spread, axis=1).astype(jnp.bfloat16)]
    all_to_all x1, waiting for transfers between devices: 180 us -> 162 us  [body(): lax.all_to_all(outgoing, 'shard', split_axis=0, concat_axis=0, tiled=True)]
    unnamed x26 -> x22, local copies, waits for them, and re-layouts: 9.14 us -> 1.07 us
    select_n x6 -> x0, other arithmetic: 7.36 us -> none  [the longest x2 7.29 us: body(): outgoing = jnp.take(features, wanted, axis=0)]
    dot_general x1, matrix products: 2.14 us -> 8.55 us  [body(): jnp.dot(aggregate, nbr_weight, preferred_element_type=jnp.float32)]
    dot_general x2 -> x7, matrix products: 12 us -> 12.4 us  [the longest x1 5.59 us: body(): jnp.dot(pick, projected, preferred_element_type=jnp.float32)]
  transfers between devices with their start and end apart: 2 -> 2, of which waited for: 2 -> 2; matrix products, arithmetic and copies ran while one was open for 2% -> 9% of each run, Pallas kernels for 0% -> 0%
where the time goes in v1:
time: 283 us; the launch traced here: 282 us
  waiting for transfers between devices  190 us (67%)
  other arithmetic  23.7 us (8%)
  matrix products  23.4 us (8%)
  blocking collectives  22.1 us (8%)
  between operations  14.3 us (5%)
  starting transfers between devices  6.13 us (2%)
  local copies, waits for them, and re-layouts  2.91 us (1%)
    all_to_all x1, waiting for transfers between devices, body(): lax.all_to_all(outgoing, 'shard', split_axis=0, concat_axis=0, tiled=True)  162 us
    all_gather x1, waiting for transfers between devices, body(): lax.all_gather(embedding, 'region', axis=0, tiled=True)  27.3 us
    all_to_all x1, blocking collectives, body(): lax.all_to_all(requests, 'shard', split_axis=0, concat_axis=0, tiled=True)  22.1 us
    reduce_sum x1, other arithmetic, body(): mix = jnp.sum(spread, axis=1).astype(jnp.bfloat16)  18.3 us
    dot_general x1, matrix products, body(): jnp.dot(aggregate, nbr_weight, preferred_element_type=jnp.float32)  8.55 us
    all_to_all x1, starting transfers between devices, body(): lax.all_to_all(outgoing, 'shard', split_axis=0, concat_axis=0, tiled=True)  5.9 us
  transfers between devices with their start and end apart: 2, of which 2 were waited for; matrix products, arithmetic and copies ran while one was open for 9% of the time, Pallas kernels for 0%

profile of v1, /device:TPU:1, one launch (start us, length us, event | category | flops | bytes accessed | tf_op | source)
XLA Modules:
  0.0 282.1 jit_solution(14949762110008972222)
XLA Ops:
  7.2 0.0 copy-start
  7.2 0.0 copy-start.1
  7.2 0.0 copy-start.7
  7.2 1.0 copy.60
  8.2 0.1 reshape.271
  8.3 0.1 reshape.272
  8.4 0.2 convert_reduce_fusion
  8.6 0.1 fusion.45
  8.8 0.3 fusion.15
  9.1 1.3 convolution_convert_fusion.1
  10.4 22.1 %all_to_all.14 = s32[64,1,64]{2,1,0:T(1,128)S(1)} all-to-all(s32[64,1,64]{2,1,0:T(1,128)S(1)} %bitcast.42), channel_id=1, replica_groups=mesh['region'=4,'shard'=64] {'shard'}, dimensions={0} | all-to-all | bytes 32768 | tf_op jit(solution)/shard_map/all_to_all | solution.py:72
  32.5 0.5 broadcast.306
  33.0 0.7 reduce.6
  33.8 0.1 eq.123
  33.8 0.0 copy-done
  33.8 0.0 copy-done.1
  33.8 0.0 copy-done.7
  33.9 5.6 %convolution_convert_fusion = bf16[4096,1024]{1,0:T(8,128)(2,1)} fusion(s32[4096]{0:T(1024)S(1)} %eq.123, bf16[256,1024]{1,0:T(8,128)(2,1)S(1)} %copy-done.1, bf16[1024,1024]{1,0:T(8,128)(2,1)S(1)} %copy-done, f32[1024]{0:T(1024)S(1)} %copy-done.7), kind=kOutput, calls=%fused_computation.2 | convolution fusion | flops 2690383872 | bytes 11030528 | tf_op jit(solution)/shard_map/dot_general | solution.py:76
  39.4 5.9 %all-to-all-start.1 = ((bf16[64,64,1024]{2,1,0:T(8,128)(2,1)}), bf16[64,64,1024]{2,1,0:T(8,128)(2,1)}, u32[]{:S(2)}, u32[]{:S(2)}) async-start(bf16[64,64,1024]{2,1,0:T(8,128)(2,1)} %bitcast.40), calls=%async_computation.1 | async-start | bytes 16777216 | tf_op jit(solution)/shard_map/all_to_all | solution.py:78
  45.4 0.2 all-gather.2.cloned.1.call-start
  45.6 0.1 convert_element_type.68
  45.7 0.1 copy.61
  45.8 0.0 copy-done.2
  45.8 0.1 copy.62
  45.9 0.0 copy-done.4
  45.9 0.6 fusion.54
  46.5 1.3 compare_select_fusion.1
  47.8 0.0 copy-done.3
  47.9 0.1 copy.63
  48.0 2.5 fusion.55
  50.5 0.0 copy-start.8
  50.5 18.3 %select_reduce_fusion = bf16[256,4096]{1,0:T(8,128)(2,1)} fusion(f32[256,8]{1,0:T(8,128)S(1)} %copy.63, s32[256,8]{1,0:T(8,128)S(1)} %copy.62), kind=kLoop, calls=%fused_computation | loop fusion | flops 24117248 | bytes 2113536 | tf_op jit(solution)/shard_map/reduce_sum | solution.py:86
  68.8 162.3 %all-to-all-done.1 = bf16[64,64,1024]{2,1,0:T(8,128)(2,1)} async-done(((bf16[64,64,1024]{2,1,0:T(8,128)(2,1)}), bf16[64,64,1024]{2,1,0:T(8,128)(2,1)}, u32[]{:S(2)}, u32[]{:S(2)}) %all-to-all-start.1) | async-done | bytes 8388640 | tf_op jit(solution)/shard_map/all_to_all | solution.py:78
  231.1 0.0 copy-done.8
  231.1 8.5 %multiply_reduce_fusion = (f32[256]{0:T(256)S(1)}, f32[256,1024]{1,0:T(8,128)}) fusion(f32[1024]{0:T(1024)S(1)} %copy-done.8, f32[256,1024]{1,0:T(8,128)S(1)} %fusion.55, bf16[1024,1024]{1,0:T(8,128)(2,1)} %param.18, bf16[4096,1024]{1,0:T(8,128)(2,1)} %bitcast.13, bf16[256,4096]{1,0:T(8,128)(2,1)} %select_reduce_fusion, f32[256]{0:T(256)S(1)} %get-tuple-element.14), kind=kOutput, calls=%fused_computation.28 | convolution fusion | flops 2686189312 | bytes 14686208 | tf_op jit(solution)/shard_map/dot_general | solution.py:93
  239.7 2.2 multiply_convert_fusion
  241.9 0.0 all-gather.2.cloned.1.call-update
  241.9 0.0 copy-done.9
  241.9 0.1 iota_compare_fusion.16
  242.0 0.0 copy-done.6
  242.0 1.3 fusion.35
  243.3 0.0 copy-done.5
  243.3 1.4 fusion.20
  244.7 27.3 %all-gather.2.cloned.1.call-done = bf16[1024,1024]{1,0:T(8,128)(2,1)} async-done(((bf16[256,1024]{1,0:T(8,128)(2,1)}), bf16[1024,1024]{1,0:T(8,128)(2,1)}) %all-gather.2.cloned.1.call-update) | async-done | bytes 2097168 | tf_op jit(solution)/shard_map/all_gather | solution.py:113
  272.0 2.4 fusion.19
  274.4 0.1 reduce_sum.78
  274.5 0.1 copy.66
  274.6 0.7 select_reduce_fusion.1
  (18 shorter events, 0.2 us)
Async XLA Ops:
  7.2 26.7 %copy-start = (bf16[1024,1024]{1,0:T(8,128)(2,1)S(1)}, bf16[1024,1024]{1,0:T(8,128)(2,1)}, u32[]{:S(2)}) copy-start(bf16[1024,1024]{1,0:T(8,128)(2,1)} %param.15) | copy-start | bytes 6291460
  7.2 26.7 %copy-start.1 = (bf16[256,1024]{1,0:T(8,128)(2,1)S(1)}, bf16[256,1024]{1,0:T(8,128)(2,1)}, u32[]{:S(2)}) copy-start(bf16[256,1024]{1,0:T(8,128)(2,1)} %param.14) | copy-start | bytes 1572868
  7.2 26.7 %copy-start.7 = (f32[1024]{0:T(1024)S(1)}, f32[1024]{0:T(1024)}, u32[]{:S(2)}) copy-start(f32[1024]{0:T(1024)} %param.16) | copy-start | bytes 12292
  39.4 6.3 %copy-start.2 = (s32[256,8]{0,1:T(8,128)S(1)}, s32[256,8]{0,1:T(8,128)}, u32[]{:S(2)}) copy-start(s32[256,8]{0,1:T(8,128)} %param.20) | copy-start | bytes 24580
  39.4 6.5 %copy-start.4 = (s32[2]{0:T(128)S(1)}, s32[2]{0:T(128)}, u32[]{:S(2)}) copy-start(s32[2]{0:T(128)} %param.22) | copy-start | bytes 28
  39.4 8.4 %copy-start.3 = (s32[256,8]{0,1:T(8,128)S(1)}, s32[256,8]{0,1:T(8,128)}, u32[]{:S(2)}) copy-start(s32[256,8]{0,1:T(8,128)} %param.21) | copy-start | bytes 24580
  39.4 191.7 %all-to-all-start.1 = ((bf16[64,64,1024]{2,1,0:T(8,128)(2,1)}), bf16[64,64,1024]{2,1,0:T(8,128)(2,1)}, u32[]{:S(2)}, u32[]{:S(2)}) async-start(bf16[64,64,1024]{2,1,0:T(8,128)(2,1)} %bitcast.40), calls=%async_computation.1 | async-start | bytes 16777216 | tf_op jit(solution)/shard_map/all_to_all | solution.py:78
  45.4 226.6 %all-gather.2.cloned.1.call-start = ((), (), s32[]{:S(2)}) async-start(), calls=%async_computation.2 | async-start | bytes 2621440 | tf_op jit(solution)/shard_map/all_gather | solution.py:113
  50.5 180.7 %copy-start.8 = (f32[1024]{0:T(1024)S(1)}, f32[1024]{0:T(1024)}, u32[]{:S(2)}) copy-start(f32[1024]{0:T(1024)} %param.19) | copy-start | bytes 12292
  239.7 2.2 copy-start.9
  239.7 2.3 copy-start.6
  239.7 3.6 %copy-start.5 = (s32[64]{0:T(128)S(1)}, s32[64]{0:T(128)}, u32[]{:S(2)}) copy-start(s32[64]{0:T(128)} %param.24) | copy-start | bytes 772
Sparse Core Ops, SparseCore 0:
  242.0 29.8 all-gather.1

commit v2 on v1

--- a/solution.py
+++ b/solution.py
@@ -59,34 +59,69 @@
     flat_ids = nbr_ids.reshape(-1)
     owners = flat_ids // item_dev
     local_row = flat_ids % item_dev
-    owner_hot = owners[:, None] == jnp.arange(shards, dtype=jnp.int32)[None, :]
-    counts = exclusive_counts(owner_hot.astype(jnp.bfloat16), 128)
-    slot_rank = jnp.sum(jnp.where(owner_hot, counts, 0.0), axis=1).astype(jnp.int32)
-    rank_hot = slot_rank[:, None] == jnp.arange(capacity, dtype=jnp.int32)[None, :]
-    row_by_rank = jnp.where(rank_hot, local_row[:, None].astype(jnp.float32), 0.0)
-    requests = jnp.dot(
-        owner_hot.astype(jnp.bfloat16).T,
-        row_by_rank.astype(jnp.bfloat16),
-        preferred_element_type=jnp.float32,
-    ).astype(jnp.int32)
-    wanted = lax.all_to_all(requests, "shard", split_axis=0, concat_axis=0, tiled=True)
-    pick = (
-        wanted.reshape(-1)[:, None] == jnp.arange(item_dev, dtype=jnp.int32)[None, :]
-    ).astype(jnp.bfloat16)
-    outgoing = jnp.dot(pick, projected, preferred_element_type=jnp.float32).astype(jnp.bfloat16)
-    outgoing = outgoing.reshape(shards, capacity, hidden)
-    incoming = lax.all_to_all(outgoing, "shard", split_axis=0, concat_axis=0, tiled=True)
 
-    column = (owners * capacity + slot_rank).reshape(item_dev, fanout)
-    spread = jnp.where(
-        column[:, :, None] == jnp.arange(shards * capacity, dtype=jnp.int32)[None, None, :],
-        slot_weight[:, :, None].astype(jnp.float32),
-        0.0,
-    )
-    mix = jnp.sum(spread, axis=1).astype(jnp.bfloat16)
-    summed = jnp.dot(
-        mix, incoming.reshape(shards * capacity, hidden), preferred_element_type=jnp.float32
-    )
+    def exchange(server, value, rank, cap, table_of):
+        server_hot = server[:, None] == jnp.arange(shards, dtype=jnp.int32)[None, :]
+        rank_hot = rank[:, None] == jnp.arange(cap, dtype=jnp.int32)[None, :]
+        lo = jnp.where(rank_hot, (value % item_dev)[:, None].astype(jnp.float32), 0.0)
+        hi = jnp.where(rank_hot, (value // item_dev)[:, None].astype(jnp.float32), 0.0)
+        both = jnp.dot(
+            server_hot.astype(jnp.bfloat16).T,
+            jnp.concatenate([lo, hi], axis=1).astype(jnp.bfloat16),
+            preferred_element_type=jnp.float32,
+        ).astype(jnp.int32)
+        requests = both[:, cap:] * item_dev + both[:, :cap]
+        wanted = lax.all_to_all(requests, "shard", split_axis=0, concat_axis=0, tiled=True)
+        table, index = table_of(wanted.reshape(-1))
+        pick = (index[:, None] == jnp.arange(table.shape[0], dtype=jnp.int32)[None, :]).astype(
+            jnp.bfloat16
+        )
+        outgoing = jnp.dot(pick, table, preferred_element_type=jnp.float32).astype(jnp.bfloat16)
+        outgoing = outgoing.reshape(shards, cap, hidden)
+        incoming = lax.all_to_all(outgoing, "shard", split_axis=0, concat_axis=0, tiled=True)
+        column = (server * cap + rank).reshape(item_dev, fanout)
+        spread = jnp.where(
+            column[:, :, None] == jnp.arange(shards * cap, dtype=jnp.int32)[None, None, :],
+            slot_weight[:, :, None].astype(jnp.float32),
+            0.0,
+        )
+        mix = jnp.sum(spread, axis=1).astype(jnp.bfloat16)
+        return jnp.dot(
+            mix, incoming.reshape(shards * cap, hidden), preferred_element_type=jnp.float32
+        )
+
+    def rank_within(group, groups):
+        hot = group[:, None] == jnp.arange(groups, dtype=jnp.int32)[None, :]
+        counts = exclusive_counts(hot.astype(jnp.bfloat16), 128)
+        rank = jnp.sum(jnp.where(hot, counts, 0.0), axis=1).astype(jnp.int32)
+        totals = jnp.sum(hot.astype(jnp.float32), axis=0)
+        return rank, totals
+
+    chips = shards // 2
+    fast_cap = capacity * 3 // 4
+    chip = owners // 2
+    chip_rank, chip_totals = rank_within(chip, chips)
+    crowded = jnp.max(chip_totals) > 2 * fast_cap
+    any_crowded = lax.pmax(crowded.astype(jnp.int32), ("region", "shard"))
+
+    def by_owner(_):
+        rank, _totals = rank_within(owners, shards)
+        return exchange(owners, local_row, rank, capacity, lambda w: (projected, w))
+
+    def by_chip(_):
+        core = lax.axis_index("shard") % 2
+        pairs = [(i, i ^ 1) for i in range(shards)]
+        sibling = lax.ppermute(projected, "shard", pairs)
+        table = jnp.concatenate([projected, sibling], axis=0)
+
+        def table_of(w):
+            return table, ((w // item_dev) ^ core) * item_dev + w % item_dev
+
+        server = chip * 2 + chip_rank % 2
+        value = (owners % 2) * item_dev + local_row
+        return exchange(server, value, chip_rank // 2, fast_cap, table_of)
+
+    summed = lax.cond(any_crowded == 0, by_chip, by_owner, 0)
     aggregate = (summed / weight_sum).astype(jnp.bfloat16)
     activation = (
         jnp.dot(features, self_weight, preferred_element_type=jnp.float32)

time: 283 us -> 345 us (1.22); the launches traced: 282 us -> 338 us
  blocking collectives: 22.1 us -> 81.4 us
  waiting for transfers between devices: 190 us -> 159 us
  starting transfers between devices: 6.13 us -> 12.6 us
  loops' own time: 0 us -> 6.12 us
  local copies, waits for them, and re-layouts: 2.91 us -> 8.79 us
  other arithmetic: 23.7 us -> 28.3 us
    pmax x0 -> x1, blocking collectives: none -> 81.4 us  [body(): any_crowded = lax.pmax(crowded.astype(jnp.int32), ('region', 'shard'))]
    all_to_all x1 -> x2, waiting for transfers between devices: 162 us -> 133 us  [the longest x1 124 us: exchange(): lax.all_to_all(outgoing, 'shard', split_axis=0, concat_axis=0, tiled=True)]
    all_to_all x1 -> x0, blocking collectives: 22.1 us -> none  [body(): lax.all_to_all(requests, 'shard', split_axis=0, concat_axis=0, tiled=True)]
    dot_general x2 -> x4, matrix products: 6.92 us -> 14.5 us  [the longest x1 7.06 us: exchange(): jnp.dot(pick, table, preferred_element_type=jnp.float32)]
    dot_general x1, matrix products: 8.55 us -> 2.12 us  [body(): jnp.dot(aggregate, nbr_weight, preferred_element_type=jnp.float32)]
    another operation x0 -> x1, loops' own time: none -> 6.12 us  [body(): summed = lax.cond(any_crowded == 0, by_chip, by_owner, 0)]
    all_to_all x1 -> x2, starting transfers between devices: 5.9 us -> 11.5 us  [the longest x1 5.89 us: exchange(): lax.all_to_all(outgoing, 'shard', split_axis=0, concat_axis=0, tiled=True)]
    reduce_sum x1 -> x3, other arithmetic: 18.3 us -> 18.5 us  [the longest x1 16.4 us: exchange(): mix = jnp.sum(spread, axis=1).astype(jnp.bfloat16)]
  transfers between devices with their start and end apart: 2 -> 4, of which waited for: 2 -> 3; matrix products, arithmetic and copies ran while one was open for 9% -> 8% of each run, Pallas kernels for 0% -> 0%
where the time goes in v2:
time: 345 us; the launch traced here: 338 us
  waiting for transfers between devices  159 us (46%)
  blocking collectives  81.4 us (24%)
  other arithmetic  28.3 us (8%)
  matrix products  26.4 us (8%)
  between operations  15.8 us (5%)
  starting transfers between devices  12.6 us (4%)
  local copies, waits for them, and re-layouts  8.79 us (3%)
  loops' own time  6.12 us (2%)
    all_to_all x1, waiting for transfers between devices, exchange(): lax.all_to_all(outgoing, 'shard', split_axis=0, concat_axis=0, tiled=True)  124 us
    pmax x1, blocking collectives, body(): any_crowded = lax.pmax(crowded.astype(jnp.int32), ('region', 'shard'))  81.4 us
    all_gather x1, waiting for transfers between devices, body(): lax.all_gather(embedding, 'region', axis=0, tiled=True)  25.2 us
    reduce_sum x1, other arithmetic, exchange(): mix = jnp.sum(spread, axis=1).astype(jnp.bfloat16)  16.4 us
    all_to_all x1, waiting for transfers between devices, exchange(): lax.all_to_all(requests, 'shard', split_axis=0, concat_axis=0, tiled=True)  9.3 us
    dot_general x1, matrix products, exchange(): jnp.dot(pick, table, preferred_element_type=jnp.float32)  7.06 us
  transfers between devices with their start and end apart: 4, of which 3 were waited for; matrix products, arithmetic and copies ran while one was open for 8% of the time, Pallas kernels for 0%

profile of v2, /device:TPU:1, one launch (start us, length us, event | category | flops | bytes accessed | tf_op | source)
XLA Modules:
  0.0 338.1 jit_solution(16584266343315895675)
XLA Ops:
  7.2 1.0 copy.45
  8.2 0.1 reshape.348
  8.3 0.6 negate_select_fusion.21
  8.9 0.6 fusion.83
  9.5 0.6 broadcast_compare_fusion
  10.1 0.1 reshape.349
  10.2 0.6 convolution_bitcast_fusion
  10.8 0.3 convert_reduce_fusion.1
  11.2 1.3 fusion.89
  12.5 1.3 compare_select_fusion.1
  13.9 0.7 fusion.82
  14.6 0.1 convert_reduce_fusion.2
  14.8 0.6 reduce_max.9
  16.0 0.8 copy.46
  16.8 81.4 %pmax.7 = s32[]{:T(128)} all-reduce(s32[]{:T(128)S(6)} %convert_element_type.110), channel_id=1, replica_groups=mesh['region'=4,'shard'=64] {'region','shard'}, use_global_device_ids=true, to_apply=%region_2.3 | all-reduce | flops 1 | bytes 8 | tf_op jit(solution)/shard_map/pmax | solution.py:105
  98.9 0.7 convert_reduce_fusion.3
  99.7 3.5 %fusion.92 = f32[256,1024]{1,0:T(8,128)} fusion(bf16[256,1024]{1,0:T(8,128)(2,1)} %param.16, bf16[1024,1024]{1,0:T(8,128)(2,1)} %param.19), kind=kOutput, calls=%fused_computation.198 | convolution fusion | flops 536870912 | bytes 3670016 | tf_op jit(solution)/shard_map/dot_general | solution.py:127
  103.2 1.5 fusion.58
  104.7 1.3 eq.218
  106.0 1.1 eq.219
  107.1 0.6 broadcast.390
  107.7 0.6 broadcast.391
  108.3 0.6 ne.146
  108.9 187.7 %conditional.1 = (f32[256,1024]{1,0:T(8,128)S(1)}) conditional(s32[]{:T(128)} %convert_element_type.111, (s32[2048]{0:T(1024)S(1)}, s32[256,8]{1,0:T(8,128)S(1)}, s32[2048]{0:T(1024)S(1)}, bf16[256,1024]{1,0:T(8,128)(2,1)}) %tuple.18, (s32[2048]{0:T(1024)S(1)}, s32[2048]{0:T(1024)}, s32[2048]{0:T(1024)}, pred[2048]{0:T(1024)(128)(4,1)}, ...), branch_computations={%region_4.8_spmd, %region_8.11_spmd} | conditional | flops 4883597312 | bytes 49127476 | solution.py:124
  114.5 1.0 collective-permute-start
  115.5 0.3 copy.49
  115.9 1.9 select_reduce_fusion.2
  117.9 1.6 select_convert_fusion.3
  119.6 0.9 convolution_convert_fusion.2
  120.4 0.7 slice_add_fusion.1
  121.1 5.6 %all-to-all-start.2 = ((s32[64,1,48]{2,1,0:T(1,128)}), s32[64,1,48]{2,1,0:T(1,128)S(1)}, u32[]{:S(2)}, u32[]{:S(2)}) async-start(s32[64,1,48]{2,1,0:T(1,128)} %bitcast.10), calls=%async_computation.2 | async-start | bytes 65536 | tf_op jit(solution)/shard_map/cond/branch_1_fun/all_to_all | solution.py:74
  126.8 9.3 %all-to-all-done.2 = s32[64,1,48]{2,1,0:T(1,128)S(1)} async-done(((s32[64,1,48]{2,1,0:T(1,128)}), s32[64,1,48]{2,1,0:T(1,128)S(1)}, u32[]{:S(2)}, u32[]{:S(2)}) %all-to-all-start.2) | async-done | bytes 12320 | tf_op jit(solution)/shard_map/cond/branch_1_fun/all_to_all | solution.py:74
  136.1 0.6 broadcast.481
  136.7 0.8 reduce.12
  137.6 7.1 %fusion.21 = bf16[3072,1024]{1,0:T(8,128)(2,1)} fusion(s32[3072]{0:T(1024)S(1)} %fusion.34, bf16[256,1024]{1,0:T(8,128)(2,1)} %collective-permute-done, bf16[256,1024]{1,0:T(8,128)(2,1)} %get-tuple-element.89), kind=kOutput, calls=%fused_computation.47 | convolution fusion | flops 3228041216 | bytes 7352320 | tf_op jit(solution)/shard_map/cond/branch_1_fun/dot_general | solution.py:79
  144.6 5.9 %all-to-all-start.3 = ((bf16[64,48,1024]{2,1,0:T(8,128)(2,1)}), bf16[64,48,1024]{2,1,0:T(8,128)(2,1)}, u32[]{:S(2)}, u32[]{:S(2)}) async-start(bf16[64,48,1024]{2,1,0:T(8,128)(2,1)} %bitcast.87), calls=%async_computation.3 | async-start | bytes 12582912 | tf_op jit(solution)/shard_map/cond/branch_1_fun/all_to_all | solution.py:81
  150.5 0.1 eq.154
  150.7 16.4 %select_reduce_fusion.1 = bf16[256,3072]{1,0:T(8,128)(2,1)} fusion(f32[256,8]{1,0:T(8,128)S(1)} %convert_element_type.93, s32[256,8]{1,0:T(8,128)S(1)} %eq.154), kind=kLoop, calls=%fused_computation.43 | loop fusion | flops 18087936 | bytes 1589248 | tf_op jit(solution)/shard_map/cond/branch_1_fun/reduce_sum | solution.py:88
  167.1 124.1 %all-to-all-done.3 = bf16[64,48,1024]{2,1,0:T(8,128)(2,1)} async-done(((bf16[64,48,1024]{2,1,0:T(8,128)(2,1)}), bf16[64,48,1024]{2,1,0:T(8,128)(2,1)}, u32[]{:S(2)}, u32[]{:S(2)}) %all-to-all-start.3) | async-done | bytes 6291488 | tf_op jit(solution)/shard_map/cond/branch_1_fun/all_to_all | solution.py:81
  291.2 5.1 %fusion.91 = f32[256,1024]{1,0:T(8,128)S(1)} fusion(bf16[256,3072]{1,0:T(8,128)(2,1)} %select_reduce_fusion.1, bf16[3072,1024]{1,0:T(8,128)(2,1)} %bitcast.12), kind=kOutput, calls=%fused_computation.197 | convolution fusion | flops 1610612736 | bytes 8912896 | tf_op jit(solution)/shard_map/cond/branch_1_fun/dot_general | solution.py:89
  296.5 2.1 multiply_reduce_fusion
  298.7 0.9 multiply_convert_fusion
  299.7 1.3 fusion.72
  301.0 1.4 fusion.63
  302.5 25.2 %all-gather.2.cloned.1.call-done = bf16[1024,1024]{1,0:T(8,128)(2,1)} async-done(((bf16[256,1024]{1,0:T(8,128)(2,1)}), bf16[1024,1024]{1,0:T(8,128)(2,1)}) %all-gather.2.cloned.1.call-update) | async-done | bytes 2097168 | tf_op jit(solution)/shard_map/all_gather | solution.py:148
  327.7 2.4 fusion.62
  330.1 0.1 reduce_sum.113
  330.3 0.7 select_reduce_fusion.3
  (43 shorter events, 0.5 us)
Async XLA Ops:
  7.2 289.4 %copy-start = (bf16[1024,1024]{1,0:T(8,128)(2,1)S(1)}, bf16[1024,1024]{1,0:T(8,128)(2,1)}, u32[]{:S(2)}) copy-start(bf16[1024,1024]{1,0:T(8,128)(2,1)} %param.20) | copy-start | bytes 6291460
  7.2 320.5 %all-gather.2.cloned.1.call-start = ((), (), s32[]{:S(2)}) async-start(), calls=%async_computation.4 | async-start | bytes 2621440 | tf_op jit(solution)/shard_map/all_gather | solution.py:148
  10.8 92.3 %copy-start.1 = (bf16[256,1024]{1,0:T(8,128)(2,1)S(1)}, bf16[256,1024]{1,0:T(8,128)(2,1)}, u32[]{:S(2)}) copy-start(bf16[256,1024]{1,0:T(8,128)(2,1)} %param.16) | copy-start | bytes 1572868
  10.8 92.3 %copy-start.11 = (f32[1024]{0:T(1024)S(1)}, f32[1024]{0:T(1024)}, u32[]{:S(2)}) copy-start(f32[1024]{0:T(1024)} %param.18) | copy-start | bytes 12292
  98.9 4.2 %copy-start.10 = (bf16[1024,1024]{1,0:T(8,128)(2,1)S(1)}, bf16[1024,1024]{1,0:T(8,128)(2,1)}, u32[]{:S(2)}) copy-start(bf16[1024,1024]{1,0:T(8,128)(2,1)} %param.17) | copy-start | bytes 6291460
  114.5 23.0 %collective-permute-start = (bf16[256,1024]{1,0:T(8,128)(2,1)}, bf16[256,1024]{1,0:T(8,128)(2,1)}, u32[]{:S(2)}, u32[]{:S(2)}) collective-permute-start(bf16[256,1024]{1,0:T(8,128)(2,1)} %get-tuple-element.89), channel_id=1, source_target_pairs={{0,1},{1,0},{2,3},{3,2},{4,5},{5,4},{6,7},{7,6},{8,9},{9,8},{10,11... | collective-permute-start | bytes 1572872 | tf_op jit(solution)/shard_map/cond/branch_1_fun/ppermute | solution.py:114
  115.8 2.0 copy-start.2
  115.8 2.0 copy-start.3
  115.9 2.0 copy-start.4
  115.9 2.0 copy-start.5
  115.9 2.0 copy-start.6
  115.9 2.0 copy-start.7
  121.1 15.0 %all-to-all-start.2 = ((s32[64,1,48]{2,1,0:T(1,128)}), s32[64,1,48]{2,1,0:T(1,128)S(1)}, u32[]{:S(2)}, u32[]{:S(2)}) async-start(s32[64,1,48]{2,1,0:T(1,128)} %bitcast.10), calls=%async_computation.2 | async-start | bytes 65536 | tf_op jit(solution)/shard_map/cond/branch_1_fun/all_to_all | solution.py:74
  144.6 146.6 %all-to-all-start.3 = ((bf16[64,48,1024]{2,1,0:T(8,128)(2,1)}), bf16[64,48,1024]{2,1,0:T(8,128)(2,1)}, u32[]{:S(2)}, u32[]{:S(2)}) async-start(bf16[64,48,1024]{2,1,0:T(8,128)(2,1)} %bitcast.87), calls=%async_computation.3 | async-start | bytes 12582912 | tf_op jit(solution)/shard_map/cond/branch_1_fun/all_to_all | solution.py:81
  298.7 1.0 copy-start.9
  298.7 2.3 copy-start.8
  298.7 3.7 %copy-start.12 = (s32[1,4]{1,0:T(1,128)S(1)}, s32[1,4]{1,0:T(1,128)}, u32[]{:S(2)}) copy-start(s32[1,4]{1,0:T(1,128)} %param.27) | copy-start | bytes 52
Sparse Core Ops, SparseCore 0:
  299.8 27.8 all-gather.1

commit v3 on v2

--- a/solution.py
+++ b/solution.py
@@ -60,7 +60,7 @@
     owners = flat_ids // item_dev
     local_row = flat_ids % item_dev
 
-    def exchange(server, value, rank, cap, table_of):
+    def make_requests(server, value, rank, cap):
         server_hot = server[:, None] == jnp.arange(shards, dtype=jnp.int32)[None, :]
         rank_hot = rank[:, None] == jnp.arange(cap, dtype=jnp.int32)[None, :]
         lo = jnp.where(rank_hot, (value % item_dev)[:, None].astype(jnp.float32), 0.0)
@@ -70,9 +70,9 @@
             jnp.concatenate([lo, hi], axis=1).astype(jnp.bfloat16),
             preferred_element_type=jnp.float32,
         ).astype(jnp.int32)
-        requests = both[:, cap:] * item_dev + both[:, :cap]
-        wanted = lax.all_to_all(requests, "shard", split_axis=0, concat_axis=0, tiled=True)
-        table, index = table_of(wanted.reshape(-1))
+        return both[:, cap:] * item_dev + both[:, :cap]
+
+    def serve(server, rank, cap, table, index):
         pick = (index[:, None] == jnp.arange(table.shape[0], dtype=jnp.int32)[None, :]).astype(
             jnp.bfloat16
         )
@@ -101,27 +101,34 @@
     fast_cap = capacity * 3 // 4
     chip = owners // 2
     chip_rank, chip_totals = rank_within(chip, chips)
-    crowded = jnp.max(chip_totals) > 2 * fast_cap
-    any_crowded = lax.pmax(crowded.astype(jnp.int32), ("region", "shard"))
+    crowded = (jnp.max(chip_totals) > 2 * fast_cap).astype(jnp.int32)
+    fast_server = chip * 2 + chip_rank % 2
+    fast_rank = chip_rank // 2
+    fast_requests = make_requests(
+        fast_server, (owners % 2) * item_dev + local_row, fast_rank, fast_cap
+    )
+    flagged = jnp.concatenate(
+        [fast_requests, jnp.broadcast_to(crowded, (shards, 1))], axis=1
+    )
+    received = lax.all_to_all(flagged, "shard", split_axis=0, concat_axis=0, tiled=True)
+    region_crowded = jnp.max(received[:, fast_cap])
+    core = lax.axis_index("shard") % 2
+    pairs = [(i, i ^ 1) for i in range(shards)]
+    sibling = lax.ppermute(projected, "shard", pairs)
 
     def by_owner(_):
         rank, _totals = rank_within(owners, shards)
-        return exchange(owners, local_row, rank, capacity, lambda w: (projected, w))
+        requests = make_requests(owners, local_row, rank, capacity)
+        wanted = lax.all_to_all(requests, "shard", split_axis=0, concat_axis=0, tiled=True)
+        return serve(owners, rank, capacity, projected, wanted.reshape(-1))
 
     def by_chip(_):
-        core = lax.axis_index("shard") % 2
-        pairs = [(i, i ^ 1) for i in range(shards)]
-        sibling = lax.ppermute(projected, "shard", pairs)
+        wanted = received[:, :fast_cap].reshape(-1)
+        index = ((wanted // item_dev) ^ core) * item_dev + wanted % item_dev
         table = jnp.concatenate([projected, sibling], axis=0)
+        return serve(fast_server, fast_rank, fast_cap, table, index)
 
-        def table_of(w):
-            return table, ((w // item_dev) ^ core) * item_dev + w % item_dev
-
-        server = chip * 2 + chip_rank % 2
-        value = (owners % 2) * item_dev + local_row
-        return exchange(server, value, chip_rank // 2, fast_cap, table_of)
-
-    summed = lax.cond(any_crowded == 0, by_chip, by_owner, 0)
+    summed = lax.cond(region_crowded == 0, by_chip, by_owner, 0)
     aggregate = (summed / weight_sum).astype(jnp.bfloat16)
     activation = (
         jnp.dot(features, self_weight, preferred_element_type=jnp.float32)

time: 345 us -> 246 us (0.71); the launches traced: 338 us -> 245 us
  blocking collectives: 81.4 us -> 0 us
  starting transfers between devices: 12.6 us -> 24 us
  waiting for transfers between devices: 159 us -> 151 us
  local copies, waits for them, and re-layouts: 8.79 us -> 2.85 us
  loops' own time: 6.12 us -> 0.3 us
  other arithmetic: 28.3 us -> 24.5 us
    pmax x1 -> x0, blocking collectives: 81.4 us -> none  [body(): any_crowded = lax.pmax(crowded.astype(jnp.int32), ('region', 'shard'))]
    all_to_all x2, starting transfers between devices: 11.5 us -> 23.5 us  [the longest x1 13 us: body(): lax.all_to_all(flagged, 'shard', split_axis=0, concat_axis=0, tiled=True)]
    all_to_all x2, waiting for transfers between devices: 133 us -> 124 us  [the longest x1 124 us: serve(): lax.all_to_all(outgoing, 'shard', split_axis=0, concat_axis=0, tiled=True)]
    another operation x1, loops' own time: 6.12 us -> 0.3 us  [body(): summed = lax.cond(region_crowded == 0, by_chip, by_owner, 0)]
    reduce_sum x2 -> x1, other arithmetic: 18.4 us -> 16.5 us  [serve(): mix = jnp.sum(spread, axis=1).astype(jnp.bfloat16)]
  transfers between devices with their start and end apart: 4 -> 4, of which waited for: 3 -> 2; matrix products, arithmetic and copies ran while one was open for 8% -> 12% of each run, Pallas kernels for 0% -> 0%
where the time goes in v3:
time: 246 us; the launch traced here: 245 us
  waiting for transfers between devices  151 us (61%)
  matrix products  27 us (11%)
  other arithmetic  24.5 us (10%)
  starting transfers between devices  24 us (10%)
  between operations  15.7 us (6%)
  local copies, waits for them, and re-layouts  2.85 us (1%)
    all_to_all x1, waiting for transfers between devices, serve(): lax.all_to_all(outgoing, 'shard', split_axis=0, concat_axis=0, tiled=True)  124 us
    all_gather x1, waiting for transfers between devices, body(): lax.all_gather(embedding, 'region', axis=0, tiled=True)  27.2 us
    reduce_sum x1, other arithmetic, serve(): mix = jnp.sum(spread, axis=1).astype(jnp.bfloat16)  16.5 us
    all_to_all x1, starting transfers between devices, body(): lax.all_to_all(flagged, 'shard', split_axis=0, concat_axis=0, tiled=True)  13 us
    all_to_all x1, starting transfers between devices, serve(): lax.all_to_all(outgoing, 'shard', split_axis=0, concat_axis=0, tiled=True)  10.5 us
    dot_general x1, matrix products, serve(): jnp.dot(pick, table, preferred_element_type=jnp.float32)  6.98 us
    dot_general x1, matrix products, serve(): jnp.dot(mix, incoming.reshape(shards * cap, hidden), preferred_element_ty...  6.04 us
  transfers between devices with their start and end apart: 4, of which 2 were waited for; matrix products, arithmetic and copies ran while one was open for 12% of the time, Pallas kernels for 0%

profile of v3, /device:TPU:1, one launch (start us, length us, event | category | flops | bytes accessed | tf_op | source)
XLA Modules:
  0.0 245.4 jit_solution(4352698795999912129)
XLA Ops:
  7.2 0.0 copy-start
  7.2 0.0 copy-start.1
  7.2 1.0 copy.38
  8.2 0.1 reshape.475
  8.3 0.1 reshape.474
  8.4 0.1 convert_reduce_fusion.2
  8.6 0.1 fusion.81
  8.7 0.2 fusion.54
  9.0 1.6 select_convert_fusion.3
  10.6 0.9 convolution_convert_fusion.2
  11.5 0.0 copy-start.5
  11.5 0.1 slice_add_fusion.1
  11.6 0.1 convert_reduce_fusion.1
  11.8 0.6 reduce_max.18
  13.0 0.6 concatenate.19
  13.6 13.0 %all-to-all-start.3 = ((s32[64,1,49]{2,1,0:T(1,128)}), s32[64,1,49]{2,1,0:T(1,128)S(1)}, u32[]{:S(2)}, u32[]{:S(2)}) async-start(s32[64,1,49]{2,1,0:T(1,128)} %bitcast.14), calls=%async_computation.3 | async-start | bytes 65536 | tf_op jit(solution)/shard_map/all_to_all | solution.py:113
  26.6 0.0 all-gather.2.cloned.1.call-start
  26.7 3.1 %fusion.47 = bf16[256,1024]{1,0:T(8,128)(2,1)} fusion(bf16[256,1024]{1,0:T(8,128)(2,1)S(1)} %copy-done.1, bf16[1024,1024]{1,0:T(8,128)(2,1)} %param.17, f32[1024]{0:T(1024)S(1)} %copy-done.8), kind=kOutput, calls=%fused_computation.89 | convolution fusion | flops 537657344 | bytes 3149824 | tf_op jit(solution)/shard_map/dot_general | solution.py:50
  29.8 0.5 collective-permute-start
  30.2 0.6 fusion.93
  30.8 1.3 compare_select_fusion.1
  32.1 0.1 copy.41
  32.3 2.5 %fusion.96 = f32[256,1024]{1,0:T(8,128)S(1)} fusion(bf16[256,1024]{1,0:T(8,128)(2,1)} %param.16, bf16[1024,1024]{1,0:T(8,128)(2,1)} %param.19), kind=kOutput, calls=%fused_computation.208 | convolution fusion | flops 536870912 | bytes 3670016 | tf_op jit(solution)/shard_map/dot_general | solution.py:134
  34.8 0.8 convert_reduce_fusion.3
  35.5 0.6 broadcast_compare_fusion.1
  36.1 0.0 all-to-all-done.3
  36.1 0.8 slice_reduce_fusion
  37.7 164.5 %conditional.1 = (f32[256,1024]{1,0:T(8,128)}) conditional(s32[]{:T(128)} %convert_element_type.132, (s32[2048]{0:T(1024)S(1)}, s32[256,8]{1,0:T(8,128)S(1)}, s32[2048]{0:T(1024)S(1)}, s32[2048]{0:T(1024)S(1)}, bf16[256,1024]{1,0:T(8,128)(2,1)}) %tuple.20, (s32[2048]{0:T(1024)S(1)}, s32[2048]{0:T(1024)S(1)}, s32[2048]{0:T(1024)S(1)}, ...), branch_computations={%region_5.9_spmd, %region_9.11_spmd} | conditional | flops 4856862720 | bytes 49135668 | solution.py:131
  37.9 0.1 reshape.468
  38.0 7.0 %fusion.1 = bf16[3072,1024]{1,0:T(8,128)(2,1)} fusion(s32[3072]{0:T(1024)S(1)} %fusion.10, bf16[256,1024]{1,0:T(8,128)(2,1)} %get-tuple-element.153, bf16[256,1024]{1,0:T(8,128)(2,1)} %get-tuple-element.152), kind=kOutput, calls=%fused_computation.4 | convolution fusion | flops 3228041216 | bytes 7352320 | tf_op jit(solution)/shard_map/cond/branch_1_fun/dot_general | solution.py:79
  45.0 10.5 %all-to-all-start.2 = ((bf16[64,48,1024]{2,1,0:T(8,128)(2,1)}), bf16[64,48,1024]{2,1,0:T(8,128)(2,1)}, u32[]{:S(2)}, u32[]{:S(2)}) async-start(bf16[64,48,1024]{2,1,0:T(8,128)(2,1)} %bitcast.88), calls=%async_computation.2 | async-start | bytes 12582912 | tf_op jit(solution)/shard_map/cond/branch_1_fun/all_to_all | solution.py:81
  55.6 0.1 eq.136
  55.7 16.5 %select_reduce_fusion = bf16[256,3072]{1,0:T(8,128)(2,1)} fusion(f32[256,8]{1,0:T(8,128)S(1)} %convert_element_type.105, s32[256,8]{1,0:T(8,128)S(1)} %eq.136), kind=kLoop, calls=%fused_computation | loop fusion | flops 18087936 | bytes 1589248 | tf_op jit(solution)/shard_map/cond/branch_1_fun/reduce_sum | solution.py:88
  72.3 123.9 %all-to-all-done.2 = bf16[64,48,1024]{2,1,0:T(8,128)(2,1)} async-done(((bf16[64,48,1024]{2,1,0:T(8,128)(2,1)}), bf16[64,48,1024]{2,1,0:T(8,128)(2,1)}, u32[]{:S(2)}, u32[]{:S(2)}) %all-to-all-start.2) | async-done | bytes 6291488 | tf_op jit(solution)/shard_map/cond/branch_1_fun/all_to_all | solution.py:81
  196.1 6.0 %fusion.94 = f32[256,1024]{1,0:T(8,128)} fusion(bf16[256,3072]{1,0:T(8,128)(2,1)} %select_reduce_fusion, bf16[3072,1024]{1,0:T(8,128)(2,1)} %bitcast.9), kind=kOutput, calls=%fused_computation.206 | convolution fusion | flops 1610612736 | bytes 8912896 | tf_op jit(solution)/shard_map/cond/branch_1_fun/dot_general | solution.py:89
  202.2 2.1 multiply_reduce_fusion
  204.3 0.0 copy-start.7
  204.3 0.0 copy-start.6
  204.3 0.9 multiply_convert_fusion
  205.2 0.0 all-gather.2.cloned.1.call-update
  205.3 0.1 iota_compare_fusion.30
  205.3 1.3 fusion.67
  206.6 1.4 fusion.55
  208.0 27.2 %all-gather.2.cloned.1.call-done = bf16[1024,1024]{1,0:T(8,128)(2,1)} async-done(((bf16[256,1024]{1,0:T(8,128)(2,1)}), bf16[1024,1024]{1,0:T(8,128)(2,1)}) %all-gather.2.cloned.1.call-update) | async-done | bytes 2097168 | tf_op jit(solution)/shard_map/all_gather | solution.py:155
  235.2 2.4 fusion.51
  237.6 0.1 reduce_sum.114
  237.8 0.1 copy.42
  237.9 0.7 select_reduce_fusion.2
  (36 shorter events, 0.3 us)
Async XLA Ops:
  7.2 195.0 %copy-start = (bf16[1024,1024]{1,0:T(8,128)(2,1)S(1)}, bf16[1024,1024]{1,0:T(8,128)(2,1)}, u32[]{:S(2)}) copy-start(bf16[1024,1024]{1,0:T(8,128)(2,1)} %param.20) | copy-start | bytes 6291460
  7.2 19.5 %copy-start.1 = (bf16[256,1024]{1,0:T(8,128)(2,1)S(1)}, bf16[256,1024]{1,0:T(8,128)(2,1)}, u32[]{:S(2)}) copy-start(bf16[256,1024]{1,0:T(8,128)(2,1)} %param.16) | copy-start | bytes 1572868
  7.2 19.5 %copy-start.8 = (f32[1024]{0:T(1024)S(1)}, f32[1024]{0:T(1024)}, u32[]{:S(2)}) copy-start(f32[1024]{0:T(1024)} %param.18) | copy-start | bytes 12292
  11.5 18.7 %copy-start.5 = (s32[2]{0:T(128)S(1)}, s32[2]{0:T(128)}, u32[]{:S(2)}) copy-start(s32[2]{0:T(128)} %param.24) | copy-start | bytes 28
  11.6 20.5 %copy-start.2 = (s32[256,8]{0,1:T(8,128)S(1)}, s32[256,8]{0,1:T(8,128)}, u32[]{:S(2)}) copy-start(s32[256,8]{0,1:T(8,128)} %param.23) | copy-start | bytes 24580
  13.6 22.5 %all-to-all-start.3 = ((s32[64,1,49]{2,1,0:T(1,128)}), s32[64,1,49]{2,1,0:T(1,128)S(1)}, u32[]{:S(2)}, u32[]{:S(2)}) async-start(s32[64,1,49]{2,1,0:T(1,128)} %bitcast.14), calls=%async_computation.3 | async-start | bytes 65536 | tf_op jit(solution)/shard_map/all_to_all | solution.py:113
  26.6 208.6 %all-gather.2.cloned.1.call-start = ((), (), s32[]{:S(2)}) async-start(), calls=%async_computation.4 | async-start | bytes 2621440 | tf_op jit(solution)/shard_map/all_gather | solution.py:155
  29.8 7.8 %collective-permute-start = (bf16[256,1024]{1,0:T(8,128)(2,1)}, bf16[256,1024]{1,0:T(8,128)(2,1)}, u32[]{:S(2)}, u32[]{:S(2)}) collective-permute-start(bf16[256,1024]{1,0:T(8,128)(2,1)} %fusion.47), channel_id=1, source_target_pairs={{0,1},{1,0},{2,3},{3,2},{4,5},{5,4},{6,7},{7,6},{8,9},{9,8},{10,11... | collective-permute-start | bytes 1572872 | tf_op jit(solution)/shard_map/ppermute | solution.py:117
  45.0 10.6 %copy-start.3 = (pred[2048]{0:T(1024)(128)(4,1)S(1)}, pred[2048]{0:T(1024)(128)(4,1)}, u32[]{:S(2)}) copy-start(pred[2048]{0:T(1024)(128)(4,1)} %get-tuple-element.146) | copy-start | bytes 6148 | tf_op jit(solution)/shard_map/cond
  45.0 10.6 %copy-start.4 = (pred[2048]{0:T(1024)(128)(4,1)S(1)}, pred[2048]{0:T(1024)(128)(4,1)}, u32[]{:S(2)}) copy-start(pred[2048]{0:T(1024)(128)(4,1)} %get-tuple-element.138) | copy-start | bytes 6148 | tf_op jit(solution)/shard_map/cond
  45.0 151.1 %all-to-all-start.2 = ((bf16[64,48,1024]{2,1,0:T(8,128)(2,1)}), bf16[64,48,1024]{2,1,0:T(8,128)(2,1)}, u32[]{:S(2)}, u32[]{:S(2)}) async-start(bf16[64,48,1024]{2,1,0:T(8,128)(2,1)} %bitcast.88), calls=%async_computation.2 | async-start | bytes 12582912 | tf_op jit(solution)/shard_map/cond/branch_1_fun/all_to_all | solution.py:81
  204.3 1.0 copy-start.9
  204.3 1.1 copy-start.7
  204.3 2.3 copy-start.6
Sparse Core Ops, SparseCore 0:
  205.4 29.8 all-gather.1

commit v4 on v3

--- a/solution.py
+++ b/solution.py
@@ -72,7 +72,7 @@
         ).astype(jnp.int32)
         return both[:, cap:] * item_dev + both[:, :cap]
 
-    def serve(server, rank, cap, table, index):
+    def serve(server, rank, cap, table, index, valid):
         pick = (index[:, None] == jnp.arange(table.shape[0], dtype=jnp.int32)[None, :]).astype(
             jnp.bfloat16
         )
@@ -80,9 +80,10 @@
         outgoing = outgoing.reshape(shards, cap, hidden)
         incoming = lax.all_to_all(outgoing, "shard", split_axis=0, concat_axis=0, tiled=True)
         column = (server * cap + rank).reshape(item_dev, fanout)
+        weight = jnp.where(valid.reshape(item_dev, fanout), slot_weight, 0)
         spread = jnp.where(
             column[:, :, None] == jnp.arange(shards * cap, dtype=jnp.int32)[None, None, :],
-            slot_weight[:, :, None].astype(jnp.float32),
+            weight[:, :, None].astype(jnp.float32),
             0.0,
         )
         mix = jnp.sum(spread, axis=1).astype(jnp.bfloat16)
@@ -98,37 +99,52 @@
         return rank, totals
 
     chips = shards // 2
-    fast_cap = capacity * 3 // 4
+    main_cap = capacity * 3 // 4
+    spill_cap = capacity - main_cap
     chip = owners // 2
     chip_rank, chip_totals = rank_within(chip, chips)
-    crowded = (jnp.max(chip_totals) > 2 * fast_cap).astype(jnp.int32)
-    fast_server = chip * 2 + chip_rank % 2
-    fast_rank = chip_rank // 2
-    fast_requests = make_requests(
-        fast_server, (owners % 2) * item_dev + local_row, fast_rank, fast_cap
-    )
-    flagged = jnp.concatenate(
-        [fast_requests, jnp.broadcast_to(crowded, (shards, 1))], axis=1
-    )
+    crowded = (jnp.max(chip_totals) > 2 * main_cap).astype(jnp.int32)
+    server = chip * 2 + chip_rank % 2
+    server_rank = chip_rank // 2
+    value = (owners % 2) * item_dev + local_row
+    requests = make_requests(server, value, server_rank, main_cap)
+    flagged = jnp.concatenate([requests, jnp.broadcast_to(crowded, (shards, 1))], axis=1)
     received = lax.all_to_all(flagged, "shard", split_axis=0, concat_axis=0, tiled=True)
-    region_crowded = jnp.max(received[:, fast_cap])
+    region_crowded = jnp.max(received[:, main_cap])
     core = lax.axis_index("shard") % 2
     pairs = [(i, i ^ 1) for i in range(shards)]
     sibling = lax.ppermute(projected, "shard", pairs)
-
-    def by_owner(_):
-        rank, _totals = rank_within(owners, shards)
-        requests = make_requests(owners, local_row, rank, capacity)
-        wanted = lax.all_to_all(requests, "shard", split_axis=0, concat_axis=0, tiled=True)
-        return serve(owners, rank, capacity, projected, wanted.reshape(-1))
-
-    def by_chip(_):
-        wanted = received[:, :fast_cap].reshape(-1)
-        index = ((wanted // item_dev) ^ core) * item_dev + wanted % item_dev
-        table = jnp.concatenate([projected, sibling], axis=0)
-        return serve(fast_server, fast_rank, fast_cap, table, index)
-
-    summed = lax.cond(region_crowded == 0, by_chip, by_owner, 0)
+    table = jnp.concatenate([projected, sibling], axis=0)
+
+    def table_index(wanted):
+        return ((wanted // item_dev) ^ core) * item_dev + wanted % item_dev
+
+    summed = serve(
+        server,
+        server_rank,
+        main_cap,
+        table,
+        table_index(received[:, :main_cap].reshape(-1)),
+        server_rank < main_cap,
+    )
+
+    def spill(_):
+        spill_rank = server_rank - main_cap
+        spill_requests = make_requests(server, value, spill_rank, spill_cap)
+        wanted = lax.all_to_all(spill_requests, "shard", split_axis=0, concat_axis=0, tiled=True)
+        return serve(
+            server,
+            spill_rank,
+            spill_cap,
+            table,
+            table_index(wanted.reshape(-1)),
+            spill_rank >= 0,
+        )
+
+    def no_spill(_):
+        return jnp.zeros_like(summed)
+
+    summed = summed + lax.cond(region_crowded == 0, no_spill, spill, 0)
     aggregate = (summed / weight_sum).astype(jnp.bfloat16)
     activation = (
         jnp.dot(features, self_weight, preferred_element_type=jnp.float32)

time: 246 us -> 246 us (level)
  other arithmetic: 24.5 us -> 28.6 us
  starting transfers between devices: 24 us -> 21 us
  matrix products: 27 us -> 24.5 us
    dot_general x1 -> x0, matrix products: 6.04 us -> none  [serve(): jnp.dot(mix, incoming.reshape(shards * cap, hidden), preferred_element_ty...]
    dot_general x1, matrix products: 2.11 us -> 6.87 us  [body(): jnp.dot(aggregate, nbr_weight, preferred_element_type=jnp.float32)]
    all_to_all x1, starting transfers between devices: 10.5 us -> 7.4 us  [serve(): lax.all_to_all(outgoing, 'shard', split_axis=0, concat_axis=0, tiled=True)]
    all_to_all x1, waiting for transfers between devices: 0.01 us -> 2.89 us  [body(): lax.all_to_all(flagged, 'shard', split_axis=0, concat_axis=0, tiled=True)]
    all_to_all x1, waiting for transfers between devices: 124 us -> 121 us  [serve(): lax.all_to_all(outgoing, 'shard', split_axis=0, concat_axis=0, tiled=True)]
  transfers between devices with their start and end apart: 4 -> 4, of which waited for: 2 -> 3; matrix products, arithmetic and copies ran while one was open for 12% -> 12% of each run, Pallas kernels for 0% -> 0%
where the time goes in v4:
time: 246 us; the launch traced here: 245 us
  waiting for transfers between devices  151 us (61%)
  other arithmetic  28.6 us (12%)
  matrix products  24.5 us (10%)
  starting transfers between devices  21 us (9%)
  between operations  15.6 us (6%)
  local copies, waits for them, and re-layouts  3.97 us (2%)
    all_to_all x1, waiting for transfers between devices, serve(): lax.all_to_all(outgoing, 'shard', split_axis=0, concat_axis=0, tiled=True)  121 us
    all_gather x1, waiting for transfers between devices, body(): lax.all_gather(embedding, 'region', axis=0, tiled=True)  27.2 us
    reduce_sum x1, other arithmetic, serve(): mix = jnp.sum(spread, axis=1).astype(jnp.bfloat16)  16.5 us
    all_to_all x1, starting transfers between devices, body(): lax.all_to_all(flagged, 'shard', split_axis=0, concat_axis=0, tiled=True)  13 us
    all_to_all x1, starting transfers between devices, serve(): lax.all_to_all(outgoing, 'shard', split_axis=0, concat_axis=0, tiled=True)  7.4 us
    dot_general x1, matrix products, body(): jnp.dot(aggregate, nbr_weight, preferred_element_type=jnp.float32)  6.87 us
    dot_general x1, matrix products, serve(): jnp.dot(pick, table, preferred_element_type=jnp.float32)  6.58 us
  transfers between devices with their start and end apart: 4, of which 3 were waited for; matrix products, arithmetic and copies ran while one was open for 12% of the time, Pallas kernels for 0%

profile of v4, /device:TPU:1, one launch (start us, length us, event | category | flops | bytes accessed | tf_op | source)
XLA Modules:
  0.0 245.2 jit_solution(3766500507576355711)
XLA Ops:
  7.2 0.0 copy-start
  7.2 1.0 copy.54
  8.2 0.1 reshape.565
  8.3 0.1 reshape.566
  8.4 0.1 convert_reduce_fusion.1
  8.6 0.1 fusion.92
  8.7 0.2 fusion.46
  9.0 1.6 select_convert_fusion.4
  10.6 0.9 convolution_convert_fusion.1
  11.5 0.1 slice_add_fusion.1
  11.6 0.0 copy-start.3
  11.6 0.1 convert_reduce_fusion
  11.8 0.6 reduce_max.18
  13.0 0.6 concatenate.19
  13.6 13.0 %all-to-all-start.2 = ((s32[64,1,49]{2,1,0:T(1,128)}), s32[64,1,49]{2,1,0:T(1,128)S(1)}, u32[]{:S(2)}, u32[]{:S(2)}) async-start(s32[64,1,49]{2,1,0:T(1,128)} %bitcast.14), calls=%async_computation.2 | async-start | bytes 65536 | tf_op jit(solution)/shard_map/all_to_all | solution.py:112
  26.6 2.3 fusion.39
  28.9 0.5 collective-permute-start
  29.5 0.6 fusion.109
  30.1 1.3 compare_select_fusion.1
  31.5 0.1 copy.59
  31.6 0.8 convert_reduce_fusion.2
  32.4 0.6 fusion.108
  33.0 2.9 %all-to-all-done.2 = s32[64,1,49]{2,1,0:T(1,128)S(1)} async-done(((s32[64,1,49]{2,1,0:T(1,128)}), s32[64,1,49]{2,1,0:T(1,128)S(1)}, u32[]{:S(2)}, u32[]{:S(2)}) %all-to-all-start.2) | async-done | bytes 12576 | tf_op jit(solution)/shard_map/all_to_all | solution.py:112
  35.9 0.1 reshape.567
  35.9 0.7 slice_reduce_fusion
  37.3 0.6 fusion.78
  37.9 2.1 pad_maximum_fusion
  40.0 1.1 conditional.1
  40.0 1.1 broadcast.732
  41.1 6.6 %fusion.32 = bf16[3072,1024]{1,0:T(8,128)(2,1)} fusion(s32[3072]{0:T(1024)} %fusion.78, bf16[256,1024]{1,0:T(8,128)(2,1)} %collective-permute-done, bf16[256,1024]{1,0:T(8,128)(2,1)S(1)} %fusion.39), kind=kOutput, calls=%fused_computation.69 | convolution fusion | flops 3228041216 | bytes 7352320 | tf_op jit(solution)/shard_map/dot_general | solution.py:79
  47.7 7.4 %all-to-all-start.3 = ((bf16[64,48,1024]{2,1,0:T(8,128)(2,1)}), bf16[64,48,1024]{2,1,0:T(8,128)(2,1)}, u32[]{:S(2)}, u32[]{:S(2)}) async-start(bf16[64,48,1024]{2,1,0:T(8,128)(2,1)} %bitcast.65), calls=%async_computation.3 | async-start | bytes 12582912 | tf_op jit(solution)/shard_map/all_to_all | solution.py:81
  55.1 0.0 all-gather.2.cloned.1.call-start
  55.2 0.1 convert_element_type.113
  55.3 0.3 fusion.63
  55.6 2.5 %fusion.111 = f32[256,1024]{1,0:T(8,128)S(1)} fusion(bf16[256,1024]{1,0:T(8,128)(2,1)} %param.16, bf16[1024,1024]{1,0:T(8,128)(2,1)} %param.19), kind=kOutput, calls=%fused_computation.238 | convolution fusion | flops 536870912 | bytes 3670016 | tf_op jit(solution)/shard_map/dot_general | solution.py:150
  58.1 16.5 %select_reduce_fusion.1 = bf16[256,3072]{1,0:T(8,128)(2,1)} fusion(f32[256,8]{1,0:T(8,128)S(1)} %get-tuple-element.151, s32[256,8]{1,0:T(8,128)S(1)} %get-tuple-element.150), kind=kLoop, calls=%fused_computation.65 | loop fusion | flops 18087936 | bytes 1589248 | tf_op jit(solution)/shard_map/reduce_sum | solution.py:89
  74.6 121.4 %all-to-all-done.3 = bf16[64,48,1024]{2,1,0:T(8,128)(2,1)} async-done(((bf16[64,48,1024]{2,1,0:T(8,128)(2,1)}), bf16[64,48,1024]{2,1,0:T(8,128)(2,1)}, u32[]{:S(2)}, u32[]{:S(2)}) %all-to-all-start.3) | async-done | bytes 6291488 | tf_op jit(solution)/shard_map/all_to_all | solution.py:81
  196.0 6.9 %multiply_reduce_fusion = (f32[256]{0:T(256)S(1)}, f32[256,1024]{1,0:T(8,128)}) fusion(f32[1024]{0:T(1024)S(1)} %copy-done.9, f32[256,1024]{1,0:T(8,128)S(1)} %fusion.111, bf16[1024,1024]{1,0:T(8,128)(2,1)S(1)} %copy-done, f32[256,1024]{1,0:T(8,128)} %get-tuple-element.171, bf16[3072,1024]{1,0:T(8,128)(2,1)} %bitcast.17, ...), kind=kOutput, calls=%fused_computation.93 | convolution fusion | flops 2149580544 | bytes 13113344 | tf_op jit(solution)/shard_map/dot_general | solution.py:151
  202.9 2.2 multiply_convert_fusion
  205.0 0.0 all-gather.2.cloned.1.call-update
  205.1 0.1 iota_compare_fusion.27
  205.1 1.3 fusion.73
  206.4 1.4 fusion.47
  207.8 27.2 %all-gather.2.cloned.1.call-done = bf16[1024,1024]{1,0:T(8,128)(2,1)} async-done(((bf16[256,1024]{1,0:T(8,128)(2,1)}), bf16[1024,1024]{1,0:T(8,128)(2,1)}) %all-gather.2.cloned.1.call-update) | async-done | bytes 2097168 | tf_op jit(solution)/shard_map/all_gather | solution.py:171
  235.0 2.4 fusion.43
  237.5 0.1 reduce_sum.97
  237.6 0.1 copy.62
  237.7 0.7 select_reduce_fusion.2
  (38 shorter events, 0.2 us)
Async XLA Ops:
  7.2 188.8 %copy-start = (bf16[1024,1024]{1,0:T(8,128)(2,1)S(1)}, bf16[1024,1024]{1,0:T(8,128)(2,1)}, u32[]{:S(2)}) copy-start(bf16[1024,1024]{1,0:T(8,128)(2,1)} %param.20) | copy-start | bytes 6291460
  7.2 19.4 %copy-start.1 = (bf16[256,1024]{1,0:T(8,128)(2,1)S(1)}, bf16[256,1024]{1,0:T(8,128)(2,1)}, u32[]{:S(2)}) copy-start(bf16[256,1024]{1,0:T(8,128)(2,1)} %param.16) | copy-start | bytes 1572868
  7.2 19.4 %copy-start.8 = (f32[1024]{0:T(1024)S(1)}, f32[1024]{0:T(1024)}, u32[]{:S(2)}) copy-start(f32[1024]{0:T(1024)} %param.18) | copy-start | bytes 12292
  11.6 17.9 %copy-start.4 = (s32[2]{0:T(128)S(1)}, s32[2]{0:T(128)}, u32[]{:S(2)}) copy-start(s32[2]{0:T(128)} %param.24) | copy-start | bytes 28
  11.6 19.9 %copy-start.3 = (s32[256,8]{0,1:T(8,128)S(1)}, s32[256,8]{0,1:T(8,128)}, u32[]{:S(2)}) copy-start(s32[256,8]{0,1:T(8,128)} %param.23) | copy-start | bytes 24580
  13.6 22.2 %all-to-all-start.2 = ((s32[64,1,49]{2,1,0:T(1,128)}), s32[64,1,49]{2,1,0:T(1,128)S(1)}, u32[]{:S(2)}, u32[]{:S(2)}) async-start(s32[64,1,49]{2,1,0:T(1,128)} %bitcast.14), calls=%async_computation.2 | async-start | bytes 65536 | tf_op jit(solution)/shard_map/all_to_all | solution.py:112
  28.9 9.0 %collective-permute-start = (bf16[256,1024]{1,0:T(8,128)(2,1)S(1)}, bf16[256,1024]{1,0:T(8,128)(2,1)}, u32[]{:S(2)}, u32[]{:S(2)}) collective-permute-start(bf16[256,1024]{1,0:T(8,128)(2,1)S(1)} %fusion.39), channel_id=1, source_target_pairs={{0,1},{1,0},{2,3},{3,2},{4,5},{5,4},{6,7},{7,6},{8,9},{9,8},{10,11... | collective-permute-start | bytes 1572872 | tf_op jit(solution)/shard_map/ppermute | solution.py:116
  47.7 7.5 %copy-start.2 = (s32[16,128]{1,0:T(8,128)S(1)}, s32[16,128]{1,0:T(8,128)}, u32[]{:S(2)}) copy-start(s32[16,128]{1,0:T(8,128)} %get-tuple-element.152) | copy-start | bytes 24580
  47.7 148.2 %all-to-all-start.3 = ((bf16[64,48,1024]{2,1,0:T(8,128)(2,1)}), bf16[64,48,1024]{2,1,0:T(8,128)(2,1)}, u32[]{:S(2)}, u32[]{:S(2)}) async-start(bf16[64,48,1024]{2,1,0:T(8,128)(2,1)} %bitcast.65), calls=%async_computation.3 | async-start | bytes 12582912 | tf_op jit(solution)/shard_map/all_to_all | solution.py:81
  55.1 179.9 %all-gather.2.cloned.1.call-start = ((), (), s32[]{:S(2)}) async-start(), calls=%async_computation.4 | async-start | bytes 2621440 | tf_op jit(solution)/shard_map/all_gather | solution.py:171
  55.6 140.4 %copy-start.5 = (f32[256]{0:T(256)S(1)}, f32[256]{0:T(256)}, u32[]{:S(2)}) copy-start(f32[256]{0:T(256)} %get-tuple-element.139) | copy-start | bytes 3076
  55.6 140.4 %copy-start.9 = (f32[1024]{0:T(1024)S(1)}, f32[1024]{0:T(1024)}, u32[]{:S(2)}) copy-start(f32[1024]{0:T(1024)} %param.21) | copy-start | bytes 12292
  202.8 2.2 copy-start.10
  202.8 2.3 copy-start.7
  202.8 3.6 %copy-start.6 = (s32[64]{0:T(128)S(1)}, s32[64]{0:T(128)}, u32[]{:S(2)}) copy-start(s32[64]{0:T(128)} %param.26) | copy-start | bytes 772
Sparse Core Ops, SparseCore 0:
  205.2 29.8 all-gather.1

commit v5 on v4

--- a/solution.py
+++ b/solution.py
@@ -98,26 +98,34 @@
         totals = jnp.sum(hot.astype(jnp.float32), axis=0)
         return rank, totals
 
-    chips = shards // 2
-    main_cap = capacity * 3 // 4
+    partner = shards // 4
+    members = 4
+    groups = shards // members
+    main_cap = capacity * 5 // 8
     spill_cap = capacity - main_cap
-    chip = owners // 2
-    chip_rank, chip_totals = rank_within(chip, chips)
-    crowded = (jnp.max(chip_totals) > 2 * main_cap).astype(jnp.int32)
-    server = chip * 2 + chip_rank % 2
-    server_rank = chip_rank // 2
-    value = (owners % 2) * item_dev + local_row
+    low = owners % 2
+    high = (owners // partner) % 2
+    group = (owners // (2 * partner)) * (partner // 2) + (owners % partner) // 2
+    group_rank, group_totals = rank_within(group, groups)
+    crowded = (jnp.max(group_totals) > members * main_cap).astype(jnp.int32)
+    turn = group_rank % members
+    group_base = (owners // (2 * partner)) * (2 * partner) + (owners % partner) // 2 * 2
+    server = group_base + (turn // 2) * partner + turn % 2
+    server_rank = group_rank // members
+    value = (high * 2 + low) * item_dev + local_row
     requests = make_requests(server, value, server_rank, main_cap)
     flagged = jnp.concatenate([requests, jnp.broadcast_to(crowded, (shards, 1))], axis=1)
     received = lax.all_to_all(flagged, "shard", split_axis=0, concat_axis=0, tiled=True)
     region_crowded = jnp.max(received[:, main_cap])
-    core = lax.axis_index("shard") % 2
-    pairs = [(i, i ^ 1) for i in range(shards)]
-    sibling = lax.ppermute(projected, "shard", pairs)
-    table = jnp.concatenate([projected, sibling], axis=0)
+    me = lax.axis_index("shard")
+    my_code = ((me // partner) % 2) * 2 + me % 2
+    sibling = lax.ppermute(projected, "shard", [(i, i ^ 1) for i in range(shards)])
+    across = lax.ppermute(projected, "shard", [(i, i ^ partner) for i in range(shards)])
+    across_sibling = lax.ppermute(across, "shard", [(i, i ^ 1) for i in range(shards)])
+    table = jnp.concatenate([projected, sibling, across, across_sibling], axis=0)
 
     def table_index(wanted):
-        return ((wanted // item_dev) ^ core) * item_dev + wanted % item_dev
+        return ((wanted // item_dev) ^ my_code) * item_dev + wanted % item_dev
 
     summed = serve(
         server,

time: 246 us -> 228 us (0.927)
  waiting for transfers between devices: 151 us -> 136 us
  other arithmetic: 28.6 us -> 22.8 us
  matrix products: 24.5 us -> 27.2 us
    all_to_all x1, waiting for transfers between devices: 121 us -> 104 us  [serve(): lax.all_to_all(outgoing, 'shard', split_axis=0, concat_axis=0, tiled=True)]
    reduce_sum x1, other arithmetic: 16.5 us -> 9.1 us  [serve(): mix = jnp.sum(spread, axis=1).astype(jnp.bfloat16)]
    ppermute x1 -> x3, starting transfers between devices: 0.54 us -> 3.93 us  [the longest x1 2.12 us: body(): lax.ppermute(projected, 'shard', [(i, i ^ partner) for i in range(shards)])]
  transfers between devices with their start and end apart: 4 -> 6, of which waited for: 3 -> 3; matrix products, arithmetic and copies ran while one was open for 12% -> 12% of each run, Pallas kernels for 0% -> 0%
where the time goes in v5:
time: 228 us; the launch traced here: 227 us
  waiting for transfers between devices  136 us (60%)
  matrix products  27.2 us (12%)
  other arithmetic  22.8 us (10%)
  starting transfers between devices  21.1 us (9%)
  between operations  15.7 us (7%)
  local copies, waits for them, and re-layouts  3.99 us (2%)
    all_to_all x1, waiting for transfers between devices, serve(): lax.all_to_all(outgoing, 'shard', split_axis=0, concat_axis=0, tiled=True)  104 us
    all_gather x1, waiting for transfers between devices, body(): lax.all_gather(embedding, 'region', axis=0, tiled=True)  27.3 us
    all_to_all x1, starting transfers between devices, body(): lax.all_to_all(flagged, 'shard', split_axis=0, concat_axis=0, tiled=True)  11 us
    reduce_sum x1, other arithmetic, serve(): mix = jnp.sum(spread, axis=1).astype(jnp.bfloat16)  9.1 us
    dot_general x1, matrix products, serve(): jnp.dot(pick, table, preferred_element_type=jnp.float32)  8.95 us
    dot_general x1, matrix products, body(): jnp.dot(aggregate, nbr_weight, preferred_element_type=jnp.float32)  6.15 us
    all_to_all x1, starting transfers between devices, serve(): lax.all_to_all(outgoing, 'shard', split_axis=0, concat_axis=0, tiled=True)  5.84 us
    all_to_all x1, waiting for transfers between devices, body(): lax.all_to_all(flagged, 'shard', split_axis=0, concat_axis=0, tiled=True)  5.02 us
  transfers between devices with their start and end apart: 6, of which 3 were waited for; matrix products, arithmetic and copies ran while one was open for 12% of the time, Pallas kernels for 0%

profile of v5, /device:TPU:1, one launch (start us, length us, event | category | flops | bytes accessed | tf_op | source)
XLA Modules:
  0.0 227.1 jit_solution(11385205463572364565)
XLA Ops:
  7.2 2.5 %fusion.49 = bf16[256,1024]{1,0:T(8,128)(2,1)S(1)} fusion(bf16[256,1024]{1,0:T(8,128)(2,1)} %param.16, bf16[1024,1024]{1,0:T(8,128)(2,1)} %param.17, f32[1024]{0:T(1024)} %param.18), kind=kOutput, calls=%fused_computation.95 | convolution fusion | flops 537657344 | bytes 3149824 | tf_op jit(solution)/shard_map/dot_general | solution.py:50
  9.7 2.1 collective-permute-start.1
  11.9 1.3 collective-permute-start
  13.1 0.1 copy.54
  13.3 0.1 reshape.702
  13.4 0.1 reshape.703
  13.5 0.1 convert_reduce_fusion.1
  13.6 0.1 fusion.118
  13.8 0.2 fusion.57
  14.1 1.6 select_convert_fusion.4
  15.7 0.9 convolution_convert_fusion.1
  16.6 0.1 slice_add_fusion.1
  16.7 0.1 convert_reduce_fusion
  16.8 0.6 reduce_max.18
  18.1 0.6 concatenate.19
  18.7 11.0 %all-to-all-start.2 = ((s32[64,1,41]{2,1,0:T(1,128)}), s32[64,1,41]{2,1,0:T(1,128)S(1)}, u32[]{:S(2)}, u32[]{:S(2)}) async-start(s32[64,1,41]{2,1,0:T(1,128)} %bitcast.14), calls=%async_computation.2 | async-start | bytes 65536 | tf_op jit(solution)/shard_map/all_to_all | solution.py:118
  29.7 0.6 fusion.147
  30.3 0.6 fusion.148
  30.9 1.3 compare_select_fusion.1
  32.2 1.2 convert_reduce_fusion.2
  33.4 0.5 collective-permute-start.2
  34.0 5.0 %all-to-all-done.2 = s32[64,1,41]{2,1,0:T(1,128)S(1)} async-done(((s32[64,1,41]{2,1,0:T(1,128)}), s32[64,1,41]{2,1,0:T(1,128)S(1)}, u32[]{:S(2)}, u32[]{:S(2)}) %all-to-all-start.2) | async-done | bytes 10528 | tf_op jit(solution)/shard_map/all_to_all | solution.py:118
  39.0 0.8 slice_reduce_fusion
  40.5 0.1 reshape.704
  40.6 0.6 fusion.77
  41.2 2.7 %pad_maximum_fusion = bf16[1024,1024]{1,0:T(8,128)(2,1)} fusion(bf16[256,1024]{1,0:T(8,128)(2,1)} %collective-permute-done.2, bf16[256,1024]{1,0:T(8,128)(2,1)S(1)} %collective-permute-done.1, bf16[256,1024]{1,0:T(8,128)(2,1)} %collective-permute-done, bf16[256,1024]{1,0:T(8,128)(2,1)S(1)} %fusion.49), kind=kLoop, calls=%fused_computation.87 | loop fusion | flops 8388608 | bytes 4194304 | tf_op jit(solution)/shard_map/concatenate | solution.py:125
  43.9 1.3 conditional.1
  44.2 1.1 broadcast.1045
  45.3 8.9 %fusion.42 = bf16[2560,1024]{1,0:T(8,128)(2,1)} fusion(s32[2560]{0:T(1024)} %fusion.77, bf16[256,1024]{1,0:T(8,128)(2,1)} %collective-permute-done.2, bf16[256,1024]{1,0:T(8,128)(2,1)} %copy-done.3, bf16[256,1024]{1,0:T(8,128)(2,1)} %collective-permute-done, bf16[256,1024]{1,0:T(8,128)(2,1)S(1)} %fusion.49), kind=kOutput, calls=%fused_computation.85 | convolution fusion | flops 5382340608 | bytes 7350272 | tf_op jit(solution)/shard_map/dot_general | solution.py:79
  54.2 5.8 %all-to-all-start.3 = ((bf16[64,40,1024]{2,1,0:T(8,128)(2,1)}), bf16[64,40,1024]{2,1,0:T(8,128)(2,1)}, u32[]{:S(2)}, u32[]{:S(2)}) async-start(bf16[64,40,1024]{2,1,0:T(8,128)(2,1)} %bitcast.63), calls=%async_computation.3 | async-start | bytes 10485760 | tf_op jit(solution)/shard_map/all_to_all | solution.py:81
  60.1 0.3 all-gather.2.cloned.1.call-start
  60.4 0.1 convert_element_type.113
  60.6 0.8 fusion.89
  61.4 0.1 copy.60
  61.5 0.8 copy.59
  62.3 3.3 %fusion.150 = f32[256,1024]{1,0:T(8,128)} fusion(bf16[256,1024]{1,0:T(8,128)(2,1)S(1)} %copy-done.1, bf16[1024,1024]{1,0:T(8,128)(2,1)} %param.19), kind=kOutput, calls=%fused_computation.323 | convolution fusion | flops 536870912 | bytes 3670016 | tf_op jit(solution)/shard_map/dot_general | solution.py:158
  65.6 9.1 %select_reduce_fusion.1 = bf16[256,2560]{1,0:T(8,128)(2,1)S(1)} fusion(f32[256,8]{1,0:T(8,128)S(1)} %copy.60, s32[256,8]{1,0:T(8,128)S(1)} %copy-done.2), kind=kLoop, calls=%fused_computation.81 | loop fusion | flops 15073280 | bytes 1327104 | tf_op jit(solution)/shard_map/reduce_sum | solution.py:89
  74.7 103.8 %all-to-all-done.3 = bf16[64,40,1024]{2,1,0:T(8,128)(2,1)} async-done(((bf16[64,40,1024]{2,1,0:T(8,128)(2,1)}), bf16[64,40,1024]{2,1,0:T(8,128)(2,1)}, u32[]{:S(2)}, u32[]{:S(2)}) %all-to-all-start.3) | async-done | bytes 5242912 | tf_op jit(solution)/shard_map/all_to_all | solution.py:81
  178.5 6.1 %multiply_reduce_fusion = (f32[256]{0:T(256)S(1)}, f32[256,1024]{1,0:T(8,128)}) fusion(f32[1024]{0:T(1024)S(1)} %copy-done.13, f32[256,1024]{1,0:T(8,128)} %fusion.150, bf16[1024,1024]{1,0:T(8,128)(2,1)S(1)} %copy-done, f32[256,1024]{1,0:T(8,128)} %get-tuple-element.290, bf16[2560,1024]{1,0:T(8,128)(2,1)} %bitcast.17, ...), kind=kOutput, calls=%fused_computation.109 | convolution fusion | flops 1881145088 | bytes 11802624 | tf_op jit(solution)/shard_map/dot_general | solution.py:159
  184.7 2.1 multiply_convert_fusion
  186.9 0.1 iota_compare_fusion.27
  186.9 1.3 fusion.72
  188.2 1.4 fusion.54
  189.7 27.3 %all-gather.2.cloned.1.call-done = bf16[1024,1024]{1,0:T(8,128)(2,1)} async-done(((bf16[256,1024]{1,0:T(8,128)(2,1)}), bf16[1024,1024]{1,0:T(8,128)(2,1)}) %all-gather.2.cloned.1.call-update) | async-done | bytes 2097168 | tf_op jit(solution)/shard_map/all_gather | solution.py:179
  216.9 2.4 %fusion.53 = f32[8,8,8,128]{3,1,2,0:T(8,128)S(1)} fusion(bf16[1024,1024]{1,0:T(8,128)(2,1)} %all-gather.2.cloned.1.call-done, f32[64]{0:T(128)S(1)} %broadcast_multiply_fusion.1, f32[64,1024]{1,0:T(8,128)S(1)} %fusion.72), kind=kOutput, calls=%fused_computation.101 | convolution fusion | flops 134545408 | bytes 2621696 | tf_op jit(solution)/shard_map/dot_general | solution.py:177
  219.3 0.1 reduce_sum.97
  219.5 0.1 copy.64
  219.5 0.7 select_reduce_fusion.2
  (53 shorter events, 0.4 us)
Async XLA Ops:
  7.2 171.3 %copy-start = (bf16[1024,1024]{1,0:T(8,128)(2,1)S(1)}, bf16[1024,1024]{1,0:T(8,128)(2,1)}, u32[]{:S(2)}) copy-start(bf16[1024,1024]{1,0:T(8,128)(2,1)} %param.20) | copy-start | bytes 6291460
  7.2 6.0 %copy-start.4 = (s32[256,8]{0,1:T(8,128)S(1)}, s32[256,8]{0,1:T(8,128)}, u32[]{:S(2)}) copy-start(s32[256,8]{0,1:T(8,128)} %param.22) | copy-start | bytes 24580
  7.2 23.1 %copy-start.9 = (s32[2]{0:T(128)S(1)}, s32[2]{0:T(128)}, u32[]{:S(2)}) copy-start(s32[2]{0:T(128)} %param.24) | copy-start | bytes 28
  7.2 25.0 %copy-start.8 = (s32[256,8]{0,1:T(8,128)S(1)}, s32[256,8]{0,1:T(8,128)}, u32[]{:S(2)}) copy-start(s32[256,8]{0,1:T(8,128)} %param.23) | copy-start | bytes 24580
  9.7 23.7 %collective-permute-start.1 = (bf16[256,1024]{1,0:T(8,128)(2,1)S(1)}, bf16[256,1024]{1,0:T(8,128)(2,1)S(1)}, u32[]{:S(2)}, u32[]{:S(2)}) collective-permute-start(bf16[256,1024]{1,0:T(8,128)(2,1)S(1)} %fusion.49), channel_id=1, source_target_pairs={{0,16},{1,17},{2,18},{3,19},{4,20},{5,21},{6,22},{7,23},{8,24},{9,... | collective-permute-start | bytes 1572872 | tf_op jit(solution)/shard_map/ppermute | solution.py:123
  11.9 29.3 %collective-permute-start = (bf16[256,1024]{1,0:T(8,128)(2,1)S(1)}, bf16[256,1024]{1,0:T(8,128)(2,1)}, u32[]{:S(2)}, u32[]{:S(2)}) collective-permute-start(bf16[256,1024]{1,0:T(8,128)(2,1)S(1)} %fusion.49), channel_id=1, source_target_pairs={{0,1},{1,0},{2,3},{3,2},{4,5},{5,4},{6,7},{7,6},{8,9},{9,8},{10,11... | collective-permute-start | bytes 1572872 | tf_op jit(solution)/shard_map/ppermute | solution.py:122
  18.7 20.3 %all-to-all-start.2 = ((s32[64,1,41]{2,1,0:T(1,128)}), s32[64,1,41]{2,1,0:T(1,128)S(1)}, u32[]{:S(2)}, u32[]{:S(2)}) async-start(s32[64,1,41]{2,1,0:T(1,128)} %bitcast.14), calls=%async_computation.2 | async-start | bytes 65536 | tf_op jit(solution)/shard_map/all_to_all | solution.py:118
  33.4 10.5 %copy-start.3 = (bf16[256,1024]{1,0:T(8,128)(2,1)}, bf16[256,1024]{1,0:T(8,128)(2,1)S(1)}, u32[]{:S(2)}) copy-start(bf16[256,1024]{1,0:T(8,128)(2,1)S(1)} %collective-permute-done.1) | copy-start | bytes 1572868
  33.4 7.8 %collective-permute-start.2 = (bf16[256,1024]{1,0:T(8,128)(2,1)S(1)}, bf16[256,1024]{1,0:T(8,128)(2,1)}, u32[]{:S(2)}, u32[]{:S(2)}) collective-permute-start(bf16[256,1024]{1,0:T(8,128)(2,1)S(1)} %collective-permute-done.1), channel_id=1, source_target_pairs={{0,1},{1,0},{2,3},{3,2},{4,5},{5,4},{6,7},{7,6},{8,9},{9,8},{10,11... | collective-permute-start | bytes 1572872 | tf_op jit(solution)/shard_map/ppermute | solution.py:124
  54.2 6.2 %copy-start.6 = (s32[16,128]{1,0:T(8,128)S(1)}, s32[16,128]{1,0:T(8,128)}, u32[]{:S(2)}) copy-start(s32[16,128]{1,0:T(8,128)} %get-tuple-element.257) | copy-start | bytes 24580
  54.2 6.4 %copy-start.5 = (s32[256,8]{0,1:T(8,128)S(1)}, s32[256,8]{0,1:T(8,128)}, u32[]{:S(2)}) copy-start(s32[256,8]{0,1:T(8,128)} %param.22) | copy-start | bytes 24580
  54.2 8.0 %copy-start.1 = (bf16[256,1024]{1,0:T(8,128)(2,1)S(1)}, bf16[256,1024]{1,0:T(8,128)(2,1)}, u32[]{:S(2)}) copy-start(bf16[256,1024]{1,0:T(8,128)(2,1)} %param.16) | copy-start | bytes 1572868
  54.2 124.2 %all-to-all-start.3 = ((bf16[64,40,1024]{2,1,0:T(8,128)(2,1)}), bf16[64,40,1024]{2,1,0:T(8,128)(2,1)}, u32[]{:S(2)}, u32[]{:S(2)}) async-start(bf16[64,40,1024]{2,1,0:T(8,128)(2,1)} %bitcast.63), calls=%async_computation.3 | async-start | bytes 10485760 | tf_op jit(solution)/shard_map/all_to_all | solution.py:81
  60.1 118.4 %copy-start.10 = (f32[256]{0:T(256)S(1)}, f32[256]{0:T(256)}, u32[]{:S(2)}) copy-start(f32[256]{0:T(256)} %get-tuple-element.241) | copy-start | bytes 3076
  60.1 118.4 %copy-start.13 = (f32[1024]{0:T(1024)S(1)}, f32[1024]{0:T(1024)}, u32[]{:S(2)}) copy-start(f32[1024]{0:T(1024)} %param.21) | copy-start | bytes 12292
  60.1 156.8 %all-gather.2.cloned.1.call-start = ((), (), s32[]{:S(2)}) async-start(), calls=%async_computation.4 | async-start | bytes 2621440 | tf_op jit(solution)/shard_map/all_gather | solution.py:179
  62.3 3.3 %copy-start.2 = (s32[256,8]{1,0:T(8,128)S(1)}, s32[256,8]{1,0:T(8,128)}, u32[]{:S(2)}) copy-start(s32[256,8]{1,0:T(8,128)} %copy.59) | copy-start | bytes 24580
  178.5 8.4 %copy-start.14 = (s32[1,4]{1,0:T(1,128)S(1)}, s32[1,4]{1,0:T(1,128)}, u32[]{:S(2)}) copy-start(s32[1,4]{1,0:T(1,128)} %param.27) | copy-start | bytes 52
  178.5 8.4 %copy-start.12 = (s32[64]{0:T(128)S(1)}, s32[64]{0:T(128)}, u32[]{:S(2)}) copy-start(s32[64]{0:T(128)} %param.25) | copy-start | bytes 772
  178.5 9.7 %copy-start.11 = (s32[64]{0:T(128)S(1)}, s32[64]{0:T(128)}, u32[]{:S(2)}) copy-start(s32[64]{0:T(128)} %param.26) | copy-start | bytes 772
Sparse Core Ops, SparseCore 0:
  187.0 29.8 all-gather.1

commit v6 on v5

--- a/solution.py
+++ b/solution.py
@@ -113,16 +113,18 @@
     server = group_base + (turn // 2) * partner + turn % 2
     server_rank = group_rank // members
     value = (high * 2 + low) * item_dev + local_row
-    requests = make_requests(server, value, server_rank, main_cap)
+    requests = make_requests(server, value, server_rank, capacity)
     flagged = jnp.concatenate([requests, jnp.broadcast_to(crowded, (shards, 1))], axis=1)
     received = lax.all_to_all(flagged, "shard", split_axis=0, concat_axis=0, tiled=True)
-    region_crowded = jnp.max(received[:, main_cap])
+    region_crowded = jnp.max(received[:, capacity])
     me = lax.axis_index("shard")
     my_code = ((me // partner) % 2) * 2 + me % 2
-    sibling = lax.ppermute(projected, "shard", [(i, i ^ 1) for i in range(shards)])
     across = lax.ppermute(projected, "shard", [(i, i ^ partner) for i in range(shards)])
-    across_sibling = lax.ppermute(across, "shard", [(i, i ^ 1) for i in range(shards)])
-    table = jnp.concatenate([projected, sibling, across, across_sibling], axis=0)
+    pair = jnp.concatenate([projected, across], axis=0)
+    sibling = lax.ppermute(pair, "shard", [(i, i ^ 1) for i in range(shards)])
+    table = jnp.concatenate(
+        [projected, sibling[:item_dev], across, sibling[item_dev:]], axis=0
+    )
 
     def table_index(wanted):
         return ((wanted // item_dev) ^ my_code) * item_dev + wanted % item_dev
@@ -138,15 +140,9 @@
 
     def spill(_):
         spill_rank = server_rank - main_cap
-        spill_requests = make_requests(server, value, spill_rank, spill_cap)
-        wanted = lax.all_to_all(spill_requests, "shard", split_axis=0, concat_axis=0, tiled=True)
+        wanted = received[:, main_cap:capacity].reshape(-1)
         return serve(
-            server,
-            spill_rank,
-            spill_cap,
-            table,
-            table_index(wanted.reshape(-1)),
-            spill_rank >= 0,
+            server, spill_rank, spill_cap, table, table_index(wanted), spill_rank >= 0
         )
 
     def no_spill(_):
@@ -169,19 +165,31 @@
     positive_pick = (positive_ids[:, None] == items).astype(jnp.bfloat16)
     query_emb = jnp.dot(query_pick, embedding, preferred_element_type=jnp.float32)
     positive_emb = jnp.dot(positive_pick, embedding, preferred_element_type=jnp.float32)
-    positive_score = score_scale / hidden * jnp.sum(query_emb * positive_emb, axis=-1)
-    neg_lists = neg_blocks[0]
+    queries = query_emb.shape[0]
+    pairs_rows = jnp.concatenate([query_emb, positive_emb], axis=0).astype(jnp.bfloat16)
+    everyone = lax.all_gather(pairs_rows, "region", axis=0, tiled=False)
+    their_queries = everyone[:, :queries]
+    their_positives = everyone[:, queries:]
+    positive_score = (
+        score_scale
+        / hidden
+        * jnp.sum(
+            their_queries.astype(jnp.float32) * their_positives.astype(jnp.float32), axis=-1
+        )
+    )
     scores = (
         score_scale
         / hidden
-        * jnp.dot(
-            query_emb.astype(jnp.bfloat16),
-            lax.all_gather(embedding, "region", axis=0, tiled=True).T,
-            preferred_element_type=jnp.float32,
-        )
-    )
-    hinge_all = jnp.maximum(scores - positive_score[:, None] + margin_value, 0.0)
-    block_mean = jnp.mean(hinge_all.reshape(query_emb.shape[0], -1, block_rows), axis=-1)
+        * jnp.einsum(
+            "rqh,ih->rqi", their_queries, embedding, preferred_element_type=jnp.float32
+        )
+    )
+    hinge_all = jnp.maximum(scores - positive_score[:, :, None] + margin_value, 0.0)
+    regions = everyone.shape[0]
+    local_mean = jnp.mean(hinge_all.reshape(regions, queries, -1, block_rows), axis=-1)
+    returned = lax.all_to_all(local_mean, "region", split_axis=0, concat_axis=0, tiled=True)
+    block_mean = returned.transpose(1, 0, 2).reshape(queries, -1)
+    neg_lists = neg_blocks[0]
     pool_ids = jnp.arange(block_mean.shape[1], dtype=jnp.int32)
     picked = jnp.where(
         neg_lists[None, :, None] == pool_ids[None, None, :], block_mean[:, None, :], 0.0

time: 228 us -> 243 us (1.066)
  starting transfers between devices: 21.1 us -> 29.6 us
  local copies, waits for them, and re-layouts: 3.99 us -> 8.29 us
  waiting for transfers between devices: 136 us -> 140 us
  matrix products: 27.2 us -> 23.6 us
    ppermute x1, waiting for transfers between devices: 0.01 us -> 10.1 us  [body(): lax.ppermute(projected, 'shard', [(i, i ^ partner) for i in range(shards)])]
    all_gather x1, waiting for transfers between devices: 27.3 us -> 21.4 us  [body(): everyone = lax.all_gather(pairs_rows, 'region', axis=0, tiled=False)]
    all_to_all x1, waiting for transfers between devices: 5.02 us -> 0.01 us  [body(): lax.all_to_all(flagged, 'shard', split_axis=0, concat_axis=0, tiled=True)]
    all_to_all x1, starting transfers between devices: 5.84 us -> 10.3 us  [serve(): lax.all_to_all(outgoing, 'shard', split_axis=0, concat_axis=0, tiled=True)]
    all_to_all x0 -> x1, waiting for transfers between devices: none -> 3.98 us  [body(): lax.all_to_all(local_mean, 'region', split_axis=0, concat_axis=0, tiled=T...]
    all_to_all x0 -> x1, starting transfers between devices: none -> 3.6 us  [body(): lax.all_to_all(local_mean, 'region', split_axis=0, concat_axis=0, tiled=T...]
  transfers between devices with their start and end apart: 6 -> 6, of which waited for: 3 -> 4; matrix products, arithmetic and copies ran while one was open for 12% -> 9% of each run, Pallas kernels for 0% -> 0%
where the time goes in v6:
time: 243 us; the launch traced here: 240 us
  waiting for transfers between devices  140 us (58%)
  starting transfers between devices  29.6 us (12%)
  matrix products  23.6 us (10%)
  other arithmetic  22.8 us (9%)
  between operations  15.7 us (6%)
  local copies, waits for them, and re-layouts  8.29 us (3%)
    all_to_all x1, waiting for transfers between devices, serve(): lax.all_to_all(outgoing, 'shard', split_axis=0, concat_axis=0, tiled=True)  105 us
    all_gather x1, waiting for transfers between devices, body(): everyone = lax.all_gather(pairs_rows, 'region', axis=0, tiled=False)  21.4 us
    all_to_all x1, starting transfers between devices, body(): lax.all_to_all(flagged, 'shard', split_axis=0, concat_axis=0, tiled=True)  13 us
    all_to_all x1, starting transfers between devices, serve(): lax.all_to_all(outgoing, 'shard', split_axis=0, concat_axis=0, tiled=True)  10.3 us
    ppermute x1, waiting for transfers between devices, body(): lax.ppermute(projected, 'shard', [(i, i ^ partner) for i in range(shards)])  10.1 us
    reduce_sum x1, other arithmetic, serve(): mix = jnp.sum(spread, axis=1).astype(jnp.bfloat16)  9.1 us
    dot_general x1, matrix products, serve(): jnp.dot(pick, table, preferred_element_type=jnp.float32)  8.78 us
    dot_general x1, matrix products, body(): jnp.dot(aggregate, nbr_weight, preferred_element_type=jnp.float32)  6.16 us
  transfers between devices with their start and end apart: 6, of which 4 were waited for; matrix products, arithmetic and copies ran while one was open for 9% of the time, Pallas kernels for 0%

profile of v6, /device:TPU:1, one launch (start us, length us, event | category | flops | bytes accessed | tf_op | source)
XLA Modules:
  0.0 240.3 jit_solution(10538450442484232969)
XLA Ops:
  7.2 1.0 copy.54
  8.2 0.1 reshape.722
  8.5 0.1 fusion.106
  8.7 0.2 fusion.45
  9.0 1.6 select_convert_fusion.2
  10.6 0.9 convolution_convert_fusion.2
  11.6 0.1 convert_reduce_fusion
  11.7 0.6 reduce_max.18
  13.0 0.6 concatenate.33
  13.6 13.0 %all-to-all-start.1 = ((s32[64,1,65]{2,1,0:T(1,128)}), s32[64,1,65]{2,1,0:T(1,128)S(1)}, u32[]{:S(2)}, u32[]{:S(2)}) async-start(s32[64,1,65]{2,1,0:T(1,128)} %bitcast.13), calls=%async_computation.1 | async-start | bytes 65536 | tf_op jit(solution)/shard_map/all_to_all | solution.py:118
  26.6 2.3 fusion.37
  28.9 1.4 collective-permute-start
  30.4 0.6 fusion.136
  31.0 1.3 compare_select_fusion.1
  32.3 10.1 %collective-permute-done = bf16[256,1024]{1,0:T(8,128)(2,1)S(1)} collective-permute-done((bf16[256,1024]{1,0:T(8,128)(2,1)S(1)}, bf16[256,1024]{1,0:T(8,128)(2,1)S(1)}, u32[]{:S(2)}, u32[]{:S(2)}) %collective-permute-start) | collective-permute-done | bytes 524320 | tf_op jit(solution)/shard_map/ppermute | solution.py:122
  42.3 1.0 pad_maximum_fusion.1
  43.4 1.2 collective-permute-start.1
  44.6 0.6 convert_reduce_fusion.2
  45.2 0.7 slice_reduce_fusion
  46.7 0.6 fusion.65
  47.3 1.3 fusion.134
  48.6 0.8 copy-done.2
  49.3 1.5 pad_maximum_fusion
  50.9 1.1 conditional.1
  50.9 1.1 broadcast.1020
  52.0 8.8 %fusion.30 = bf16[2560,1024]{1,0:T(8,128)(2,1)} fusion(s32[2560]{0:T(1024)} %fusion.65, bf16[256,1024]{1,0:T(8,128)(2,1)} %copy-done.3, bf16[256,1024]{1,0:T(8,128)(2,1)S(1)} %collective-permute-done, bf16[256,1024]{1,0:T(8,128)(2,1)} %copy-done.2, bf16[256,1024]{1,0:T(8,128)(2,1)S(1)} %fusion.37), kind=kOutput, calls=%fused_computation.57 | convolution fusion | flops 5382340608 | bytes 7350272 | tf_op jit(solution)/shard_map/dot_general | solution.py:79
  60.8 10.3 %all-to-all-start.2 = ((bf16[64,40,1024]{2,1,0:T(8,128)(2,1)}), bf16[64,40,1024]{2,1,0:T(8,128)(2,1)}, u32[]{:S(2)}, u32[]{:S(2)}) async-start(bf16[64,40,1024]{2,1,0:T(8,128)(2,1)} %bitcast.69), calls=%async_computation.2 | async-start | bytes 10485760 | tf_op jit(solution)/shard_map/all_to_all | solution.py:81
  71.4 0.1 copy.60
  71.6 0.8 copy.59
  72.4 3.3 %fusion.138 = f32[256,1024]{1,0:T(8,128)} fusion(bf16[256,1024]{1,0:T(8,128)(2,1)S(1)} %copy-done.5, bf16[1024,1024]{1,0:T(8,128)(2,1)} %param.19), kind=kOutput, calls=%fused_computation.300 | convolution fusion | flops 536870912 | bytes 3670016 | tf_op jit(solution)/shard_map/dot_general | solution.py:154
  75.7 9.1 %select_reduce_fusion.1 = bf16[256,2560]{1,0:T(8,128)(2,1)S(1)} fusion(f32[256,8]{1,0:T(8,128)S(1)} %copy.60, s32[256,8]{1,0:T(8,128)S(1)} %copy-done.6), kind=kLoop, calls=%fused_computation.53 | loop fusion | flops 15073280 | bytes 1327104 | tf_op jit(solution)/shard_map/reduce_sum | solution.py:89
  84.8 104.7 %all-to-all-done.2 = bf16[64,40,1024]{2,1,0:T(8,128)(2,1)} async-done(((bf16[64,40,1024]{2,1,0:T(8,128)(2,1)}), bf16[64,40,1024]{2,1,0:T(8,128)(2,1)}, u32[]{:S(2)}, u32[]{:S(2)}) %all-to-all-start.2) | async-done | bytes 5242912 | tf_op jit(solution)/shard_map/all_to_all | solution.py:81
  189.5 6.2 %multiply_reduce_fusion.1 = (f32[256]{0:T(256)S(1)}, f32[256,1024]{1,0:T(8,128)}) fusion(f32[1024]{0:T(1024)S(1)} %copy-done.14, f32[256,1024]{1,0:T(8,128)} %fusion.138, bf16[1024,1024]{1,0:T(8,128)(2,1)S(1)} %copy-done, f32[256,1024]{1,0:T(8,128)} %get-tuple-element.228, bf16[2560,1024]{1,0:T(8,128)(2,1)} %bitcast.16, ...), kind=kOutput, calls=%fused_computation.84 | convolution fusion | flops 1881145088 | bytes 11802624 | tf_op jit(solution)/shard_map/dot_general | solution.py:155
  195.7 1.3 multiply_convert_fusion
  197.1 0.2 fusion.42
  197.4 0.2 fusion.41
  197.6 0.7 pad_maximum_fusion.2
  198.3 21.4 %all-gather.2.cloned.1.call-done = bf16[4,128,1024]{2,1,0:T(8,128)(2,1)} async-done(((bf16[1,128,1024]{2,1,0:T(8,128)(2,1)}), bf16[4,128,1024]{2,1,0:T(8,128)(2,1)}) %all-gather.2.cloned.1.call-update) | async-done | bytes 1048592 | tf_op jit(solution)/shard_map/all_gather | solution.py:170
  219.7 1.4 multiply_reduce_fusion
  221.2 1.4 fusion.40
  222.6 0.1 reshape.727
  222.7 0.3 reduce_sum.97
  223.2 0.7 reshape.746
  223.9 3.6 %all-to-all-start.3 = ((f32[4,1,128]{2,1,0:T(1,128)}), f32[4,1,128]{2,1,0:T(1,128)S(1)}, u32[]{:S(2)}, u32[]{:S(2)}) async-start(f32[4,1,128]{2,1,0:T(1,128)} %reshape.746), calls=%async_computation.3 | async-start | bytes 4096 | tf_op jit(solution)/shard_map/all_to_all | solution.py:190
  227.5 4.0 %all-to-all-done.3 = f32[4,1,128]{2,1,0:T(1,128)S(1)} async-done(((f32[4,1,128]{2,1,0:T(1,128)}), f32[4,1,128]{2,1,0:T(1,128)S(1)}, u32[]{:S(2)}, u32[]{:S(2)}) %all-to-all-start.3) | async-done | bytes 2080 | tf_op jit(solution)/shard_map/all_to_all | solution.py:190
  231.5 0.5 broadcast.1193
  232.0 0.7 reduce.4
  232.8 0.7 select_reduce_fusion.2
  (64 shorter events, 1.2 us)
Async XLA Ops:
  7.2 182.3 %copy-start = (bf16[1024,1024]{1,0:T(8,128)(2,1)S(1)}, bf16[1024,1024]{1,0:T(8,128)(2,1)}, u32[]{:S(2)}) copy-start(bf16[1024,1024]{1,0:T(8,128)(2,1)} %param.20) | copy-start | bytes 6291460
  7.2 19.4 %copy-start.4 = (bf16[256,1024]{1,0:T(8,128)(2,1)S(1)}, bf16[256,1024]{1,0:T(8,128)(2,1)}, u32[]{:S(2)}) copy-start(bf16[256,1024]{1,0:T(8,128)(2,1)} %param.16) | copy-start | bytes 1572868
  7.2 19.4 %copy-start.13 = (f32[1024]{0:T(1024)S(1)}, f32[1024]{0:T(1024)}, u32[]{:S(2)}) copy-start(f32[1024]{0:T(1024)} %param.18) | copy-start | bytes 12292
  9.0 21.4 %copy-start.9 = (s32[2]{0:T(128)S(1)}, s32[2]{0:T(128)}, u32[]{:S(2)}) copy-start(s32[2]{0:T(128)} %param.24) | copy-start | bytes 28
  11.6 33.0 %copy-start.8 = (s32[256,8]{0,1:T(8,128)S(1)}, s32[256,8]{0,1:T(8,128)}, u32[]{:S(2)}) copy-start(s32[256,8]{0,1:T(8,128)} %param.23) | copy-start | bytes 24580
  13.6 31.6 %all-to-all-start.1 = ((s32[64,1,65]{2,1,0:T(1,128)}), s32[64,1,65]{2,1,0:T(1,128)S(1)}, u32[]{:S(2)}, u32[]{:S(2)}) async-start(s32[64,1,65]{2,1,0:T(1,128)} %bitcast.13), calls=%async_computation.1 | async-start | bytes 65536 | tf_op jit(solution)/shard_map/all_to_all | solution.py:118
  28.9 13.4 %collective-permute-start = (bf16[256,1024]{1,0:T(8,128)(2,1)S(1)}, bf16[256,1024]{1,0:T(8,128)(2,1)S(1)}, u32[]{:S(2)}, u32[]{:S(2)}) collective-permute-start(bf16[256,1024]{1,0:T(8,128)(2,1)S(1)} %fusion.37), channel_id=1, source_target_pairs={{0,16},{1,17},{2,18},{3,19},{4,20},{5,21},{6,22},{7,23},{8,24},{9,... | collective-permute-start | bytes 1572872 | tf_op jit(solution)/shard_map/ppermute | solution.py:122
  43.4 3.9 %collective-permute-start.1 = (bf16[512,1024]{1,0:T(8,128)(2,1)}, bf16[512,1024]{1,0:T(8,128)(2,1)}, u32[]{:S(2)}, u32[]{:S(2)}) collective-permute-start(bf16[512,1024]{1,0:T(8,128)(2,1)} %pad_maximum_fusion.1), channel_id=1, source_target_pairs={{0,1},{1,0},{2,3},{3,2},{4,5},{5,4},{6,7},{7,6},{8,9},{9,8},{10,11... | collective-permute-start | bytes 3145736 | tf_op jit(solution)/shard_map/ppermute | solution.py:124
  48.5 0.8 copy-start.2
  48.6 2.3 copy-start.3
  60.8 10.6 %copy-start.7 = (s32[256,8]{0,1:T(8,128)S(1)}, s32[256,8]{0,1:T(8,128)}, u32[]{:S(2)}) copy-start(s32[256,8]{0,1:T(8,128)} %param.22) | copy-start | bytes 24580
  60.8 11.6 %copy-start.5 = (bf16[256,1024]{1,0:T(8,128)(2,1)S(1)}, bf16[256,1024]{1,0:T(8,128)(2,1)}, u32[]{:S(2)}) copy-start(bf16[256,1024]{1,0:T(8,128)(2,1)} %param.16) | copy-start | bytes 1572868
  60.8 128.7 %all-to-all-start.2 = ((bf16[64,40,1024]{2,1,0:T(8,128)(2,1)}), bf16[64,40,1024]{2,1,0:T(8,128)(2,1)}, u32[]{:S(2)}, u32[]{:S(2)}) async-start(bf16[64,40,1024]{2,1,0:T(8,128)(2,1)} %bitcast.69), calls=%async_computation.2 | async-start | bytes 10485760 | tf_op jit(solution)/shard_map/all_to_all | solution.py:81
  71.2 118.4 %copy-start.10 = (f32[256]{0:T(256)S(1)}, f32[256]{0:T(256)}, u32[]{:S(2)}) copy-start(f32[256]{0:T(256)} %get-tuple-element.191) | copy-start | bytes 3076
  71.2 118.3 %copy-start.14 = (f32[1024]{0:T(1024)S(1)}, f32[1024]{0:T(1024)}, u32[]{:S(2)}) copy-start(f32[1024]{0:T(1024)} %param.21) | copy-start | bytes 12292
  71.2 148.6 %all-gather.2.cloned.1.call-start = ((), (), s32[]{:S(2)}) async-start(), calls=%async_computation.4 | async-start | bytes 1310720 | tf_op jit(solution)/shard_map/all_gather | solution.py:170
  72.4 3.3 %copy-start.6 = (s32[256,8]{1,0:T(8,128)S(1)}, s32[256,8]{1,0:T(8,128)}, u32[]{:S(2)}) copy-start(s32[256,8]{1,0:T(8,128)} %copy.59) | copy-start | bytes 24580
  189.5 7.5 %copy-start.11 = (s32[64]{0:T(128)S(1)}, s32[64]{0:T(128)}, u32[]{:S(2)}) copy-start(s32[64]{0:T(128)} %param.26) | copy-start | bytes 772
  189.5 7.8 %copy-start.12 = (s32[64]{0:T(128)S(1)}, s32[64]{0:T(128)}, u32[]{:S(2)}) copy-start(s32[64]{0:T(128)} %param.25) | copy-start | bytes 772
  197.1 36.4 %copy-start.1 = (bf16[256,1024]{1,0:T(8,128)(2,1)}, bf16[256,1024]{1,0:T(8,128)(2,1)S(1)}, u32[]{:S(2)}) copy-start(bf16[256,1024]{1,0:T(8,128)(2,1)S(1)} %multiply_convert_fusion) | copy-start | bytes 1572868
  197.1 30.4 %copy-start.15 = (s32[1,4]{1,0:T(1,128)S(1)}, s32[1,4]{1,0:T(1,128)}, u32[]{:S(2)}) copy-start(s32[1,4]{1,0:T(1,128)} %param.27) | copy-start | bytes 52
  223.9 7.7 %all-to-all-start.3 = ((f32[4,1,128]{2,1,0:T(1,128)}), f32[4,1,128]{2,1,0:T(1,128)S(1)}, u32[]{:S(2)}, u32[]{:S(2)}) async-start(f32[4,1,128]{2,1,0:T(1,128)} %reshape.746), calls=%async_computation.3 | async-start | bytes 4096 | tf_op jit(solution)/shard_map/all_to_all | solution.py:190
Sparse Core Ops, SparseCore 0:
  198.5 21.2 all-gather.1

commit v7 on v5

--- a/solution.py
+++ b/solution.py
@@ -113,10 +113,10 @@
     server = group_base + (turn // 2) * partner + turn % 2
     server_rank = group_rank // members
     value = (high * 2 + low) * item_dev + local_row
-    requests = make_requests(server, value, server_rank, main_cap)
+    requests = make_requests(server, value, server_rank, capacity)
     flagged = jnp.concatenate([requests, jnp.broadcast_to(crowded, (shards, 1))], axis=1)
     received = lax.all_to_all(flagged, "shard", split_axis=0, concat_axis=0, tiled=True)
-    region_crowded = jnp.max(received[:, main_cap])
+    region_crowded = jnp.max(received[:, capacity])
     me = lax.axis_index("shard")
     my_code = ((me // partner) % 2) * 2 + me % 2
     sibling = lax.ppermute(projected, "shard", [(i, i ^ 1) for i in range(shards)])
@@ -138,15 +138,9 @@
 
     def spill(_):
         spill_rank = server_rank - main_cap
-        spill_requests = make_requests(server, value, spill_rank, spill_cap)
-        wanted = lax.all_to_all(spill_requests, "shard", split_axis=0, concat_axis=0, tiled=True)
+        wanted = received[:, main_cap:capacity].reshape(-1)
         return serve(
-            server,
-            spill_rank,
-            spill_cap,
-            table,
-            table_index(wanted.reshape(-1)),
-            spill_rank >= 0,
+            server, spill_rank, spill_cap, table, table_index(wanted), spill_rank >= 0
         )
 
     def no_spill(_):

time: 228 us -> 227 us (level)
  no operation moved by 1% of the time
where the time goes in v7:
time: 227 us
  waiting for transfers between devices  136 us (60%)
  matrix products  27.1 us (12%)
  other arithmetic  22.7 us (10%)
  starting transfers between devices  20.7 us (9%)
  between operations  15.7 us (7%)
  local copies, waits for them, and re-layouts  4.02 us (2%)
    all_to_all x1, waiting for transfers between devices, serve(): lax.all_to_all(outgoing, 'shard', split_axis=0, concat_axis=0, tiled=True)  104 us
    all_gather x1, waiting for transfers between devices, body(): lax.all_gather(embedding, 'region', axis=0, tiled=True)  27.3 us
    all_to_all x1, starting transfers between devices, body(): lax.all_to_all(flagged, 'shard', split_axis=0, concat_axis=0, tiled=True)  11 us
    reduce_sum x1, other arithmetic, serve(): mix = jnp.sum(spread, axis=1).astype(jnp.bfloat16)  9.1 us
    dot_general x1, matrix products, serve(): jnp.dot(pick, table, preferred_element_type=jnp.float32)  8.87 us
    dot_general x1, matrix products, body(): jnp.dot(aggregate, nbr_weight, preferred_element_type=jnp.float32)  6.15 us
    all_to_all x1, starting transfers between devices, serve(): lax.all_to_all(outgoing, 'shard', split_axis=0, concat_axis=0, tiled=True)  5.84 us
    all_to_all x1, waiting for transfers between devices, body(): lax.all_to_all(flagged, 'shard', split_axis=0, concat_axis=0, tiled=True)  5.12 us
  transfers between devices with their start and end apart: 6, of which 3 were waited for; matrix products, arithmetic and copies ran while one was open for 12% of the time, Pallas kernels for 0%

profile of v7, /device:TPU:1, one launch (start us, length us, event | category | flops | bytes accessed | tf_op | source)
XLA Modules:
  0.0 226.7 jit_solution(17703175844196886202)
XLA Ops:
  7.2 2.5 %fusion.37 = bf16[256,1024]{1,0:T(8,128)(2,1)S(1)} fusion(bf16[256,1024]{1,0:T(8,128)(2,1)} %param.16, bf16[1024,1024]{1,0:T(8,128)(2,1)} %param.17, f32[1024]{0:T(1024)} %param.18), kind=kOutput, calls=%fused_computation.67 | convolution fusion | flops 537657344 | bytes 3149824 | tf_op jit(solution)/shard_map/dot_general | solution.py:50
  9.7 2.1 collective-permute-start.1
  11.9 1.3 collective-permute-start
  13.1 0.1 copy.49
  13.3 0.1 reshape.693
  13.4 0.1 reshape.694
  13.5 0.1 convert_reduce_fusion.1
  13.6 0.1 fusion.106
  13.8 0.2 fusion.45
  14.1 1.6 select_convert_fusion.2
  15.7 0.9 convolution_convert_fusion
  16.6 0.1 slice_add_fusion
  16.7 0.1 convert_reduce_fusion
  16.8 0.6 reduce_max.18
  18.1 0.6 concatenate.15
  18.7 11.0 %all-to-all-start.1 = ((s32[64,1,65]{2,1,0:T(1,128)}), s32[64,1,65]{2,1,0:T(1,128)S(1)}, u32[]{:S(2)}, u32[]{:S(2)}) async-start(s32[64,1,65]{2,1,0:T(1,128)} %bitcast.13), calls=%async_computation.1 | async-start | bytes 65536 | tf_op jit(solution)/shard_map/all_to_all | solution.py:118
  29.7 0.6 fusion.135
  30.3 1.3 compare_select_fusion.1
  31.6 0.6 fusion.134
  32.2 1.2 convert_reduce_fusion.2
  33.4 0.5 collective-permute-start.2
  33.9 5.1 %all-to-all-done.1 = s32[64,1,65]{2,1,0:T(1,128)S(1)} async-done(((s32[64,1,65]{2,1,0:T(1,128)}), s32[64,1,65]{2,1,0:T(1,128)S(1)}, u32[]{:S(2)}, u32[]{:S(2)}) %all-to-all-start.1) | async-done | bytes 16672 | tf_op jit(solution)/shard_map/all_to_all | solution.py:118
  39.0 0.8 slice_reduce_fusion
  40.5 0.1 reshape.695
  40.5 0.6 fusion.65
  41.2 2.7 %pad_maximum_fusion = bf16[1024,1024]{1,0:T(8,128)(2,1)} fusion(bf16[256,1024]{1,0:T(8,128)(2,1)} %collective-permute-done.2, bf16[256,1024]{1,0:T(8,128)(2,1)S(1)} %collective-permute-done.1, bf16[256,1024]{1,0:T(8,128)(2,1)} %collective-permute-done, bf16[256,1024]{1,0:T(8,128)(2,1)S(1)} %fusion.37), kind=kLoop, calls=%fused_computation.59 | loop fusion | flops 8388608 | bytes 4194304 | tf_op jit(solution)/shard_map/concatenate | solution.py:125
  43.9 1.2 conditional.1
  43.9 1.1 broadcast.1024
  45.0 8.9 %fusion.30 = bf16[2560,1024]{1,0:T(8,128)(2,1)} fusion(s32[2560]{0:T(1024)} %fusion.65, bf16[256,1024]{1,0:T(8,128)(2,1)} %collective-permute-done.2, bf16[256,1024]{1,0:T(8,128)(2,1)} %copy-done.3, bf16[256,1024]{1,0:T(8,128)(2,1)} %collective-permute-done, bf16[256,1024]{1,0:T(8,128)(2,1)S(1)} %fusion.37), kind=kOutput, calls=%fused_computation.57 | convolution fusion | flops 5382340608 | bytes 7350272 | tf_op jit(solution)/shard_map/dot_general | solution.py:79
  53.9 5.8 %all-to-all-start.2 = ((bf16[64,40,1024]{2,1,0:T(8,128)(2,1)}), bf16[64,40,1024]{2,1,0:T(8,128)(2,1)}, u32[]{:S(2)}, u32[]{:S(2)}) async-start(bf16[64,40,1024]{2,1,0:T(8,128)(2,1)} %bitcast.61), calls=%async_computation.2 | async-start | bytes 10485760 | tf_op jit(solution)/shard_map/all_to_all | solution.py:81
  59.8 0.1 convert_element_type.100
  60.0 0.1 copy.50
  60.0 0.8 fusion.77
  60.8 0.1 copy.55
  60.9 0.8 copy.54
  61.7 3.3 %fusion.137 = f32[256,1024]{1,0:T(8,128)} fusion(bf16[256,1024]{1,0:T(8,128)(2,1)S(1)} %copy-done.1, bf16[1024,1024]{1,0:T(8,128)(2,1)} %param.19), kind=kOutput, calls=%fused_computation.295 | convolution fusion | flops 536870912 | bytes 3670016 | tf_op jit(solution)/shard_map/dot_general | solution.py:152
  65.0 9.1 %select_reduce_fusion.1 = bf16[256,2560]{1,0:T(8,128)(2,1)S(1)} fusion(f32[256,8]{1,0:T(8,128)S(1)} %copy.55, s32[256,8]{1,0:T(8,128)S(1)} %copy-done.2), kind=kLoop, calls=%fused_computation.53 | loop fusion | flops 15073280 | bytes 1327104 | tf_op jit(solution)/shard_map/reduce_sum | solution.py:89
  74.1 104.1 %all-to-all-done.2 = bf16[64,40,1024]{2,1,0:T(8,128)(2,1)} async-done(((bf16[64,40,1024]{2,1,0:T(8,128)(2,1)}), bf16[64,40,1024]{2,1,0:T(8,128)(2,1)}, u32[]{:S(2)}, u32[]{:S(2)}) %all-to-all-start.2) | async-done | bytes 5242912 | tf_op jit(solution)/shard_map/all_to_all | solution.py:81
  178.2 6.1 %multiply_reduce_fusion = (f32[256]{0:T(256)S(1)}, f32[256,1024]{1,0:T(8,128)}) fusion(f32[1024]{0:T(1024)S(1)} %copy-done.12, f32[256,1024]{1,0:T(8,128)} %fusion.137, bf16[1024,1024]{1,0:T(8,128)(2,1)S(1)} %copy-done, f32[256,1024]{1,0:T(8,128)} %get-tuple-element.226, bf16[2560,1024]{1,0:T(8,128)(2,1)} %bitcast.16, ...), kind=kOutput, calls=%fused_computation.81 | convolution fusion | flops 1881145088 | bytes 11802624 | tf_op jit(solution)/shard_map/dot_general | solution.py:153
  184.4 2.1 multiply_convert_fusion
  186.5 0.1 iota_compare_fusion.24
  186.6 1.3 fusion.60
  187.9 1.4 fusion.42
  189.3 27.3 %all-gather.2.cloned.1.call-done = bf16[1024,1024]{1,0:T(8,128)(2,1)} async-done(((bf16[256,1024]{1,0:T(8,128)(2,1)}), bf16[1024,1024]{1,0:T(8,128)(2,1)}) %all-gather.2.cloned.1.call-update) | async-done | bytes 2097168 | tf_op jit(solution)/shard_map/all_gather | solution.py:173
  216.6 2.4 %fusion.41 = f32[8,8,8,128]{3,1,2,0:T(8,128)S(1)} fusion(bf16[1024,1024]{1,0:T(8,128)(2,1)} %all-gather.2.cloned.1.call-done, f32[64]{0:T(128)S(1)} %broadcast_multiply_fusion.1, f32[64,1024]{1,0:T(8,128)S(1)} %fusion.60), kind=kOutput, calls=%fused_computation.73 | convolution fusion | flops 134545408 | bytes 2621696 | tf_op jit(solution)/shard_map/dot_general | solution.py:171
  219.0 0.1 reduce_sum.97
  219.1 0.1 copy.59
  219.2 0.7 select_reduce_fusion.2
  (52 shorter events, 0.4 us)
Async XLA Ops:
  7.2 171.0 %copy-start = (bf16[1024,1024]{1,0:T(8,128)(2,1)S(1)}, bf16[1024,1024]{1,0:T(8,128)(2,1)}, u32[]{:S(2)}) copy-start(bf16[1024,1024]{1,0:T(8,128)(2,1)} %param.20) | copy-start | bytes 6291460
  7.2 6.0 %copy-start.4 = (s32[256,8]{0,1:T(8,128)S(1)}, s32[256,8]{0,1:T(8,128)}, u32[]{:S(2)}) copy-start(s32[256,8]{0,1:T(8,128)} %param.22) | copy-start | bytes 24580
  7.2 22.5 %copy-start.8 = (s32[2]{0:T(128)S(1)}, s32[2]{0:T(128)}, u32[]{:S(2)}) copy-start(s32[2]{0:T(128)} %param.24) | copy-start | bytes 28
  7.2 25.0 %copy-start.7 = (s32[256,8]{0,1:T(8,128)S(1)}, s32[256,8]{0,1:T(8,128)}, u32[]{:S(2)}) copy-start(s32[256,8]{0,1:T(8,128)} %param.23) | copy-start | bytes 24580
  9.7 23.7 %collective-permute-start.1 = (bf16[256,1024]{1,0:T(8,128)(2,1)S(1)}, bf16[256,1024]{1,0:T(8,128)(2,1)S(1)}, u32[]{:S(2)}, u32[]{:S(2)}) collective-permute-start(bf16[256,1024]{1,0:T(8,128)(2,1)S(1)} %fusion.37), channel_id=1, source_target_pairs={{0,16},{1,17},{2,18},{3,19},{4,20},{5,21},{6,22},{7,23},{8,24},{9,... | collective-permute-start | bytes 1572872 | tf_op jit(solution)/shard_map/ppermute | solution.py:123
  11.9 29.3 %collective-permute-start = (bf16[256,1024]{1,0:T(8,128)(2,1)S(1)}, bf16[256,1024]{1,0:T(8,128)(2,1)}, u32[]{:S(2)}, u32[]{:S(2)}) collective-permute-start(bf16[256,1024]{1,0:T(8,128)(2,1)S(1)} %fusion.37), channel_id=1, source_target_pairs={{0,1},{1,0},{2,3},{3,2},{4,5},{5,4},{6,7},{7,6},{8,9},{9,8},{10,11... | collective-permute-start | bytes 1572872 | tf_op jit(solution)/shard_map/ppermute | solution.py:122
  18.7 20.3 %all-to-all-start.1 = ((s32[64,1,65]{2,1,0:T(1,128)}), s32[64,1,65]{2,1,0:T(1,128)S(1)}, u32[]{:S(2)}, u32[]{:S(2)}) async-start(s32[64,1,65]{2,1,0:T(1,128)} %bitcast.13), calls=%async_computation.1 | async-start | bytes 65536 | tf_op jit(solution)/shard_map/all_to_all | solution.py:118
  33.4 10.5 %copy-start.3 = (bf16[256,1024]{1,0:T(8,128)(2,1)}, bf16[256,1024]{1,0:T(8,128)(2,1)S(1)}, u32[]{:S(2)}) copy-start(bf16[256,1024]{1,0:T(8,128)(2,1)S(1)} %collective-permute-done.1) | copy-start | bytes 1572868
  33.4 7.8 %collective-permute-start.2 = (bf16[256,1024]{1,0:T(8,128)(2,1)S(1)}, bf16[256,1024]{1,0:T(8,128)(2,1)}, u32[]{:S(2)}, u32[]{:S(2)}) collective-permute-start(bf16[256,1024]{1,0:T(8,128)(2,1)S(1)} %collective-permute-done.1), channel_id=1, source_target_pairs={{0,1},{1,0},{2,3},{3,2},{4,5},{5,4},{6,7},{7,6},{8,9},{9,8},{10,11... | collective-permute-start | bytes 1572872 | tf_op jit(solution)/shard_map/ppermute | solution.py:124
  53.9 5.9 %copy-start.6 = (s32[16,128]{1,0:T(8,128)S(1)}, s32[16,128]{1,0:T(8,128)}, u32[]{:S(2)}) copy-start(s32[16,128]{1,0:T(8,128)} %get-tuple-element.201) | copy-start | bytes 24580
  53.9 6.1 %copy-start.5 = (s32[256,8]{0,1:T(8,128)S(1)}, s32[256,8]{0,1:T(8,128)}, u32[]{:S(2)}) copy-start(s32[256,8]{0,1:T(8,128)} %param.22) | copy-start | bytes 24580
  53.9 7.8 %copy-start.1 = (bf16[256,1024]{1,0:T(8,128)(2,1)S(1)}, bf16[256,1024]{1,0:T(8,128)(2,1)}, u32[]{:S(2)}) copy-start(bf16[256,1024]{1,0:T(8,128)(2,1)} %param.16) | copy-start | bytes 1572868
  53.9 124.2 %all-to-all-start.2 = ((bf16[64,40,1024]{2,1,0:T(8,128)(2,1)}), bf16[64,40,1024]{2,1,0:T(8,128)(2,1)}, u32[]{:S(2)}, u32[]{:S(2)}) async-start(bf16[64,40,1024]{2,1,0:T(8,128)(2,1)} %bitcast.61), calls=%async_computation.2 | async-start | bytes 10485760 | tf_op jit(solution)/shard_map/all_to_all | solution.py:81
  59.8 118.4 %copy-start.9 = (f32[256]{0:T(256)S(1)}, f32[256]{0:T(256)}, u32[]{:S(2)}) copy-start(f32[256]{0:T(256)} %get-tuple-element.191) | copy-start | bytes 3076
  59.8 118.4 %copy-start.12 = (f32[1024]{0:T(1024)S(1)}, f32[1024]{0:T(1024)}, u32[]{:S(2)}) copy-start(f32[1024]{0:T(1024)} %param.21) | copy-start | bytes 12292
  59.8 156.8 %all-gather.2.cloned.1.call-start = ((), (), s32[]{:S(2)}) async-start(), calls=%async_computation.3 | async-start | bytes 2621440 | tf_op jit(solution)/shard_map/all_gather | solution.py:173
  61.7 3.3 %copy-start.2 = (s32[256,8]{1,0:T(8,128)S(1)}, s32[256,8]{1,0:T(8,128)}, u32[]{:S(2)}) copy-start(s32[256,8]{1,0:T(8,128)} %copy.54) | copy-start | bytes 24580
  178.2 8.4 %copy-start.13 = (s32[1,4]{1,0:T(1,128)S(1)}, s32[1,4]{1,0:T(1,128)}, u32[]{:S(2)}) copy-start(s32[1,4]{1,0:T(1,128)} %param.27) | copy-start | bytes 52
  178.2 8.4 %copy-start.11 = (s32[64]{0:T(128)S(1)}, s32[64]{0:T(128)}, u32[]{:S(2)}) copy-start(s32[64]{0:T(128)} %param.25) | copy-start | bytes 772
  178.2 9.7 %copy-start.10 = (s32[64]{0:T(128)S(1)}, s32[64]{0:T(128)}, u32[]{:S(2)}) copy-start(s32[64]{0:T(128)} %param.26) | copy-start | bytes 772
Sparse Core Ops, SparseCore 0:
  186.7 29.8 all-gather.1

commit v8 on v7

--- a/solution.py
+++ b/solution.py
@@ -170,7 +170,13 @@
         / hidden
         * jnp.dot(
             query_emb.astype(jnp.bfloat16),
-            lax.all_gather(embedding, "region", axis=0, tiled=True).T,
+            lax.all_to_all(
+                jnp.tile(embedding, (lax.axis_size("region"), 1)),
+                "region",
+                split_axis=0,
+                concat_axis=0,
+                tiled=True,
+            ).T,
             preferred_element_type=jnp.float32,
         )
     )

time: 227 us -> 215 us (0.947)
  between operations: 15.7 us -> 2.32 us
  starting transfers between devices: 20.7 us -> 25.2 us
    all_gather x1 -> x0, waiting for transfers between devices: 27.3 us -> none  [body(): lax.all_gather(embedding, 'region', axis=0, tiled=True)]
    all_to_all x0 -> x1, waiting for transfers between devices: none -> 25.5 us  [body(): lax.all_to_all(jnp.tile(embedding, (lax.axis_size('region'), 1)), 'region...]
    all_to_all x0 -> x1, starting transfers between devices: none -> 4.57 us  [body(): lax.all_to_all(jnp.tile(embedding, (lax.axis_size('region'), 1)), 'region...]
where the time goes in v8:
time: 215 us
  waiting for transfers between devices  135 us (63%)
  starting transfers between devices  25.2 us (12%)
  matrix products  25 us (12%)
  other arithmetic  22 us (10%)
  local copies, waits for them, and re-layouts  5.6 us (3%)
  between operations  2.32 us (1%)
    all_to_all x1, waiting for transfers between devices, serve(): lax.all_to_all(outgoing, 'shard', split_axis=0, concat_axis=0, tiled=True)  104 us
    all_to_all x1, waiting for transfers between devices, body(): lax.all_to_all(jnp.tile(embedding, (lax.axis_size('region'), 1)), 'region...  25.5 us
    all_to_all x1, starting transfers between devices, body(): lax.all_to_all(flagged, 'shard', split_axis=0, concat_axis=0, tiled=True)  11 us
    reduce_sum x1, other arithmetic, serve(): mix = jnp.sum(spread, axis=1).astype(jnp.bfloat16)  9.1 us
    dot_general x1, matrix products, serve(): jnp.dot(pick, table, preferred_element_type=jnp.float32)  8.87 us
    dot_general x1, matrix products, body(): jnp.dot(aggregate, nbr_weight, preferred_element_type=jnp.float32)  6.14 us
    all_to_all x1, starting transfers between devices, serve(): lax.all_to_all(outgoing, 'shard', split_axis=0, concat_axis=0, tiled=True)  5.84 us
    all_to_all x1, waiting for transfers between devices, body(): lax.all_to_all(flagged, 'shard', split_axis=0, concat_axis=0, tiled=True)  5.12 us
  transfers between devices with their start and end apart: 6, of which 3 were waited for; matrix products, arithmetic and copies ran while one was open for 12% of the time, Pallas kernels for 0%

profile of v8, /device:TPU:1, one launch (start us, length us, event | category | flops | bytes accessed | tf_op | source)
XLA Modules:
  0.0 214.9 jit_solution(4925608072198699215)
XLA Ops:
  0.7 2.5 %fusion.37 = bf16[256,1024]{1,0:T(8,128)(2,1)S(1)} fusion(bf16[256,1024]{1,0:T(8,128)(2,1)} %param.16, bf16[1024,1024]{1,0:T(8,128)(2,1)} %param.17, f32[1024]{0:T(1024)} %param.18), kind=kOutput, calls=%fused_computation.67 | convolution fusion | flops 537657344 | bytes 3149824 | tf_op jit(solution)/shard_map/dot_general | solution.py:50
  3.2 2.1 collective-permute-start.1
  5.3 1.3 collective-permute-start
  6.6 0.1 copy.49
  6.7 0.1 reshape.700
  6.8 0.1 reshape.701
  7.0 0.1 convert_reduce_fusion.1
  7.1 0.1 fusion.106
  7.2 0.2 fusion.45
  7.5 1.6 select_convert_fusion.2
  9.2 0.9 convolution_convert_fusion
  10.1 0.1 slice_add_fusion
  10.1 0.1 convert_reduce_fusion
  10.3 0.6 reduce_max.18
  11.5 0.6 concatenate.15
  12.1 11.0 %all-to-all-start.1 = ((s32[64,1,65]{2,1,0:T(1,128)}), s32[64,1,65]{2,1,0:T(1,128)S(1)}, u32[]{:S(2)}, u32[]{:S(2)}) async-start(s32[64,1,65]{2,1,0:T(1,128)} %bitcast.13), calls=%async_computation.1 | async-start | bytes 65536 | tf_op jit(solution)/shard_map/all_to_all | solution.py:118
  23.2 0.6 fusion.135
  23.8 1.3 compare_select_fusion.1
  25.1 0.6 fusion.134
  25.7 1.2 convert_reduce_fusion.2
  26.9 0.5 collective-permute-start.2
  27.3 5.1 %all-to-all-done.1 = s32[64,1,65]{2,1,0:T(1,128)S(1)} async-done(((s32[64,1,65]{2,1,0:T(1,128)}), s32[64,1,65]{2,1,0:T(1,128)S(1)}, u32[]{:S(2)}, u32[]{:S(2)}) %all-to-all-start.1) | async-done | bytes 16672 | tf_op jit(solution)/shard_map/all_to_all | solution.py:118
  32.5 0.8 slice_reduce_fusion
  33.9 0.1 reshape.702
  34.0 0.6 fusion.65
  34.6 2.7 %pad_maximum_fusion = bf16[1024,1024]{1,0:T(8,128)(2,1)} fusion(bf16[256,1024]{1,0:T(8,128)(2,1)} %collective-permute-done.2, bf16[256,1024]{1,0:T(8,128)(2,1)S(1)} %collective-permute-done.1, bf16[256,1024]{1,0:T(8,128)(2,1)} %collective-permute-done, bf16[256,1024]{1,0:T(8,128)(2,1)S(1)} %fusion.37), kind=kLoop, calls=%fused_computation.59 | loop fusion | flops 8388608 | bytes 4194304 | tf_op jit(solution)/shard_map/concatenate | solution.py:125
  37.3 1.2 conditional.1
  37.4 1.1 broadcast.1027
  38.5 8.9 %fusion.30 = bf16[2560,1024]{1,0:T(8,128)(2,1)} fusion(s32[2560]{0:T(1024)} %fusion.65, bf16[256,1024]{1,0:T(8,128)(2,1)} %collective-permute-done.2, bf16[256,1024]{1,0:T(8,128)(2,1)} %copy-done.4, bf16[256,1024]{1,0:T(8,128)(2,1)} %collective-permute-done, bf16[256,1024]{1,0:T(8,128)(2,1)S(1)} %fusion.37), kind=kOutput, calls=%fused_computation.57 | convolution fusion | flops 5382340608 | bytes 7350272 | tf_op jit(solution)/shard_map/dot_general | solution.py:79
  47.4 5.8 %all-to-all-start.2 = ((bf16[64,40,1024]{2,1,0:T(8,128)(2,1)}), bf16[64,40,1024]{2,1,0:T(8,128)(2,1)}, u32[]{:S(2)}, u32[]{:S(2)}) async-start(bf16[64,40,1024]{2,1,0:T(8,128)(2,1)} %bitcast.62), calls=%async_computation.2 | async-start | bytes 10485760 | tf_op jit(solution)/shard_map/all_to_all | solution.py:81
  53.3 0.1 convert_element_type.100
  53.4 0.8 fusion.77
  54.2 0.1 copy.55
  54.3 0.8 copy.54
  55.1 3.3 %fusion.137 = f32[256,1024]{1,0:T(8,128)} fusion(bf16[256,1024]{1,0:T(8,128)(2,1)S(1)} %copy-done.2, bf16[1024,1024]{1,0:T(8,128)(2,1)} %param.19), kind=kOutput, calls=%fused_computation.295 | convolution fusion | flops 536870912 | bytes 3670016 | tf_op jit(solution)/shard_map/dot_general | solution.py:152
  58.4 9.1 %select_reduce_fusion.1 = bf16[256,2560]{1,0:T(8,128)(2,1)S(1)} fusion(f32[256,8]{1,0:T(8,128)S(1)} %copy.55, s32[256,8]{1,0:T(8,128)S(1)} %copy-done.3), kind=kLoop, calls=%fused_computation.53 | loop fusion | flops 15073280 | bytes 1327104 | tf_op jit(solution)/shard_map/reduce_sum | solution.py:89
  67.5 104.1 %all-to-all-done.2 = bf16[64,40,1024]{2,1,0:T(8,128)(2,1)} async-done(((bf16[64,40,1024]{2,1,0:T(8,128)(2,1)}), bf16[64,40,1024]{2,1,0:T(8,128)(2,1)}, u32[]{:S(2)}, u32[]{:S(2)}) %all-to-all-start.2) | async-done | bytes 5242912 | tf_op jit(solution)/shard_map/all_to_all | solution.py:81
  171.6 6.1 %multiply_reduce_fusion = (f32[256]{0:T(256)S(1)}, f32[256,1024]{1,0:T(8,128)}) fusion(f32[1024]{0:T(1024)S(1)} %copy-done.13, f32[256,1024]{1,0:T(8,128)} %fusion.137, bf16[1024,1024]{1,0:T(8,128)(2,1)S(1)} %copy-done, f32[256,1024]{1,0:T(8,128)} %get-tuple-element.226, bf16[2560,1024]{1,0:T(8,128)(2,1)} %bitcast.16, ...), kind=kOutput, calls=%fused_computation.81 | convolution fusion | flops 1881145088 | bytes 11802624 | tf_op jit(solution)/shard_map/dot_general | solution.py:153
  177.8 1.3 multiply_convert_fusion
  179.2 1.6 tile.2
  180.8 4.6 %all-to-all-start.3 = ((bf16[4,256,1024]{2,1,0:T(8,128)(2,1)}), bf16[4,256,1024]{2,1,0:T(8,128)(2,1)}, u32[]{:S(2)}, u32[]{:S(2)}) async-start(bf16[4,256,1024]{2,1,0:T(8,128)(2,1)} %tile.2), calls=%async_computation.3 | async-start | bytes 4194304 | tf_op jit(solution)/shard_map/all_to_all | solution.py:173
  185.4 0.1 iota_compare_fusion.24
  185.4 0.2 fusion.60
  185.7 0.3 fusion.42
  186.0 25.5 %all-to-all-done.3 = bf16[4,256,1024]{2,1,0:T(8,128)(2,1)} async-done(((bf16[4,256,1024]{2,1,0:T(8,128)(2,1)}), bf16[4,256,1024]{2,1,0:T(8,128)(2,1)}, u32[]{:S(2)}, u32[]{:S(2)}) %all-to-all-start.3) | async-done | bytes 2097184 | tf_op jit(solution)/shard_map/all_to_all | solution.py:173
  211.6 2.4 %fusion.41 = f32[8,8,8,128]{3,1,2,0:T(8,128)S(1)} fusion(bf16[1024,1024]{1,0:T(8,128)(2,1)} %bitcast.18, f32[64]{0:T(128)S(1)} %broadcast_multiply_fusion.1, f32[64,1024]{1,0:T(8,128)S(1)} %fusion.60), kind=kOutput, calls=%fused_computation.73 | convolution fusion | flops 134545408 | bytes 2621696 | tf_op jit(solution)/shard_map/dot_general | solution.py:171
  214.0 0.1 reduce_sum.97
  214.2 0.7 select_reduce_fusion.2
  (54 shorter events, 0.5 us)
Async XLA Ops:
  0.6 171.0 %copy-start = (bf16[1024,1024]{1,0:T(8,128)(2,1)S(1)}, bf16[1024,1024]{1,0:T(8,128)(2,1)}, u32[]{:S(2)}) copy-start(bf16[1024,1024]{1,0:T(8,128)(2,1)} %param.20) | copy-start | bytes 6291460
  0.6 6.0 %copy-start.5 = (s32[256,8]{0,1:T(8,128)S(1)}, s32[256,8]{0,1:T(8,128)}, u32[]{:S(2)}) copy-start(s32[256,8]{0,1:T(8,128)} %param.22) | copy-start | bytes 24580
  0.7 22.5 %copy-start.9 = (s32[2]{0:T(128)S(1)}, s32[2]{0:T(128)}, u32[]{:S(2)}) copy-start(s32[2]{0:T(128)} %param.24) | copy-start | bytes 28
  0.7 25.0 %copy-start.8 = (s32[256,8]{0,1:T(8,128)S(1)}, s32[256,8]{0,1:T(8,128)}, u32[]{:S(2)}) copy-start(s32[256,8]{0,1:T(8,128)} %param.23) | copy-start | bytes 24580
  3.2 23.7 %collective-permute-start.1 = (bf16[256,1024]{1,0:T(8,128)(2,1)S(1)}, bf16[256,1024]{1,0:T(8,128)(2,1)S(1)}, u32[]{:S(2)}, u32[]{:S(2)}) collective-permute-start(bf16[256,1024]{1,0:T(8,128)(2,1)S(1)} %fusion.37), channel_id=1, source_target_pairs={{0,16},{1,17},{2,18},{3,19},{4,20},{5,21},{6,22},{7,23},{8,24},{9,... | collective-permute-start | bytes 1572872 | tf_op jit(solution)/shard_map/ppermute | solution.py:123
  5.3 29.3 %collective-permute-start = (bf16[256,1024]{1,0:T(8,128)(2,1)S(1)}, bf16[256,1024]{1,0:T(8,128)(2,1)}, u32[]{:S(2)}, u32[]{:S(2)}) collective-permute-start(bf16[256,1024]{1,0:T(8,128)(2,1)S(1)} %fusion.37), channel_id=1, source_target_pairs={{0,1},{1,0},{2,3},{3,2},{4,5},{5,4},{6,7},{7,6},{8,9},{9,8},{10,11... | collective-permute-start | bytes 1572872 | tf_op jit(solution)/shard_map/ppermute | solution.py:122
  12.1 20.3 %all-to-all-start.1 = ((s32[64,1,65]{2,1,0:T(1,128)}), s32[64,1,65]{2,1,0:T(1,128)S(1)}, u32[]{:S(2)}, u32[]{:S(2)}) async-start(s32[64,1,65]{2,1,0:T(1,128)} %bitcast.13), calls=%async_computation.1 | async-start | bytes 65536 | tf_op jit(solution)/shard_map/all_to_all | solution.py:118
  26.9 10.5 %copy-start.4 = (bf16[256,1024]{1,0:T(8,128)(2,1)}, bf16[256,1024]{1,0:T(8,128)(2,1)S(1)}, u32[]{:S(2)}) copy-start(bf16[256,1024]{1,0:T(8,128)(2,1)S(1)} %collective-permute-done.1) | copy-start | bytes 1572868
  26.9 7.8 %collective-permute-start.2 = (bf16[256,1024]{1,0:T(8,128)(2,1)S(1)}, bf16[256,1024]{1,0:T(8,128)(2,1)}, u32[]{:S(2)}, u32[]{:S(2)}) collective-permute-start(bf16[256,1024]{1,0:T(8,128)(2,1)S(1)} %collective-permute-done.1), channel_id=1, source_target_pairs={{0,1},{1,0},{2,3},{3,2},{4,5},{5,4},{6,7},{7,6},{8,9},{9,8},{10,11... | collective-permute-start | bytes 1572872 | tf_op jit(solution)/shard_map/ppermute | solution.py:124
  47.4 5.9 %copy-start.7 = (s32[16,128]{1,0:T(8,128)S(1)}, s32[16,128]{1,0:T(8,128)}, u32[]{:S(2)}) copy-start(s32[16,128]{1,0:T(8,128)} %get-tuple-element.201) | copy-start | bytes 24580
  47.4 6.1 %copy-start.6 = (s32[256,8]{0,1:T(8,128)S(1)}, s32[256,8]{0,1:T(8,128)}, u32[]{:S(2)}) copy-start(s32[256,8]{0,1:T(8,128)} %param.22) | copy-start | bytes 24580
  47.4 7.7 %copy-start.2 = (bf16[256,1024]{1,0:T(8,128)(2,1)S(1)}, bf16[256,1024]{1,0:T(8,128)(2,1)}, u32[]{:S(2)}) copy-start(bf16[256,1024]{1,0:T(8,128)(2,1)} %param.16) | copy-start | bytes 1572868
  47.4 124.2 %all-to-all-start.2 = ((bf16[64,40,1024]{2,1,0:T(8,128)(2,1)}), bf16[64,40,1024]{2,1,0:T(8,128)(2,1)}, u32[]{:S(2)}, u32[]{:S(2)}) async-start(bf16[64,40,1024]{2,1,0:T(8,128)(2,1)} %bitcast.62), calls=%async_computation.2 | async-start | bytes 10485760 | tf_op jit(solution)/shard_map/all_to_all | solution.py:81
  53.2 118.4 %copy-start.10 = (f32[256]{0:T(256)S(1)}, f32[256]{0:T(256)}, u32[]{:S(2)}) copy-start(f32[256]{0:T(256)} %get-tuple-element.191) | copy-start | bytes 3076
  53.2 118.4 %copy-start.13 = (f32[1024]{0:T(1024)S(1)}, f32[1024]{0:T(1024)}, u32[]{:S(2)}) copy-start(f32[1024]{0:T(1024)} %param.21) | copy-start | bytes 12292
  55.1 3.3 %copy-start.3 = (s32[256,8]{1,0:T(8,128)S(1)}, s32[256,8]{1,0:T(8,128)}, u32[]{:S(2)}) copy-start(s32[256,8]{1,0:T(8,128)} %copy.54) | copy-start | bytes 24580
  179.1 6.5 %copy-start.1 = (bf16[256,1024]{1,0:T(8,128)(2,1)}, bf16[256,1024]{1,0:T(8,128)(2,1)S(1)}, u32[]{:S(2)}) copy-start(bf16[256,1024]{1,0:T(8,128)(2,1)S(1)} %multiply_convert_fusion) | copy-start | bytes 1572868
  179.2 6.2 %copy-start.14 = (s32[1,4]{1,0:T(1,128)S(1)}, s32[1,4]{1,0:T(1,128)}, u32[]{:S(2)}) copy-start(s32[1,4]{1,0:T(1,128)} %param.27) | copy-start | bytes 52
  179.2 6.3 %copy-start.12 = (s32[64]{0:T(128)S(1)}, s32[64]{0:T(128)}, u32[]{:S(2)}) copy-start(s32[64]{0:T(128)} %param.25) | copy-start | bytes 772
  180.8 4.9 %copy-start.11 = (s32[64]{0:T(128)S(1)}, s32[64]{0:T(128)}, u32[]{:S(2)}) copy-start(s32[64]{0:T(128)} %param.26) | copy-start | bytes 772
  180.8 30.8 %all-to-all-start.3 = ((bf16[4,256,1024]{2,1,0:T(8,128)(2,1)}), bf16[4,256,1024]{2,1,0:T(8,128)(2,1)}, u32[]{:S(2)}, u32[]{:S(2)}) async-start(bf16[4,256,1024]{2,1,0:T(8,128)(2,1)} %tile.2), calls=%async_computation.3 | async-start | bytes 4194304 | tf_op jit(solution)/shard_map/all_to_all | solution.py:173

commit v9 on v7

--- a/solution.py
+++ b/solution.py
@@ -165,21 +165,27 @@
     positive_emb = jnp.dot(positive_pick, embedding, preferred_element_type=jnp.float32)
     positive_score = score_scale / hidden * jnp.sum(query_emb * positive_emb, axis=-1)
     neg_lists = neg_blocks[0]
+    regions = lax.axis_size("region")
+    here = lax.axis_index("region")
+    arrived = [embedding] + [
+        lax.ppermute(embedding, "region", [(r, (r + k) % regions) for r in range(regions)])
+        for k in range(1, regions)
+    ]
     scores = (
         score_scale
         / hidden
         * jnp.dot(
             query_emb.astype(jnp.bfloat16),
-            lax.all_gather(embedding, "region", axis=0, tiled=True).T,
+            jnp.concatenate(arrived, axis=0).T,
             preferred_element_type=jnp.float32,
         )
     )
     hinge_all = jnp.maximum(scores - positive_score[:, None] + margin_value, 0.0)
     block_mean = jnp.mean(hinge_all.reshape(query_emb.shape[0], -1, block_rows), axis=-1)
+    per_region = block_mean.shape[1] // regions
+    slot = ((here - neg_lists // per_region) % regions) * per_region + neg_lists % per_region
     pool_ids = jnp.arange(block_mean.shape[1], dtype=jnp.int32)
-    picked = jnp.where(
-        neg_lists[None, :, None] == pool_ids[None, None, :], block_mean[:, None, :], 0.0
-    )
+    picked = jnp.where(slot[None, :, None] == pool_ids[None, None, :], block_mean[:, None, :], 0.0)
     hinge_terms = jnp.sum(picked, axis=-1)
     return (embedding, hinge_terms)
 

time: 227 us -> 211 us (0.930)
  between operations: 15.7 us -> 2.25 us
  starting transfers between devices: 20.7 us -> 24.5 us
  matrix products: 27.1 us -> 23.6 us
    all_gather x1 -> x0, waiting for transfers between devices: 27.3 us -> none  [body(): lax.all_gather(embedding, 'region', axis=0, tiled=True)]
    ppermute x0 -> x3, waiting for transfers between devices: none -> 24.9 us  [body(): lax.ppermute(embedding, 'region', [(r, (r + k) % regions) for r in range(...]
    ppermute x0 -> x3, starting transfers between devices: none -> 3.85 us  [body(): lax.ppermute(embedding, 'region', [(r, (r + k) % regions) for r in range(...]
  transfers between devices with their start and end apart: 6 -> 8, of which waited for: 3 -> 4; matrix products, arithmetic and copies ran while one was open for 12% -> 12% of each run, Pallas kernels for 0% -> 0%
where the time goes in v9:
time: 211 us; the launch traced here: 210 us
  waiting for transfers between devices  134 us (64%)
  starting transfers between devices  24.5 us (12%)
  matrix products  23.6 us (11%)
  other arithmetic  22 us (10%)
  local copies, waits for them, and re-layouts  4.03 us (2%)
  between operations  2.25 us (1%)
    all_to_all x1, waiting for transfers between devices, serve(): lax.all_to_all(outgoing, 'shard', split_axis=0, concat_axis=0, tiled=True)  104 us
    ppermute x3, waiting for transfers between devices, body(): lax.ppermute(embedding, 'region', [(r, (r + k) % regions) for r in range(...  24.9 us
    all_to_all x1, starting transfers between devices, body(): lax.all_to_all(flagged, 'shard', split_axis=0, concat_axis=0, tiled=True)  11 us
    reduce_sum x1, other arithmetic, serve(): mix = jnp.sum(spread, axis=1).astype(jnp.bfloat16)  9.1 us
    dot_general x1, matrix products, serve(): jnp.dot(pick, table, preferred_element_type=jnp.float32)  8.88 us
    dot_general x1, matrix products, body(): jnp.dot(aggregate, nbr_weight, preferred_element_type=jnp.float32)  6.36 us
    all_to_all x1, starting transfers between devices, serve(): lax.all_to_all(outgoing, 'shard', split_axis=0, concat_axis=0, tiled=True)  5.86 us
    all_to_all x1, waiting for transfers between devices, body(): lax.all_to_all(flagged, 'shard', split_axis=0, concat_axis=0, tiled=True)  5.11 us
  transfers between devices with their start and end apart: 8, of which 4 were waited for; matrix products, arithmetic and copies ran while one was open for 12% of the time, Pallas kernels for 0%

profile of v9, /device:TPU:1, one launch (start us, length us, event | category | flops | bytes accessed | tf_op | source)
XLA Modules:
  0.0 210.5 jit_solution(16735679202700508671)
XLA Ops:
  0.7 2.5 %fusion.45 = bf16[256,1024]{1,0:T(8,128)(2,1)S(1)} fusion(bf16[256,1024]{1,0:T(8,128)(2,1)} %param.16, bf16[1024,1024]{1,0:T(8,128)(2,1)} %param.17, f32[1024]{0:T(1024)} %param.18), kind=kOutput, calls=%fused_computation.75 | convolution fusion | flops 537657344 | bytes 3149824 | tf_op jit(solution)/shard_map/dot_general | solution.py:50
  3.2 2.1 %collective-permute-start.1 = (bf16[256,1024]{1,0:T(8,128)(2,1)S(1)}, bf16[256,1024]{1,0:T(8,128)(2,1)S(1)}, u32[]{:S(2)}, u32[]{:S(2)}) collective-permute-start(bf16[256,1024]{1,0:T(8,128)(2,1)S(1)} %fusion.45), channel_id=1, source_target_pairs={{0,16},{1,17},{2,18},{3,19},{4,20},{5,21},{6,22},{7,23},{8,24},{9,... | collective-permute-start | bytes 1572872 | tf_op jit(solution)/shard_map/ppermute | solution.py:123
  5.3 1.3 collective-permute-start
  6.6 0.1 copy.49
  6.7 0.1 reshape.754
  6.8 0.1 reshape.755
  7.0 0.1 convert_reduce_fusion.1
  7.1 0.1 fusion.125
  7.2 0.2 fusion.64
  7.5 1.6 select_convert_fusion.2
  9.2 0.9 convolution_convert_fusion
  10.1 0.1 convert_reduce_fusion
  10.3 0.6 reduce_max.18
  11.5 0.6 concatenate.18
  12.1 11.0 %all-to-all-start.1 = ((s32[64,1,65]{2,1,0:T(1,128)}), s32[64,1,65]{2,1,0:T(1,128)S(1)}, u32[]{:S(2)}, u32[]{:S(2)}) async-start(s32[64,1,65]{2,1,0:T(1,128)} %bitcast.13), calls=%async_computation.1 | async-start | bytes 65536 | tf_op jit(solution)/shard_map/all_to_all | solution.py:118
  23.2 0.6 fusion.158
  23.8 1.3 compare_select_fusion.1
  25.1 0.6 fusion.157
  25.7 1.2 convert_reduce_fusion.2
  26.9 0.5 collective-permute-start.2
  27.3 5.1 %all-to-all-done.1 = s32[64,1,65]{2,1,0:T(1,128)S(1)} async-done(((s32[64,1,65]{2,1,0:T(1,128)}), s32[64,1,65]{2,1,0:T(1,128)S(1)}, u32[]{:S(2)}, u32[]{:S(2)}) %all-to-all-start.1) | async-done | bytes 16672 | tf_op jit(solution)/shard_map/all_to_all | solution.py:118
  32.4 0.8 slice_reduce_fusion
  33.8 0.1 reshape.756
  33.9 0.6 fusion.84
  34.6 2.7 %pad_maximum_fusion = bf16[1024,1024]{1,0:T(8,128)(2,1)} fusion(bf16[256,1024]{1,0:T(8,128)(2,1)} %collective-permute-done.2, bf16[256,1024]{1,0:T(8,128)(2,1)S(1)} %collective-permute-done.1, bf16[256,1024]{1,0:T(8,128)(2,1)} %collective-permute-done, bf16[256,1024]{1,0:T(8,128)(2,1)S(1)} %fusion.45), kind=kLoop, calls=%fused_computation.59 | loop fusion | flops 8388608 | bytes 4194304 | tf_op jit(solution)/shard_map/concatenate | solution.py:125
  37.3 1.2 conditional.1
  37.3 1.1 broadcast.1114
  38.4 8.9 %fusion.30 = bf16[2560,1024]{1,0:T(8,128)(2,1)} fusion(s32[2560]{0:T(1024)} %fusion.84, bf16[256,1024]{1,0:T(8,128)(2,1)} %collective-permute-done.2, bf16[256,1024]{1,0:T(8,128)(2,1)} %copy-done.4, bf16[256,1024]{1,0:T(8,128)(2,1)} %collective-permute-done, bf16[256,1024]{1,0:T(8,128)(2,1)S(1)} %fusion.45), kind=kOutput, calls=%fused_computation.57 | convolution fusion | flops 5382340608 | bytes 7350272 | tf_op jit(solution)/shard_map/dot_general | solution.py:79
  47.3 5.9 %all-to-all-start.2 = ((bf16[64,40,1024]{2,1,0:T(8,128)(2,1)}), bf16[64,40,1024]{2,1,0:T(8,128)(2,1)}, u32[]{:S(2)}, u32[]{:S(2)}) async-start(bf16[64,40,1024]{2,1,0:T(8,128)(2,1)} %bitcast.72), calls=%async_computation.2 | async-start | bytes 10485760 | tf_op jit(solution)/shard_map/all_to_all | solution.py:81
  53.2 0.1 convert_element_type.100
  53.4 0.8 fusion.96
  54.2 0.1 copy.55
  54.3 0.8 copy.54
  55.2 3.3 %fusion.160 = f32[256,1024]{1,0:T(8,128)} fusion(bf16[256,1024]{1,0:T(8,128)(2,1)S(1)} %copy-done.2, bf16[1024,1024]{1,0:T(8,128)(2,1)} %param.19), kind=kOutput, calls=%fused_computation.316 | convolution fusion | flops 536870912 | bytes 3670016 | tf_op jit(solution)/shard_map/dot_general | solution.py:152
  58.5 9.1 %select_reduce_fusion.1 = bf16[256,2560]{1,0:T(8,128)(2,1)S(1)} fusion(f32[256,8]{1,0:T(8,128)S(1)} %copy.55, s32[256,8]{1,0:T(8,128)S(1)} %copy-done.3), kind=kLoop, calls=%fused_computation.53 | loop fusion | flops 15073280 | bytes 1327104 | tf_op jit(solution)/shard_map/reduce_sum | solution.py:89
  67.6 104.0 %all-to-all-done.2 = bf16[64,40,1024]{2,1,0:T(8,128)(2,1)} async-done(((bf16[64,40,1024]{2,1,0:T(8,128)(2,1)}), bf16[64,40,1024]{2,1,0:T(8,128)(2,1)}, u32[]{:S(2)}, u32[]{:S(2)}) %all-to-all-start.2) | async-done | bytes 5242912 | tf_op jit(solution)/shard_map/all_to_all | solution.py:81
  171.6 6.4 %multiply_reduce_fusion = (f32[256]{0:T(256)S(1)}, f32[256,1024]{1,0:T(8,128)}) fusion(f32[1024]{0:T(1024)S(1)} %copy-done.13, f32[256,1024]{1,0:T(8,128)} %fusion.160, bf16[1024,1024]{1,0:T(8,128)(2,1)S(1)} %copy-done, f32[256,1024]{1,0:T(8,128)} %get-tuple-element.226, bf16[2560,1024]{1,0:T(8,128)(2,1)} %bitcast.16, ...), kind=kOutput, calls=%fused_computation.89 | convolution fusion | flops 1881145088 | bytes 11802624 | tf_op jit(solution)/shard_map/dot_general | solution.py:153
  178.0 1.3 multiply_convert_fusion
  179.4 2.8 %collective-permute-start.5 = (bf16[256,1024]{1,0:T(8,128)(2,1)S(1)}, bf16[256,1024]{1,0:T(8,128)(2,1)S(1)}, u32[]{:S(2)}, u32[]{:S(2)}) collective-permute-start(bf16[256,1024]{1,0:T(8,128)(2,1)S(1)} %multiply_convert_fusion), channel_id=1, source_target_pairs={{0,192},{64,0},{128,64},{192,128},{1,193},{65,1},{129,65},{193,129... | collective-permute-start | bytes 1572872 | tf_op jit(solution)/shard_map/ppermute | solution.py:171
  182.2 0.3 collective-permute-start.4
  182.5 0.7 collective-permute-start.3
  183.2 0.2 fusion.79
  183.5 0.3 fusion.61
  183.8 20.5 %collective-permute-done.5 = bf16[256,1024]{1,0:T(8,128)(2,1)S(1)} collective-permute-done((bf16[256,1024]{1,0:T(8,128)(2,1)S(1)}, bf16[256,1024]{1,0:T(8,128)(2,1)S(1)}, u32[]{:S(2)}, u32[]{:S(2)}) %collective-permute-start.5) | collective-permute-done | bytes 524320 | tf_op jit(solution)/shard_map/ppermute | solution.py:171
  204.3 4.4 %collective-permute-done.3 = bf16[256,1024]{1,0:T(8,128)(2,1)S(1)} collective-permute-done((bf16[256,1024]{1,0:T(8,128)(2,1)S(1)}, bf16[256,1024]{1,0:T(8,128)(2,1)S(1)}, u32[]{:S(2)}, u32[]{:S(2)}) %collective-permute-start.3) | collective-permute-done | bytes 524320 | tf_op jit(solution)/shard_map/ppermute | solution.py:171
  208.8 0.8 fusion.58
  209.6 0.1 reduce_sum.97
  209.8 0.7 select_reduce_fusion.2
  (58 shorter events, 0.6 us)
Async XLA Ops:
  0.6 171.0 %copy-start = (bf16[1024,1024]{1,0:T(8,128)(2,1)S(1)}, bf16[1024,1024]{1,0:T(8,128)(2,1)}, u32[]{:S(2)}) copy-start(bf16[1024,1024]{1,0:T(8,128)(2,1)} %param.20) | copy-start | bytes 6291460
  0.6 6.0 %copy-start.5 = (s32[256,8]{0,1:T(8,128)S(1)}, s32[256,8]{0,1:T(8,128)}, u32[]{:S(2)}) copy-start(s32[256,8]{0,1:T(8,128)} %param.22) | copy-start | bytes 24580
  0.7 22.5 %copy-start.9 = (s32[2]{0:T(128)S(1)}, s32[2]{0:T(128)}, u32[]{:S(2)}) copy-start(s32[2]{0:T(128)} %param.24) | copy-start | bytes 28
  0.7 25.0 %copy-start.8 = (s32[256,8]{0,1:T(8,128)S(1)}, s32[256,8]{0,1:T(8,128)}, u32[]{:S(2)}) copy-start(s32[256,8]{0,1:T(8,128)} %param.23) | copy-start | bytes 24580
  3.2 23.7 %collective-permute-start.1 = (bf16[256,1024]{1,0:T(8,128)(2,1)S(1)}, bf16[256,1024]{1,0:T(8,128)(2,1)S(1)}, u32[]{:S(2)}, u32[]{:S(2)}) collective-permute-start(bf16[256,1024]{1,0:T(8,128)(2,1)S(1)} %fusion.45), channel_id=1, source_target_pairs={{0,16},{1,17},{2,18},{3,19},{4,20},{5,21},{6,22},{7,23},{8,24},{9,... | collective-permute-start | bytes 1572872 | tf_op jit(solution)/shard_map/ppermute | solution.py:123
  5.3 29.2 %collective-permute-start = (bf16[256,1024]{1,0:T(8,128)(2,1)S(1)}, bf16[256,1024]{1,0:T(8,128)(2,1)}, u32[]{:S(2)}, u32[]{:S(2)}) collective-permute-start(bf16[256,1024]{1,0:T(8,128)(2,1)S(1)} %fusion.45), channel_id=1, source_target_pairs={{0,1},{1,0},{2,3},{3,2},{4,5},{5,4},{6,7},{7,6},{8,9},{9,8},{10,11... | collective-permute-start | bytes 1572872 | tf_op jit(solution)/shard_map/ppermute | solution.py:122
  12.1 20.3 %all-to-all-start.1 = ((s32[64,1,65]{2,1,0:T(1,128)}), s32[64,1,65]{2,1,0:T(1,128)S(1)}, u32[]{:S(2)}, u32[]{:S(2)}) async-start(s32[64,1,65]{2,1,0:T(1,128)} %bitcast.13), calls=%async_computation.1 | async-start | bytes 65536 | tf_op jit(solution)/shard_map/all_to_all | solution.py:118
  26.9 10.4 %copy-start.4 = (bf16[256,1024]{1,0:T(8,128)(2,1)}, bf16[256,1024]{1,0:T(8,128)(2,1)S(1)}, u32[]{:S(2)}) copy-start(bf16[256,1024]{1,0:T(8,128)(2,1)S(1)} %collective-permute-done.1) | copy-start | bytes 1572868
  26.9 7.7 %collective-permute-start.2 = (bf16[256,1024]{1,0:T(8,128)(2,1)S(1)}, bf16[256,1024]{1,0:T(8,128)(2,1)}, u32[]{:S(2)}, u32[]{:S(2)}) collective-permute-start(bf16[256,1024]{1,0:T(8,128)(2,1)S(1)} %collective-permute-done.1), channel_id=1, source_target_pairs={{0,1},{1,0},{2,3},{3,2},{4,5},{5,4},{6,7},{7,6},{8,9},{9,8},{10,11... | collective-permute-start | bytes 1572872 | tf_op jit(solution)/shard_map/ppermute | solution.py:124
  47.3 5.9 %copy-start.7 = (s32[16,128]{1,0:T(8,128)S(1)}, s32[16,128]{1,0:T(8,128)}, u32[]{:S(2)}) copy-start(s32[16,128]{1,0:T(8,128)} %get-tuple-element.201) | copy-start | bytes 24580
  47.3 6.1 %copy-start.6 = (s32[256,8]{0,1:T(8,128)S(1)}, s32[256,8]{0,1:T(8,128)}, u32[]{:S(2)}) copy-start(s32[256,8]{0,1:T(8,128)} %param.22) | copy-start | bytes 24580
  47.3 7.8 %copy-start.14 = (s32[1,4]{1,0:T(1,128)S(1)}, s32[1,4]{1,0:T(1,128)}, u32[]{:S(2)}) copy-start(s32[1,4]{1,0:T(1,128)} %param.27) | copy-start | bytes 52
  47.3 7.9 %copy-start.2 = (bf16[256,1024]{1,0:T(8,128)(2,1)S(1)}, bf16[256,1024]{1,0:T(8,128)(2,1)}, u32[]{:S(2)}) copy-start(bf16[256,1024]{1,0:T(8,128)(2,1)} %param.16) | copy-start | bytes 1572868
  47.3 124.3 %all-to-all-start.2 = ((bf16[64,40,1024]{2,1,0:T(8,128)(2,1)}), bf16[64,40,1024]{2,1,0:T(8,128)(2,1)}, u32[]{:S(2)}, u32[]{:S(2)}) async-start(bf16[64,40,1024]{2,1,0:T(8,128)(2,1)} %bitcast.72), calls=%async_computation.2 | async-start | bytes 10485760 | tf_op jit(solution)/shard_map/all_to_all | solution.py:81
  53.2 118.4 %copy-start.10 = (f32[256]{0:T(256)S(1)}, f32[256]{0:T(256)}, u32[]{:S(2)}) copy-start(f32[256]{0:T(256)} %get-tuple-element.191) | copy-start | bytes 3076
  53.2 118.4 %copy-start.13 = (f32[1024]{0:T(1024)S(1)}, f32[1024]{0:T(1024)}, u32[]{:S(2)}) copy-start(f32[1024]{0:T(1024)} %param.21) | copy-start | bytes 12292
  55.1 3.4 %copy-start.3 = (s32[256,8]{1,0:T(8,128)S(1)}, s32[256,8]{1,0:T(8,128)}, u32[]{:S(2)}) copy-start(s32[256,8]{1,0:T(8,128)} %copy.54) | copy-start | bytes 24580
  171.6 11.6 %copy-start.12 = (s32[64]{0:T(128)S(1)}, s32[64]{0:T(128)}, u32[]{:S(2)}) copy-start(s32[64]{0:T(128)} %param.25) | copy-start | bytes 772
  171.6 11.9 %copy-start.11 = (s32[64]{0:T(128)S(1)}, s32[64]{0:T(128)}, u32[]{:S(2)}) copy-start(s32[64]{0:T(128)} %param.26) | copy-start | bytes 772
  179.4 30.2 %copy-start.1 = (bf16[256,1024]{1,0:T(8,128)(2,1)}, bf16[256,1024]{1,0:T(8,128)(2,1)S(1)}, u32[]{:S(2)}) copy-start(bf16[256,1024]{1,0:T(8,128)(2,1)S(1)} %multiply_convert_fusion) | copy-start | bytes 1572868
  179.4 25.0 %collective-permute-start.5 = (bf16[256,1024]{1,0:T(8,128)(2,1)S(1)}, bf16[256,1024]{1,0:T(8,128)(2,1)S(1)}, u32[]{:S(2)}, u32[]{:S(2)}) collective-permute-start(bf16[256,1024]{1,0:T(8,128)(2,1)S(1)} %multiply_convert_fusion), channel_id=1, source_target_pairs={{0,192},{64,0},{128,64},{192,128},{1,193},{65,1},{129,65},{193,129... | collective-permute-start | bytes 1572872 | tf_op jit(solution)/shard_map/ppermute | solution.py:171
  182.2 22.2 %collective-permute-start.4 = (bf16[256,1024]{1,0:T(8,128)(2,1)S(1)}, bf16[256,1024]{1,0:T(8,128)(2,1)S(1)}, u32[]{:S(2)}, u32[]{:S(2)}) collective-permute-start(bf16[256,1024]{1,0:T(8,128)(2,1)S(1)} %multiply_convert_fusion), channel_id=1, source_target_pairs={{0,128},{64,192},{128,0},{192,64},{1,129},{65,193},{129,1},{193,65... | collective-permute-start | bytes 1572872 | tf_op jit(solution)/shard_map/ppermute | solution.py:171
  182.5 26.2 %collective-permute-start.3 = (bf16[256,1024]{1,0:T(8,128)(2,1)S(1)}, bf16[256,1024]{1,0:T(8,128)(2,1)S(1)}, u32[]{:S(2)}, u32[]{:S(2)}) collective-permute-start(bf16[256,1024]{1,0:T(8,128)(2,1)S(1)} %multiply_convert_fusion), channel_id=1, source_target_pairs={{0,64},{64,128},{128,192},{192,0},{1,65},{65,129},{129,193},{193,1... | collective-permute-start | bytes 1572872 | tf_op jit(solution)/shard_map/ppermute | solution.py:171

commit v10 on v9

--- a/solution.py
+++ b/solution.py
@@ -167,9 +167,19 @@
     neg_lists = neg_blocks[0]
     regions = lax.axis_size("region")
     here = lax.axis_index("region")
-    arrived = [embedding] + [
-        lax.ppermute(embedding, "region", [(r, (r + k) % regions) for r in range(regions)])
-        for k in range(1, regions)
+    def shift(x, k):
+        return lax.ppermute(x, "region", [(r, (r + k) % regions) for r in range(regions)])
+
+    split = item_dev // 2
+    from_left = shift(embedding, 1)
+    from_right = shift(jnp.concatenate([embedding, embedding[split:]], axis=0), -1)
+    relayed = shift(from_right[item_dev:], -1)
+    direct = shift(embedding[:split], 2)
+    arrived = [
+        embedding,
+        from_left,
+        jnp.concatenate([direct, relayed], axis=0),
+        from_right[:item_dev],
     ]
     scores = (
         score_scale

time: 211 us -> 216 us (1.024)
  starting transfers between devices: 24.5 us -> 28.8 us
    ppermute x3 -> x4, starting transfers between devices: 3.85 us -> 8.09 us  [shift(): lax.ppermute(x, 'region', [(r, (r + k) % regions) for r in range(regions)])]
    ppermute x3 -> x4, waiting for transfers between devices: 24.9 us -> 24.3 us  [shift(): lax.ppermute(x, 'region', [(r, (r + k) % regions) for r in range(regions)])]
  transfers between devices with their start and end apart: 8 -> 9, of which waited for: 4 -> 4; matrix products, arithmetic and copies ran while one was open for 12% -> 11% of each run, Pallas kernels for 0% -> 0%
where the time goes in v10:
time: 216 us; the launch traced here: 214 us
  waiting for transfers between devices  135 us (62%)
  starting transfers between devices  28.8 us (13%)
  matrix products  23.4 us (11%)
  other arithmetic  20.7 us (10%)
  local copies, waits for them, and re-layouts  4.21 us (2%)
  between operations  2.32 us (1%)
    all_to_all x1, waiting for transfers between devices, serve(): lax.all_to_all(outgoing, 'shard', split_axis=0, concat_axis=0, tiled=True)  105 us
    ppermute x4, waiting for transfers between devices, shift(): lax.ppermute(x, 'region', [(r, (r + k) % regions) for r in range(regions)])  24.3 us
    all_to_all x1, starting transfers between devices, body(): lax.all_to_all(flagged, 'shard', split_axis=0, concat_axis=0, tiled=True)  11 us
    reduce_sum x1, other arithmetic, serve(): mix = jnp.sum(spread, axis=1).astype(jnp.bfloat16)  9.1 us
    dot_general x1, matrix products, serve(): jnp.dot(pick, table, preferred_element_type=jnp.float32)  8.89 us
    ppermute x4, starting transfers between devices, shift(): lax.ppermute(x, 'region', [(r, (r + k) % regions) for r in range(regions)])  8.09 us
    dot_general x1, matrix products, body(): jnp.dot(aggregate, nbr_weight, preferred_element_type=jnp.float32)  6.14 us
    all_to_all x1, starting transfers between devices, serve(): lax.all_to_all(outgoing, 'shard', split_axis=0, concat_axis=0, tiled=True)  5.87 us
  transfers between devices with their start and end apart: 9, of which 4 were waited for; matrix products, arithmetic and copies ran while one was open for 11% of the time, Pallas kernels for 0%

profile of v10, /device:TPU:1, one launch (start us, length us, event | category | flops | bytes accessed | tf_op | source)
XLA Modules:
  0.0 214.3 jit_solution(18290732651780568897)
XLA Ops:
  0.7 2.5 %fusion.37 = bf16[256,1024]{1,0:T(8,128)(2,1)S(1)} fusion(bf16[256,1024]{1,0:T(8,128)(2,1)} %param.16, bf16[1024,1024]{1,0:T(8,128)(2,1)} %param.17, f32[1024]{0:T(1024)} %param.18), kind=kOutput, calls=%fused_computation.67 | convolution fusion | flops 537657344 | bytes 3149824 | tf_op jit(solution)/shard_map/dot_general | solution.py:50
  3.2 2.1 collective-permute-start.1
  5.3 1.3 collective-permute-start
  6.6 0.1 copy.49
  6.7 0.1 reshape.754
  6.9 0.1 reshape.755
  7.0 0.1 convert_reduce_fusion.1
  7.1 0.1 fusion.106
  7.2 0.2 fusion.45
  7.6 1.6 select_convert_fusion.2
  9.2 0.9 convolution_convert_fusion
  10.2 0.1 convert_reduce_fusion
  10.3 0.6 reduce_max.18
  11.5 0.6 concatenate.21
  12.2 11.0 %all-to-all-start.1 = ((s32[64,1,65]{2,1,0:T(1,128)}), s32[64,1,65]{2,1,0:T(1,128)S(1)}, u32[]{:S(2)}, u32[]{:S(2)}) async-start(s32[64,1,65]{2,1,0:T(1,128)} %bitcast.13), calls=%async_computation.1 | async-start | bytes 65536 | tf_op jit(solution)/shard_map/all_to_all | solution.py:118
  23.2 0.6 fusion.139
  23.8 1.3 compare_select_fusion.1
  25.1 0.6 fusion.138
  25.7 0.6 convert_reduce_fusion.2
  26.3 0.5 collective-permute-start.2
  26.8 5.7 %all-to-all-done.1 = s32[64,1,65]{2,1,0:T(1,128)S(1)} async-done(((s32[64,1,65]{2,1,0:T(1,128)}), s32[64,1,65]{2,1,0:T(1,128)S(1)}, u32[]{:S(2)}, u32[]{:S(2)}) %all-to-all-start.1) | async-done | bytes 16672 | tf_op jit(solution)/shard_map/all_to_all | solution.py:118
  32.5 0.7 slice_reduce_fusion
  33.9 0.1 reshape.756
  33.9 0.6 fusion.65
  34.6 2.7 %pad_maximum_fusion = bf16[1024,1024]{1,0:T(8,128)(2,1)} fusion(bf16[256,1024]{1,0:T(8,128)(2,1)} %collective-permute-done.2, bf16[256,1024]{1,0:T(8,128)(2,1)S(1)} %collective-permute-done.1, bf16[256,1024]{1,0:T(8,128)(2,1)} %collective-permute-done, bf16[256,1024]{1,0:T(8,128)(2,1)S(1)} %fusion.37), kind=kLoop, calls=%fused_computation.59 | loop fusion | flops 8388608 | bytes 4194304 | tf_op jit(solution)/shard_map/concatenate | solution.py:125
  37.3 1.2 conditional.1
  37.3 1.1 broadcast.1114
  38.5 8.9 %fusion.30 = bf16[2560,1024]{1,0:T(8,128)(2,1)} fusion(s32[2560]{0:T(1024)} %fusion.65, bf16[256,1024]{1,0:T(8,128)(2,1)} %collective-permute-done.2, bf16[256,1024]{1,0:T(8,128)(2,1)} %copy-done.4, bf16[256,1024]{1,0:T(8,128)(2,1)} %collective-permute-done, bf16[256,1024]{1,0:T(8,128)(2,1)S(1)} %fusion.37), kind=kOutput, calls=%fused_computation.57 | convolution fusion | flops 5382340608 | bytes 7350272 | tf_op jit(solution)/shard_map/dot_general | solution.py:79
  47.4 5.9 %all-to-all-start.2 = ((bf16[64,40,1024]{2,1,0:T(8,128)(2,1)}), bf16[64,40,1024]{2,1,0:T(8,128)(2,1)}, u32[]{:S(2)}, u32[]{:S(2)}) async-start(bf16[64,40,1024]{2,1,0:T(8,128)(2,1)} %bitcast.73), calls=%async_computation.2 | async-start | bytes 10485760 | tf_op jit(solution)/shard_map/all_to_all | solution.py:81
  53.2 0.1 convert_element_type.100
  53.5 0.1 copy.55
  53.6 0.8 copy.54
  54.4 3.3 %fusion.141 = f32[256,1024]{1,0:T(8,128)} fusion(bf16[256,1024]{1,0:T(8,128)(2,1)S(1)} %copy-done.2, bf16[1024,1024]{1,0:T(8,128)(2,1)} %param.19), kind=kOutput, calls=%fused_computation.314 | convolution fusion | flops 536870912 | bytes 3670016 | tf_op jit(solution)/shard_map/dot_general | solution.py:152
  57.7 9.1 %select_reduce_fusion.1 = bf16[256,2560]{1,0:T(8,128)(2,1)S(1)} fusion(f32[256,8]{1,0:T(8,128)S(1)} %copy.55, s32[256,8]{1,0:T(8,128)S(1)} %copy-done.3), kind=kLoop, calls=%fused_computation.53 | loop fusion | flops 15073280 | bytes 1327104 | tf_op jit(solution)/shard_map/reduce_sum | solution.py:89
  66.8 104.8 %all-to-all-done.2 = bf16[64,40,1024]{2,1,0:T(8,128)(2,1)} async-done(((bf16[64,40,1024]{2,1,0:T(8,128)(2,1)}), bf16[64,40,1024]{2,1,0:T(8,128)(2,1)}, u32[]{:S(2)}, u32[]{:S(2)}) %all-to-all-start.2) | async-done | bytes 5242912 | tf_op jit(solution)/shard_map/all_to_all | solution.py:81
  171.6 6.1 %multiply_reduce_fusion = (f32[256]{0:T(256)S(1)}, f32[256,1024]{1,0:T(8,128)}) fusion(f32[1024]{0:T(1024)S(1)} %copy-done.15, f32[256,1024]{1,0:T(8,128)} %fusion.141, bf16[1024,1024]{1,0:T(8,128)(2,1)S(1)} %copy-done, f32[256,1024]{1,0:T(8,128)} %get-tuple-element.230, bf16[2560,1024]{1,0:T(8,128)(2,1)} %bitcast.16, ...), kind=kOutput, calls=%fused_computation.81 | convolution fusion | flops 1881145088 | bytes 11802624 | tf_op jit(solution)/shard_map/dot_general | solution.py:153
  177.8 1.4 constant_dynamic-update-slice_fusion.3
  179.3 2.8 %collective-permute-start.5 = (bf16[384,1024]{1,0:T(8,128)(2,1)S(1)}, bf16[384,1024]{1,0:T(8,128)(2,1)S(1)}, u32[]{:S(2)}, u32[]{:S(2)}) collective-permute-start(bf16[384,1024]{1,0:T(8,128)(2,1)S(1)} %pad_maximum_fusion.1), channel_id=1, source_target_pairs={{0,192},{64,0},{128,64},{192,128},{1,193},{65,1},{129,65},{193,129... | collective-permute-start | bytes 2359304 | tf_op jit(solution)/shard_map/ppermute | solution.py:171
  182.2 0.1 iota_compare_fusion.24
  182.3 1.6 collective-permute-start.4
  183.9 0.2 fusion.60
  184.2 0.3 fusion.42
  184.5 19.8 %collective-permute-done.5 = bf16[384,1024]{1,0:T(8,128)(2,1)S(1)} collective-permute-done((bf16[384,1024]{1,0:T(8,128)(2,1)S(1)}, bf16[384,1024]{1,0:T(8,128)(2,1)S(1)}, u32[]{:S(2)}, u32[]{:S(2)}) %collective-permute-start.5) | collective-permute-done | bytes 786464 | tf_op jit(solution)/shard_map/ppermute | solution.py:171
  204.3 3.6 %collective-permute-start.6 = (bf16[128,1024]{1,0:T(8,128)(2,1)S(1)}, bf16[128,1024]{1,0:T(8,128)(2,1)S(1)}, u32[]{:S(2)}, u32[]{:S(2)}) collective-permute-start(bf16[128,1024]{1,0:T(8,128)(2,1)S(1)} %slice.60), channel_id=1, source_target_pairs={{0,192},{64,0},{128,64},{192,128},{1,193},{65,1},{129,65},{193,129... | collective-permute-start | bytes 786440 | tf_op jit(solution)/shard_map/ppermute | solution.py:171
  208.0 4.5 %collective-permute-done.6 = bf16[128,1024]{1,0:T(8,128)(2,1)S(1)} collective-permute-done((bf16[128,1024]{1,0:T(8,128)(2,1)S(1)}, bf16[128,1024]{1,0:T(8,128)(2,1)S(1)}, u32[]{:S(2)}, u32[]{:S(2)}) %collective-permute-start.6) | collective-permute-done | bytes 262176 | tf_op jit(solution)/shard_map/ppermute | solution.py:171
  212.6 0.8 fusion.41
  213.4 0.1 reduce_sum.97
  213.6 0.7 select_reduce_fusion.2
  (71 shorter events, 0.8 us)
Async XLA Ops:
  0.6 171.0 %copy-start = (bf16[1024,1024]{1,0:T(8,128)(2,1)S(1)}, bf16[1024,1024]{1,0:T(8,128)(2,1)}, u32[]{:S(2)}) copy-start(bf16[1024,1024]{1,0:T(8,128)(2,1)} %param.20) | copy-start | bytes 6291460
  0.6 6.0 %copy-start.7 = (s32[256,8]{0,1:T(8,128)S(1)}, s32[256,8]{0,1:T(8,128)}, u32[]{:S(2)}) copy-start(s32[256,8]{0,1:T(8,128)} %param.22) | copy-start | bytes 24580
  3.2 20.0 %copy-start.11 = (s32[2]{0:T(128)S(1)}, s32[2]{0:T(128)}, u32[]{:S(2)}) copy-start(s32[2]{0:T(128)} %param.24) | copy-start | bytes 28
  3.2 22.5 %copy-start.10 = (s32[256,8]{0,1:T(8,128)S(1)}, s32[256,8]{0,1:T(8,128)}, u32[]{:S(2)}) copy-start(s32[256,8]{0,1:T(8,128)} %param.23) | copy-start | bytes 24580
  3.2 23.1 %collective-permute-start.1 = (bf16[256,1024]{1,0:T(8,128)(2,1)S(1)}, bf16[256,1024]{1,0:T(8,128)(2,1)S(1)}, u32[]{:S(2)}, u32[]{:S(2)}) collective-permute-start(bf16[256,1024]{1,0:T(8,128)(2,1)S(1)} %fusion.37), channel_id=1, source_target_pairs={{0,16},{1,17},{2,18},{3,19},{4,20},{5,21},{6,22},{7,23},{8,24},{9,... | collective-permute-start | bytes 1572872 | tf_op jit(solution)/shard_map/ppermute | solution.py:123
  5.3 29.2 %collective-permute-start = (bf16[256,1024]{1,0:T(8,128)(2,1)S(1)}, bf16[256,1024]{1,0:T(8,128)(2,1)}, u32[]{:S(2)}, u32[]{:S(2)}) collective-permute-start(bf16[256,1024]{1,0:T(8,128)(2,1)S(1)} %fusion.37), channel_id=1, source_target_pairs={{0,1},{1,0},{2,3},{3,2},{4,5},{5,4},{6,7},{7,6},{8,9},{9,8},{10,11... | collective-permute-start | bytes 1572872 | tf_op jit(solution)/shard_map/ppermute | solution.py:122
  12.2 20.3 %all-to-all-start.1 = ((s32[64,1,65]{2,1,0:T(1,128)}), s32[64,1,65]{2,1,0:T(1,128)S(1)}, u32[]{:S(2)}, u32[]{:S(2)}) async-start(s32[64,1,65]{2,1,0:T(1,128)} %bitcast.13), calls=%async_computation.1 | async-start | bytes 65536 | tf_op jit(solution)/shard_map/all_to_all | solution.py:118
  26.3 11.0 %copy-start.5 = (s32[256,8]{0,1:T(8,128)}, s32[256,8]{0,1:T(8,128)S(1)}, u32[]{:S(2)}) copy-start(s32[256,8]{0,1:T(8,128)S(1)} %get-tuple-element.194) | copy-start | bytes 24580
  26.3 10.9 %copy-start.4 = (bf16[256,1024]{1,0:T(8,128)(2,1)}, bf16[256,1024]{1,0:T(8,128)(2,1)S(1)}, u32[]{:S(2)}) copy-start(bf16[256,1024]{1,0:T(8,128)(2,1)S(1)} %collective-permute-done.1) | copy-start | bytes 1572868
  26.3 8.2 %collective-permute-start.2 = (bf16[256,1024]{1,0:T(8,128)(2,1)S(1)}, bf16[256,1024]{1,0:T(8,128)(2,1)}, u32[]{:S(2)}, u32[]{:S(2)}) collective-permute-start(bf16[256,1024]{1,0:T(8,128)(2,1)S(1)} %collective-permute-done.1), channel_id=1, source_target_pairs={{0,1},{1,0},{2,3},{3,2},{4,5},{5,4},{6,7},{7,6},{8,9},{9,8},{10,11... | collective-permute-start | bytes 1572872 | tf_op jit(solution)/shard_map/ppermute | solution.py:124
  47.3 5.9 %copy-start.9 = (s32[16,128]{1,0:T(8,128)S(1)}, s32[16,128]{1,0:T(8,128)}, u32[]{:S(2)}) copy-start(s32[16,128]{1,0:T(8,128)} %get-tuple-element.205) | copy-start | bytes 24580
  47.3 6.1 %copy-start.6 = (s32[256,8]{0,1:T(8,128)S(1)}, s32[256,8]{0,1:T(8,128)}, u32[]{:S(2)}) copy-start(s32[256,8]{0,1:T(8,128)} %copy-done.5) | copy-start | bytes 24580
  47.3 6.1 %copy-start.8 = (s32[256,8]{0,1:T(8,128)S(1)}, s32[256,8]{0,1:T(8,128)}, u32[]{:S(2)}) copy-start(s32[256,8]{0,1:T(8,128)} %param.22) | copy-start | bytes 24580
  47.4 7.0 %copy-start.2 = (bf16[256,1024]{1,0:T(8,128)(2,1)S(1)}, bf16[256,1024]{1,0:T(8,128)(2,1)}, u32[]{:S(2)}) copy-start(bf16[256,1024]{1,0:T(8,128)(2,1)} %param.16) | copy-start | bytes 1572868
  47.4 124.3 %all-to-all-start.2 = ((bf16[64,40,1024]{2,1,0:T(8,128)(2,1)}), bf16[64,40,1024]{2,1,0:T(8,128)(2,1)}, u32[]{:S(2)}, u32[]{:S(2)}) async-start(bf16[64,40,1024]{2,1,0:T(8,128)(2,1)} %bitcast.73), calls=%async_computation.2 | async-start | bytes 10485760 | tf_op jit(solution)/shard_map/all_to_all | solution.py:81
  54.4 3.3 %copy-start.3 = (s32[256,8]{1,0:T(8,128)S(1)}, s32[256,8]{1,0:T(8,128)}, u32[]{:S(2)}) copy-start(s32[256,8]{1,0:T(8,128)} %copy.54) | copy-start | bytes 24580
  54.4 117.2 %copy-start.12 = (f32[256]{0:T(256)S(1)}, f32[256]{0:T(256)}, u32[]{:S(2)}) copy-start(f32[256]{0:T(256)} %get-tuple-element.193) | copy-start | bytes 3076
  54.4 117.2 %copy-start.15 = (f32[1024]{0:T(1024)S(1)}, f32[1024]{0:T(1024)}, u32[]{:S(2)}) copy-start(f32[1024]{0:T(1024)} %param.21) | copy-start | bytes 12292
  177.8 4.3 %copy-start.16 = (s32[1,4]{1,0:T(1,128)S(1)}, s32[1,4]{1,0:T(1,128)}, u32[]{:S(2)}) copy-start(s32[1,4]{1,0:T(1,128)} %param.27) | copy-start | bytes 52
  177.8 6.1 %copy-start.14 = (s32[64]{0:T(128)S(1)}, s32[64]{0:T(128)}, u32[]{:S(2)}) copy-start(s32[64]{0:T(128)} %param.25) | copy-start | bytes 772
  179.2 5.3 %copy-start.1 = (bf16[256,1024]{1,0:T(8,128)(2,1)}, bf16[256,1024]{1,0:T(8,128)(2,1)S(1)}, u32[]{:S(2)}) copy-start(bf16[256,1024]{1,0:T(8,128)(2,1)S(1)} %get-tuple-element.192) | copy-start | bytes 1572868
  179.2 4.9 %copy-start.13 = (s32[64]{0:T(128)S(1)}, s32[64]{0:T(128)}, u32[]{:S(2)}) copy-start(s32[64]{0:T(128)} %param.26) | copy-start | bytes 772
  179.3 25.0 %collective-permute-start.5 = (bf16[384,1024]{1,0:T(8,128)(2,1)S(1)}, bf16[384,1024]{1,0:T(8,128)(2,1)S(1)}, u32[]{:S(2)}, u32[]{:S(2)}) collective-permute-start(bf16[384,1024]{1,0:T(8,128)(2,1)S(1)} %pad_maximum_fusion.1), channel_id=1, source_target_pairs={{0,192},{64,0},{128,64},{192,128},{1,193},{65,1},{129,65},{193,129... | collective-permute-start | bytes 2359304 | tf_op jit(solution)/shard_map/ppermute | solution.py:171
  182.2 25.7 %collective-permute-start.3 = (bf16[256,1024]{1,0:T(8,128)(2,1)S(1)}, bf16[256,1024]{1,0:T(8,128)(2,1)S(1)}, u32[]{:S(2)}, u32[]{:S(2)}) collective-permute-start(bf16[256,1024]{1,0:T(8,128)(2,1)S(1)} %get-tuple-element.192), channel_id=1, source_target_pairs={{0,64},{64,128},{128,192},{192,0},{1,65},{65,129},{129,193},{193,1... | collective-permute-start | bytes 1572872 | tf_op jit(solution)/shard_map/ppermute | solution.py:171
  182.3 25.7 %collective-permute-start.4 = (bf16[128,1024]{1,0:T(8,128)(2,1)S(1)}, bf16[128,1024]{1,0:T(8,128)(2,1)S(1)}, u32[]{:S(2)}, u32[]{:S(2)}) collective-permute-start(bf16[128,1024]{1,0:T(8,128)(2,1)S(1)} %get-tuple-element.202), channel_id=1, source_target_pairs={{0,128},{64,192},{128,0},{192,64},{1,129},{65,193},{129,1},{193,65... | collective-permute-start | bytes 786440 | tf_op jit(solution)/shard_map/ppermute | solution.py:171
  204.3 8.2 %collective-permute-start.6 = (bf16[128,1024]{1,0:T(8,128)(2,1)S(1)}, bf16[128,1024]{1,0:T(8,128)(2,1)S(1)}, u32[]{:S(2)}, u32[]{:S(2)}) collective-permute-start(bf16[128,1024]{1,0:T(8,128)(2,1)S(1)} %slice.60), channel_id=1, source_target_pairs={{0,192},{64,0},{128,64},{192,128},{1,193},{65,1},{129,65},{193,129... | collective-permute-start | bytes 786440 | tf_op jit(solution)/shard_map/ppermute | solution.py:171
